TPU v7x, 32 devices: a whole 2x2x4 slice. The times are simulated.
32 devices in a mesh: dp: 8 (over y, x, core), tensor: 4 (over z).
Axes of the slice: x: 2, y: 2, z: 4, core: 2. Of those that a mesh axis runs over, the one named last changes fastest.
Arguments:
- tokens: bfloat16 [12608, 512], P(('dp', 'tensor')), may hold values from -11 to 11
- cotangent: bfloat16 [12608, 512], P(('dp', 'tensor')), may hold values from -11 to 11
- routes: int32 [12608, 2], P('dp'), may hold values from 0 to 3, as said below
- slots: int32 [12608, 2], P('dp'), may hold values from -1 to 787, as said below
- norm_gains: bfloat16 [2, 512], P(None, 'dp'), may hold values from 0.5 to 1.5
- norm_biases: bfloat16 [2, 512], P(None, 'dp'), may hold values from -1 to 1
- w_qkv: bfloat16 [3, 512, 512], P(None, 'dp', 'tensor'), may hold values from -0.25 to 0.25
- qv_bias: bfloat16 [2, 512], P(None, ('tensor', 'dp')), may hold values from -1 to 1
- w_out: bfloat16 [512, 512], P('tensor', 'dp'), may hold values from -2 to 2
- out_bias: bfloat16 [512], P('dp'), may hold values from -1 to 1
- w_router: bfloat16 [512, 4], P('dp'), may hold values from -0.25 to 0.25
- w_up: bfloat16 [4, 512, 2048], P(None, 'dp', 'tensor'), may hold values from -0.25 to 0.25
- up_bias: bfloat16 [4, 2048], P(None, ('tensor', 'dp')), may hold values from -1 to 1
- w_down: bfloat16 [4, 2048, 512], P(None, 'tensor', 'dp'), may hold values from -0.5 to 0.5
- down_bias: bfloat16 [4, 512], P(None, 'dp'), may hold values from -1 to 1
Outputs:
- layer_out: float32 [12608, 512], P(('dp', 'tensor'))
- grad_tokens: float32 [12608, 512], P(('dp', 'tensor'))
- grad_norm_gains: float32 [2, 512], P(None, 'dp')
- grad_norm_biases: float32 [2, 512], P(None, 'dp')
- grad_qkv: float32 [3, 512, 512], P(None, 'dp', 'tensor')
- grad_qv_bias: float32 [2, 512], P(None, ('tensor', 'dp'))
- grad_out: float32 [512, 512], P('tensor', 'dp')
- grad_out_bias: float32 [512], P('dp')
- grad_router: float32 [512, 4], P('dp')
- grad_up: float32 [4, 512, 2048], P(None, 'dp', 'tensor')
- grad_up_bias: float32 [4, 2048], P(None, ('tensor', 'dp'))
- grad_down: float32 [4, 2048, 512], P(None, 'tensor', 'dp')
- grad_down_bias: float32 [4, 512], P(None, 'dp')
Inputs may be any that keep to these rules, and one draw needn't show every extreme that they name: `routes`: the two entries of a row name different experts. Within the 1576 rows of one index of dp, the pairs that name an expert take its slots 0, 1, 2, ... in the order of rows and, within a row, of entries; a pair past the first 788 of its expert has -1.
All inputs are finite; a program needn't handle non-finite values.
Results may differ from a plain program's by a relative error of at most 0.025.
Values may be sent and summed in bfloat16 or wider, within the bound.
No kernel may reach another device: no remote copies, remote signals or barrier semaphores. Data moves between devices by JAX's collectives and lax.ppermute only.
A program may use at most 128 MiB of HBM per device.

v0:
```python
from functools import partial

import jax
import jax.numpy as jnp
import numpy as np
from jax import lax
from jax.experimental import pallas as pl
from jax.experimental.pallas import tpu as pltpu
from jax.sharding import PartitionSpec as P

HD = 64
EXPERTS = 4
SEQ = 197
IMG_DEV = 8
PAD = 200
SMALL = 16
EPS = 1e-06
BF = jnp.bfloat16
F4 = jnp.float32
NEG = -1e30
LANES = 128
HALF = 64

NN = (((1,), (0,)), ((), ()))
NT = (((1,), (1,)), ((), ()))
TN = (((0,), (0,)), ((), ()))

VM = pl.BlockSpec()
SM = pl.BlockSpec(memory_space=pltpu.SMEM)
ANY = pl.BlockSpec(memory_space=pltpu.HBM)


def mm(a, b, dims=NN):
    return lax.dot_general(a, b, dims, preferred_element_type=F4)


def params(mib=12):
    return pltpu.CompilerParams(vmem_limit_bytes=mib * 1024 * 1024)


def cost(us):
    return pl.CostEstimate(flops=0, transcendentals=0, bytes_accessed=int(us * 3.3e4))


def xor_send(x, axis, n, mask):
    return lax.ppermute(x, axis, [(i, i ^ mask) for i in range(n)])


def ring_order(n):
    return [0] + list(range(1, n, 2)) + list(range(2, n, 2))[::-1]


def ring_step(x, n, back):
    ring = ring_order(n)
    pairs = [(ring[p], ring[(p + (-1 if back else 1)) % n]) for p in range(n)]
    return lax.ppermute(x, "tensor", pairs)


def ring_sources(n):
    ring = ring_order(n)
    pos = {r: p for p, r in enumerate(ring)}
    return [[ring[(pos[r] - s) % n] for s in range(n)] for r in range(n)]


def stages_of(n):
    if n <= 8:
        inter = list(range(2, n, 2))
        return ([[1]] if n > 1 else []) + ([inter] if inter else [])
    out, bit = [], 1
    while bit < n:
        out.append([bit])
        bit *= 2
    return out


def gather_dp(x, n):
    parts = [((0,), x[None])]
    for stage in reversed(stages_of(n)):
        new = []
        for mask in stage:
            for masks, arr in parts:
                new.append((tuple(k ^ mask for k in masks), xor_send(arr, "dp", n, mask)))
        parts = parts + new
        if n > 8 and stage != [1]:
            parts = [
                (sum((m for m, _ in parts), ()), jnp.concatenate([a for _, a in parts], axis=0))
            ]
    return parts


def scatter_dp(even, odd, n):
    got = xor_send(odd, "dp", n, 1)
    masks = list(range(0, n, 2))
    own = {k: even[i] for i, k in enumerate(masks)}
    new = {k: got[i] for i, k in enumerate(masks)}
    own = {k: (own[k].astype(F4) + new[k].astype(F4)).astype(BF) for k in masks}
    stages = stages_of(n)[1:]
    for at, stage in enumerate(stages):
        span = 0
        for m in stage:
            span |= m
        rest = [k for k in masks if not k & span]
        recv = []
        for m in stage:
            pack = [own[k ^ m] for k in rest]
            send = pack[0] if len(pack) == 1 else jnp.stack(pack)
            back = xor_send(send, "dp", n, m)
            recv.append([back] if len(pack) == 1 else [back[i] for i in range(len(pack))])
        masks = rest
        if at == len(stages) - 1:
            return [own[0]] + [r[0] for r in recv]
        own = {
            k: sum((r[i].astype(F4) for r in recv), own[k].astype(F4)).astype(BF)
            for i, k in enumerate(rest)
        }
    return [own[0]]


CORE0, CORE1 = (0, 2, 4, 6), (1, 3, 5, 7)


def to(x, mask):
    return xor_send(x, "dp", 8, mask)


def plane_first(x):
    return x, to(x, 2), to(x, 4)


def plane_far(x, from_x, from_y):
    half = x.shape[0] // 2
    return to(from_x[:half], 4), to(from_y[half:], 2)


def plane_stack(x, from_x, from_y, far):
    return jnp.stack([x, from_x, from_y, jnp.concatenate(far, axis=0)])


def gather_cores(quad):
    return [(CORE0, quad), (CORE1, to(quad, 1))]


def scatter_first(even, got):
    half = even.shape[1] // 2
    low, high = slice(0, half), slice(half, 2 * half)

    def both(mask, part):
        return [(even, (mask // 2, part)), (got, (mask // 2, part))]

    return sums(
        [
            [both(0, low), both(4, low)],
            [both(0, high), both(2, high)],
            [both(2, low), both(6, low)],
            [both(4, high), both(6, high)],
        ]
    )


def scatter_second(keep_x, keep_y, got_x, got_y):
    pairs = [(keep_x, got_x), (keep_y, got_y)]
    return sums([[[(k, at), (g, at)]] for at in (1, 0) for k, g in pairs])


def after(x, *first):
    return lax.optimization_barrier((x, *first))[0]


def arrays(parts):
    return [a for _, a in parts]


def sums_kernel(outs, count, *refs):
    for groups, out in zip(outs, refs[count:]):
        for j, group in enumerate(groups):
            total = None
            for n, at in group:
                term = (refs[n][...] if at is None else refs[n][at]).astype(F4)
                total = term if total is None else total + term
            if len(groups) == 1:
                out[...] = total.astype(out.dtype)
            else:
                out[j] = total.astype(out.dtype)


def sums(outs):
    known, flat, index, shapes = {}, [], [], []
    for groups in outs:
        index.append([])
        for group in groups:
            index[-1].append([])
            for v, at in group:
                if id(v) not in known:
                    known[id(v)] = len(flat)
                    flat.append(v)
                index[-1][-1].append((known[id(v)], at))
        v, at = groups[0][0]
        shape = v.shape if at is None else np.broadcast_to(0, v.shape)[at].shape
        shapes.append(shape if len(groups) == 1 else (len(groups),) + shape)
    return pl.pallas_call(
        partial(sums_kernel, index, len(flat)),
        out_shape=[jax.ShapeDtypeStruct(v, BF) for v in shapes],
        in_specs=[VM] * len(flat),
        out_specs=[VM] * len(shapes),
        compiler_params=params(16),
        cost_estimate=cost(1),
        name="sums",
    )(*flat)


def finish_kernel(dr, qr, *refs):
    parts, outs = refs[:4], refs[4:]
    g_qkv, g_out, g_gain, g_bias, g_outb, g_router, g_dbias, g_ub, g_qvb = outs
    total = parts[0][...].astype(F4)
    for ref in parts[1:]:
        total = total + ref[...].astype(F4)
    for s in range(3):
        g_qkv[s] = total[s * dr : (s + 1) * dr]
    g_out[...] = total[3 * dr : 4 * dr]
    low = total[4 * dr :]
    high = pltpu.roll(low, HALF, 1)
    g_gain[...] = low[0:2, :HALF]
    g_bias[...] = low[2:4, :HALF]
    g_outb[...] = low[4:5, :HALF]
    g_router[...] = low[5:9, :HALF]
    g_dbias[...] = low[9:13, :HALF]
    g_ub[...] = high[0:4, :HALF]
    g_qvb[...] = high[4:6, :qr]


def finish(parts, dr, qr):
    rows = [(2, HALF), (2, HALF), (1, HALF), (EXPERTS, HALF), (EXPERTS, HALF), (EXPERTS, HALF), (2, qr)]
    shapes = [(3, dr, LANES), (dr, LANES)] + rows
    return pl.pallas_call(
        partial(finish_kernel, dr, qr),
        out_shape=[jax.ShapeDtypeStruct(v, F4) for v in shapes],
        in_specs=[VM] * 4,
        out_specs=[VM] * len(shapes),
        compiler_params=params(),
        cost_estimate=cost(1),
        name="finish",
    )(*parts)


def add_all(parts):
    return sum((p.astype(F4) for p in parts[1:]), parts[0].astype(F4))


def moments(v, eps_rows):
    center = v - jnp.mean(v, axis=-1, keepdims=True)
    inv = lax.rsqrt(jnp.mean(center * center, axis=-1, keepdims=True) + eps_rows)
    return center * inv, inv


def norm_back(z, normed, inv):
    return inv * (
        z
        - jnp.mean(z, axis=-1, keepdims=True)
        - normed * jnp.mean(z * normed, axis=-1, keepdims=True)
    )


def exact(ref, lo, hi):
    return ref[lo:hi, :].astype(BF)


GAIN, BIAS, OUTB, QVB, ROUTER, DBIAS, UBIAS, NROWS = 0, 2, 4, 5, 8, 16, 24, 32


def in_hbm(values):
    return [pltpu.with_memory_space_constraint(v, pltpu.HBM) for v in values]


def run_copies(pairs, sems):
    copies = [pltpu.make_async_copy(a, b, sems.at[n]) for n, (a, b) in enumerate(pairs)]
    for c in copies:
        c.start()
    for c in copies:
        c.wait()


def assemble_kernel(masks, ids, *refs):
    pieces, (w_ref, rows_ref, small_ref, sems) = refs[:-4], refs[-4:]
    me, met = ids[0], ids[1]
    pairs = []
    for group, ref in zip(masks, pieces):
        dr = (ref.shape[2] - SMALL) // 4
        for idx, mask in enumerate(group):
            i = jnp.bitwise_xor(me, mask)
            for jm in range(ref.shape[1]):
                j = jnp.bitwise_xor(met, jm)
                rows_at = pl.ds(pl.multiple_of(i * dr, dr), dr)
                lanes_at = pl.ds(pl.multiple_of(j * LANES, LANES), LANES)
                for s in range(4):
                    pairs.append(
                        (ref.at[idx, jm, s * dr : (s + 1) * dr], w_ref.at[s, rows_at, lanes_at])
                    )
                pairs.append((ref.at[idx, jm, 4 * dr : 4 * dr + SMALL], small_ref.at[mask, jm]))
    run_copies(pairs, sems)
    rows_ref[...] = jnp.zeros(rows_ref.shape, F4)
    lane = lax.broadcasted_iota(jnp.int32, (SMALL, LANES), 1)
    low = lane < HALF
    odd = jnp.bitwise_and(me, 1) == 1
    nd, nt = small_ref.shape[:2]

    def small(mask, jm):
        return small_ref[mask, jm].astype(F4)

    for mask in range(0, nd, 2):
        a, b = small(mask, 0), small(mask + 1, 0)
        first, second = jnp.where(odd, b, a), jnp.where(odd, a, b)
        lo = jnp.where(low, first, pltpu.roll(second, HALF, 1))
        hi = jnp.where(low, pltpu.roll(first, HALF, 1), second)
        tile = jnp.right_shift(jnp.bitwise_xor(me, mask), 1)
        at = pl.ds(pl.multiple_of(tile * LANES, LANES), LANES)
        rows_ref[0:5, at] = lo[0:5]
        rows_ref[ROUTER : ROUTER + EXPERTS, at] = lo[5:9]
        rows_ref[DBIAS : DBIAS + EXPERTS, at] = lo[9:13]
        rows_ref[UBIAS : UBIAS + EXPERTS, at] = hi[0:4]
    qr = LANES // nd
    mine = jnp.logical_and(lane >= HALF, lane < HALF + qr)
    for jm in range(nt):
        j = jnp.bitwise_xor(met, jm)
        total = jnp.zeros((SMALL, LANES), F4)
        for mask in range(nd):
            i = jnp.bitwise_xor(me, mask)
            part = jnp.where(mine, small(mask, jm), 0.0)
            total = total + pltpu.roll(part, jnp.bitwise_and(HALF + i * qr, LANES - 1), 1)
        rows_ref[QVB : QVB + 2, pl.ds(pl.multiple_of(j * LANES, LANES), LANES)] = total[4:6]


def assemble(ids, weights, width):
    masks = [m for m, _ in weights]
    pieces = arrays(weights)
    nd, nt = sum(len(m) for m in masks), pieces[0].shape[1]
    return pl.pallas_call(
        partial(assemble_kernel, masks),
        out_shape=[
            jax.ShapeDtypeStruct((4, width, width), BF),
            jax.ShapeDtypeStruct((NROWS, width), F4),
        ],
        in_specs=[SM] + [ANY] * len(pieces),
        out_specs=[VM, VM],
        scratch_shapes=[
            pltpu.VMEM((nd, nt, SMALL, LANES), BF),
            pltpu.SemaphoreType.DMA((5 * nd * nt,)),
        ],
        compiler_params=params(8),
        cost_estimate=cost(2),
        name="assemble",
    )(ids, *pieces)


def attn_forward_kernel(
    nimg, x_ref, rows_ref, w_ref, hn2_ref, x1_out, q_out, k_out, v_out, o_out, pb_out, *scratch
):
    x1_ref, q_ref, k_ref, v_ref, o_ref, pb_ref, sems = scratch
    heads = w_ref.shape[1] // HD
    copies = []

    def leave(src, dst):
        copies.append(pltpu.make_async_copy(src, dst, sems.at[len(copies)]))
        copies[-1].start()

    width = x_ref.shape[1]
    x = x_ref[...].astype(F4)
    n1, _ = moments(x, EPS)
    hn1 = (n1 * rows_ref[0:1, :] + rows_ref[2:3, :]).astype(BF)
    q_ref[...] = (mm(hn1, w_ref[0]) + rows_ref[5:6, :]).astype(BF)
    k_ref[...] = mm(hn1, w_ref[1]).astype(BF)
    v_ref[...] = (mm(hn1, w_ref[2]) + rows_ref[6:7, :]).astype(BF)
    leave(q_ref, q_out)
    leave(k_ref, k_out)
    leave(v_ref, v_out)
    lane = lax.broadcasted_iota(jnp.int32, (PAD, LANES), 1)
    col = lax.broadcasted_iota(jnp.int32, (PAD, PAD), 1)
    for img in range(nimg):
        at = slice(img * PAD, (img + 1) * PAD)
        for pair in range(width // LANES):
            cols = slice(pair * LANES, (pair + 1) * LANES)
            qp, kp, vp = q_ref[at, cols], k_ref[at, cols], v_ref[at, cols]
            acc = jnp.zeros((PAD, LANES), F4)
            for half in range(2):
                mine = (lane < HD) if half == 0 else (lane >= HD)
                qm = jnp.where(mine, qp * jnp.asarray(HD ** (-0.5), BF), jnp.zeros_like(qp))
                s = mm(qm, kp, NT)
                s = jnp.where(col < SEQ, s, NEG)
                e = jnp.exp(s - jnp.max(s, axis=-1, keepdims=True))
                p = (e * (1.0 / jnp.sum(e, axis=-1, keepdims=True))).astype(BF)
                pb_ref[img * heads + 2 * pair + half] = p
                acc = acc + mm(p, jnp.where(mine, vp, jnp.zeros_like(vp)))
            o_ref[at, cols] = acc.astype(BF)
        mine = pl.ds(img * heads, heads)
        leave(pb_ref.at[mine], pb_out.at[mine])
    leave(o_ref, o_out)
    x1 = x + (mm(o_ref[...], w_ref[3], NT) + rows_ref[4:5, :])
    x1_ref[...] = x1
    leave(x1_ref, x1_out)
    n2, _ = moments(x1, EPS)
    hn2_ref[...] = (n2 * rows_ref[1:2, :] + rows_ref[3:4, :]).astype(BF)
    for c in copies:
        c.wait()


def attn_forward(x, rows, full, nimg):
    count, width = x.shape
    heads = width // HD
    saved = [((count, width), F4)] + [((count, width), BF)] * 4
    saved.append(((nimg * heads, PAD, PAD), BF))
    shapes = [jax.ShapeDtypeStruct((count, width), BF)] + [pltpu.HBM(*v) for v in saved]
    return pl.pallas_call(
        partial(attn_forward_kernel, nimg),
        out_shape=shapes,
        in_specs=[VM] * 3,
        out_specs=[VM] + [ANY] * len(saved),
        scratch_shapes=[pltpu.VMEM(*v) for v in saved] + [pltpu.SemaphoreType.DMA((5 + nimg,))],
        compiler_params=params(),
        cost_estimate=cost(9),
        name="attn_forward",
    )(x, rows, full)


def gather_experts_kernel(masks, ids, *refs):
    pieces, (w_ref, sems) = refs[:-2], refs[-2:]
    me = ids[0]
    pairs = []
    for group, ref in zip(masks, pieces):
        dr, ff = ref.shape[2], ref.shape[3]
        for idx, mask in enumerate(group):
            at = pl.ds(pl.multiple_of(jnp.bitwise_xor(me, mask) * dr, dr), dr)
            for e in range(EXPERTS):
                pairs.append((ref.at[idx, e], w_ref.at[at, e * ff : (e + 1) * ff]))
    run_copies(pairs, sems)


def gather_experts(ids, weights, width):
    masks = [m for m, _ in weights]
    pieces = arrays(weights)
    nd = sum(len(m) for m in masks)
    return pl.pallas_call(
        partial(gather_experts_kernel, masks),
        out_shape=jax.ShapeDtypeStruct((width, EXPERTS * pieces[0].shape[3]), BF),
        in_specs=[SM] + [ANY] * len(pieces),
        out_specs=VM,
        scratch_shapes=[pltpu.SemaphoreType.DMA((EXPERTS * nd,))],
        compiler_params=params(8),
        cost_estimate=cost(3),
        name="gather_experts",
    )(ids, *pieces)


def normal_parts(u):
    bell = jnp.exp(-0.5 * (u * u))
    t = 1.0 / (1.0 + (0.3275911 * 2.0 ** (-0.5)) * jnp.abs(u))
    poly = 0.5 * 1.061405429 * t + 0.5 * (-1.453152027)
    poly = poly * t + 0.5 * 1.421413741
    poly = poly * t + 0.5 * (-0.284496736)
    poly = poly * t + 0.5 * 0.254829592
    tail = poly * t * bell
    return jnp.where(u > 0.0, 1.0 - tail, tail), bell


def expert_kernel(
    nimg, shard, ids, keep_ref, hn2_ref, cot_ref, rows_ref, up_ref, dn_ref, m_ref, d_ref, hg_ref, dhp_ref, sm_ref
):
    own = shard == 0
    count = hn2_ref.shape[0]
    ff = hg_ref.shape[1] // EXPERTS
    hn2, cot = hn2_ref[...], cot_ref[...]
    router = exact(rows_ref, ROUTER, ROUTER + 8)
    lane = lax.broadcasted_iota(jnp.int32, (count, 8), 1)
    logits = jnp.where(lane < EXPERTS, mm(hn2, router, NT), NEG)
    e = jnp.exp(logits - jnp.max(logits, axis=-1, keepdims=True))
    probs = e / jnp.sum(e, axis=-1, keepdims=True)
    tile = ids[2 + shard] * nimg
    keep = jnp.concatenate([keep_ref[tile + i] for i in range(nimg)], axis=0)
    on = jnp.logical_or(lane == keep[:, 0:1], lane == keep[:, 1:2])
    gates = jnp.where(on, probs, 0.0).astype(BF)
    gates_f = gates.astype(F4)
    dp = jnp.zeros((count, 8), F4)
    if own:
        dbias = exact(rows_ref, DBIAS, DBIAS + 8)
        dp = mm(cot, dbias, NT)

    def pair(i, dp):
        for e in (2 * i, 2 * i + 1):
            cols = pl.ds(pl.multiple_of(e * ff, ff), ff)
            mine = lane == e
            gate = jnp.sum(jnp.where(mine, gates_f, 0.0), axis=-1, keepdims=True)
            u = mm(hn2, up_ref[:, cols]) + rows_ref[pl.ds(UBIAS + e, 1), 0:ff]
            phi, bell = normal_parts(u)
            h = u * phi
            slope = phi + u * (bell * 0.3989422804014327)
            r = mm(cot, dn_ref[:, cols])
            dp = dp + jnp.where(mine, jnp.sum(h * r, axis=-1, keepdims=True), 0.0)
            hg_ref[:, cols] = (h * gate).astype(BF)
            dhp_ref[:, cols] = (r * slope * gate).astype(BF)
        return dp

    dp = lax.fori_loop(0, EXPERTS // 2, pair, dp)
    dp = jnp.where(on, dp, 0.0)
    dl = (probs * (dp - jnp.sum(probs * dp, axis=-1, keepdims=True))).astype(BF)
    d_ref[...] = (mm(dhp_ref[...], up_ref[...], NT) + mm(dl, router)).astype(BF)
    m = mm(hg_ref[...], dn_ref[...], NT)
    sm_ref[0:8, :] = mm(dl, hn2, TN)
    if own:
        m = m + mm(gates, dbias)
        sm_ref[8:16, :] = mm(gates, cot, TN)
    else:
        sm_ref[8:16, :] = jnp.zeros((8, sm_ref.shape[1]), F4)
    m_ref[...] = m.astype(BF)


def expert_shard(ids, keep, hn2, cot, rows, up, dn, nimg, shard):
    count, width = hn2.shape
    wide = jax.ShapeDtypeStruct((count, up.shape[1]), BF)
    low = jax.ShapeDtypeStruct((count, width), BF)
    return pl.pallas_call(
        partial(expert_kernel, nimg, shard),
        out_shape=[low, low, wide, wide, jax.ShapeDtypeStruct((16, width), F4)],
        in_specs=[SM] + [VM] * 6,
        out_specs=[VM] * 5,
        compiler_params=params(),
        cost_estimate=cost(7),
        name="expert_shard",
    )(ids, keep, hn2, cot, rows, up, dn)


def expert_grad_kernel(nt, gmasks, ids, *refs):
    hn2s, cots, hgs, dhps = (refs[i * nt : (i + 1) * nt] for i in range(4))
    gub_ref = refs[4 * nt]
    grads = refs[4 * nt + 1 : 4 * nt + 1 + len(gmasks)]
    res_ref = refs[4 * nt + 1 + len(gmasks)]
    me = ids[0]
    ones = jnp.ones((8, hn2s[0].shape[0]), BF)
    sums = None
    for s in range(nt):
        part = mm(ones, dhps[s][...])
        sums = part if sums is None else sums + part
    for which in range(2):
        lefts, rights = ((hn2s, dhps), (cots, hgs))[which]
        left = jnp.concatenate([r[...] for r in lefts], axis=0)
        right = jnp.concatenate([r[...] for r in rights], axis=0)
        total = mm(left, right, TN)
        res_ref[...] = total
        for group, ref in zip(gmasks, grads):
            dr = ref.shape[3]
            for idx, mask in enumerate(group):
                at = pl.ds(pl.multiple_of(jnp.bitwise_xor(me, mask) * dr, dr), dr)
                ref[idx, which, 0] = res_ref[at, :].astype(BF)
    gub_ref[...] = sums[0:1, :]


def expert_grads(ids, hn2s, cots, hgs, dhps, gmasks, dr):
    nt = len(hn2s)
    count, width = hn2s[0].shape
    ff = hgs[0].shape[1] // EXPERTS
    fixed = pl.BlockSpec((count, width), lambda e: (0, 0))
    moving = pl.BlockSpec((count, ff), lambda e: (0, e))
    return pl.pallas_call(
        partial(expert_grad_kernel, nt, gmasks),
        grid=(EXPERTS,),
        out_shape=[jax.ShapeDtypeStruct((EXPERTS, 1, ff), F4)]
        + [jax.ShapeDtypeStruct((len(m), 2, EXPERTS, dr, ff), BF) for m in gmasks],
        in_specs=[SM] + [fixed] * (2 * nt) + [moving] * (2 * nt),
        out_specs=[pl.BlockSpec((None, 1, ff), lambda e: (e, 0, 0))]
        + [pl.BlockSpec((len(m), 2, 1, dr, ff), lambda e: (0, 0, e, 0, 0)) for m in gmasks],
        scratch_shapes=[pltpu.VMEM((width, ff), F4)],
        compiler_params=params(16),
        cost_estimate=cost(9),
        name="expert_grads",
    )(ids, *hn2s, *cots, *hgs, *dhps)


def attn_backward_kernel(nimg, nsm, ngub, gmasks, direct, ids, *refs):
    ins = 12 + ngub + nsm
    recv_ref, own_ref, x_ref, cot_ref = refs[:4]
    rows_ref, w_ref = refs[10:12]
    gubs, sms = refs[12 : 12 + ngub], refs[12 + ngub : ins]
    gtok_ref = refs[ins]
    ngrads = len(gmasks)
    grads = refs[ins + 1 : ins + 1 + ngrads]
    small_ref, do_ref, dq_ref, dk_ref, dv_ref, da_ref, hn1_ref, res_ref = refs[
        ins + 1 + ngrads : ins + 9 + ngrads
    ]
    held = refs[ins + 9 + ngrads :]
    x1_ref, q_ref, k_ref, v_ref, o_ref, pb_ref, sems = held
    copies = [
        pltpu.make_async_copy(a, b, sems.at[n]) for n, (a, b) in enumerate(zip(refs[4:10], held))
    ]
    for c in copies:
        c.start()
    width = x_ref.shape[1]
    dh = recv_ref[...].astype(F4) + own_ref[...].astype(F4)
    cot_f = cot_ref[...].astype(F4)
    copies[0].wait()
    n2, inv2 = moments(x1_ref[...], EPS)
    small_ref[...] = jnp.zeros(small_ref.shape, F4)
    small_ref[1:2, :] = jnp.sum(dh * n2, axis=0, keepdims=True)
    small_ref[3:4, :] = jnp.sum(dh, axis=0, keepdims=True)
    dx1 = cot_f + norm_back(dh * rows_ref[1:2, :], n2, inv2)
    da = dx1.astype(BF)
    da_ref[...] = da
    gtok_ref[...] = dx1
    small_ref[4:5, :] = jnp.sum(da.astype(F4), axis=0, keepdims=True)
    do_ref[...] = mm(da, w_ref[3]).astype(BF)
    lane = lax.broadcasted_iota(jnp.int32, (PAD, LANES), 1)
    scale = HD ** (-0.5)
    for c in copies[1:]:
        c.wait()

    def pair(n, carry):
        cols = pl.ds(pl.multiple_of(n * LANES, LANES), LANES)
        for img in range(nimg):
            at = slice(img * PAD, (img + 1) * PAD)
            qp, kp, vp, dop = q_ref[at, cols], k_ref[at, cols], v_ref[at, cols], do_ref[at, cols]
            zero = jnp.zeros_like(qp)
            dq = jnp.zeros((PAD, LANES), F4)
            dk = jnp.zeros((PAD, LANES), F4)
            dv = jnp.zeros((PAD, LANES), F4)
            for half in range(2):
                mine = (lane < HD) if half == 0 else (lane >= HD)
                pb = pb_ref[img * (width // HD) + 2 * n + half]
                dom = jnp.where(mine, dop, zero)
                dpb = mm(dom, vp, NT)
                p = pb.astype(F4)
                ds = (p * (dpb - jnp.sum(p * dpb, axis=-1, keepdims=True))).astype(BF)
                dv = dv + mm(pb, dom, TN)
                dq = dq + mm(ds, jnp.where(mine, kp, zero))
                dk = dk + mm(ds, jnp.where(mine, qp, zero), TN)
            dq_ref[at, cols] = (dq * scale).astype(BF)
            dk_ref[at, cols] = (dk * scale).astype(BF)
            dv_ref[at, cols] = dv.astype(BF)
        return carry

    lax.fori_loop(0, width // LANES, pair, 0)
    small_ref[QVB : QVB + 1, :] = jnp.sum(dq_ref[...].astype(F4), axis=0, keepdims=True)
    small_ref[QVB + 1 : QVB + 2, :] = jnp.sum(dv_ref[...].astype(F4), axis=0, keepdims=True)
    dh1 = (
        mm(dq_ref[...], w_ref[0], NT)
        + mm(dk_ref[...], w_ref[1], NT)
        + mm(dv_ref[...], w_ref[2], NT)
    )
    n1, inv1 = moments(x_ref[...].astype(F4), EPS)
    hn1_ref[...] = (n1 * rows_ref[0:1, :] + rows_ref[2:3, :]).astype(BF)
    small_ref[0:1, :] = jnp.sum(dh1 * n1, axis=0, keepdims=True)
    small_ref[2:3, :] = jnp.sum(dh1, axis=0, keepdims=True)
    gtok_ref[...] = gtok_ref[...] + norm_back(dh1 * rows_ref[0:1, :], n1, inv1)
    total = sms[0][...]
    for ref in sms[1:]:
        total = total + ref[...]
    small_ref[ROUTER : ROUTER + 16, :] = total
    for e in range(EXPERTS):
        ref, at = gubs[e * ngub // EXPERTS], e % (EXPERTS // ngub)
        small_ref[UBIAS + e : UBIAS + e + 1, 0 : ref.shape[2]] = ref[at]
    me, met = ids[0], ids[1]
    for s in range(4):
        left, right = [(hn1_ref, dq_ref), (hn1_ref, dk_ref), (hn1_ref, dv_ref), (da_ref, o_ref)][s]
        res_ref[...] = mm(left[...], right[...], TN)
        for group, ref in zip(gmasks, grads):
            dr = (ref.shape[2] - (SMALL if direct else 0)) // 4
            for idx, mask in enumerate(group):
                i = jnp.bitwise_xor(me, mask)
                for jm in range(ref.shape[1]):
                    j = jnp.bitwise_xor(met, jm)
                    ref[idx, jm, s * dr : (s + 1) * dr, :] = res_ref[
                        pl.ds(pl.multiple_of(i * dr, dr), dr),
                        pl.ds(pl.multiple_of(j * LANES, LANES), LANES),
                    ].astype(BF)
    if not direct:
        return
    lane = lax.broadcasted_iota(jnp.int32, (SMALL, LANES), 1)
    row = lax.broadcasted_iota(jnp.int32, (SMALL, LANES), 0)
    nd = sum(len(g) for g in gmasks)
    qr = LANES // nd
    blank = jnp.zeros((3, LANES), F4)
    for group, ref in zip(gmasks, grads):
        for idx, mask in enumerate(group):
            i = jnp.bitwise_xor(me, mask)
            odd = jnp.bitwise_and(i, 1) == 1
            tile = pl.ds(pl.multiple_of(jnp.right_shift(i, 1) * LANES, LANES), LANES)
            t = jnp.concatenate(
                [small_ref[0:5, tile], small_ref[ROUTER : ROUTER + 4, tile], small_ref[DBIAS : DBIAS + 4, tile], blank],
                axis=0,
            )
            lo = jnp.where(odd, pltpu.roll(t, HALF, 1), t)
            lo = jnp.where(lane < HALF, lo, 0.0)
            b = jnp.concatenate([small_ref[UBIAS : UBIAS + 8, tile], jnp.zeros((8, LANES), F4)], axis=0)
            hi = jnp.where(odd, b, pltpu.roll(b, HALF, 1))
            hi = jnp.where(jnp.logical_and(lane >= HALF, row < EXPERTS), hi, 0.0)
            for jm in range(ref.shape[1]):
                j = jnp.bitwise_xor(met, jm)
                g = small_ref[0:8, pl.ds(pl.multiple_of(j * LANES, LANES), LANES)]
                g = pltpu.roll(g, 7, 0)
                g = pltpu.roll(g, jnp.bitwise_and(HALF - i * qr + LANES, LANES - 1), 1)
                g = jnp.concatenate([g, jnp.zeros((8, LANES), F4)], axis=0)
                mine = jnp.logical_and(lane >= HALF, lane < HALF + qr)
                mine = jnp.logical_and(mine, jnp.logical_and(row >= 4, row < 6))
                block = lo + jnp.where(mine, g, 0.0)
                if jm == 0:
                    block = block + hi
                ref[idx, jm, 4 * dr :, :] = block.astype(BF)


def attn_backward(ids, recv, own, x, cot, saved, rows, full, gubs, sms, gmasks, direct, nt, dr):
    count, width = x.shape
    nimg = count // PAD
    extra = SMALL if direct else 0
    shapes = [jax.ShapeDtypeStruct((count, width), F4)]
    shapes += [jax.ShapeDtypeStruct((len(m), nt, 4 * dr + extra, LANES), BF) for m in gmasks]
    shapes += [jax.ShapeDtypeStruct((NROWS, width), F4)]
    low = pltpu.VMEM((count, width), BF)
    return pl.pallas_call(
        partial(attn_backward_kernel, nimg, len(sms), len(gubs), gmasks, direct),
        out_shape=shapes,
        in_specs=[SM] + [VM] * 4 + [ANY] * 6 + [VM] * (2 + len(gubs) + len(sms)),
        out_specs=[VM] * len(shapes),
        scratch_shapes=[low] * 6
        + [pltpu.VMEM((width, width), F4)]
        + [pltpu.VMEM(v.shape, v.dtype) for v in saved]
        + [pltpu.SemaphoreType.DMA((6,))],
        compiler_params=params(16),
        cost_estimate=cost(16),
        name="attn_backward",
    )(ids, recv, own, x, cot, *in_hbm(saved), rows, full, *gubs, *sms)


def per_device(
    nd,
    nt,
    tokens,
    cotangent,
    routes,
    slots,
    norm_gains,
    norm_biases,
    w_qkv,
    qv_bias,
    w_out,
    out_bias,
    w_router,
    w_up,
    up_bias,
    w_down,
    down_bias,
):
    me = lax.axis_index("dp").astype(jnp.int32)
    met = lax.axis_index("tensor").astype(jnp.int32)
    width = tokens.shape[1]
    dr = w_qkv.shape[1]
    fr, qr = up_bias.shape[1], qv_bias.shape[1]
    ff = w_up.shape[2]
    nimg = IMG_DEV // nt
    direct = nd == 8 and nt == 4 and dr == HALF and fr == HALF and nd * qr == LANES
    src = jnp.asarray(ring_sources(nt), jnp.int32)[met]
    ids = jnp.concatenate([jnp.stack([me if direct else jnp.zeros_like(me), met]), src])
    even, odd = list(range(0, nd, 2)), list(range(1, nd, 2))

    def canonical(parts):
        if direct:
            return parts
        masks = sum((m for m, _ in parts), ())
        arr = jnp.concatenate([a for _, a in parts], axis=0)
        place = [masks.index(k) for k in range(nd)]
        order = jnp.asarray(place, jnp.int32)[jnp.bitwise_xor(jnp.arange(nd), me)]
        arr = jnp.take(arr, order, axis=0)
        lead = arr.ndim - 2
        arr = jnp.moveaxis(arr, 0, lead - 1)
        arr = arr.reshape(arr.shape[: lead - 1] + (nd * dr,) + arr.shape[-1:])
        return [((0,), arr[None])]

    gmasks = [even, odd] if direct else [[0]]

    def halves(grads, lead, rows):
        if direct:
            return grads
        whole = grads[0][0]
        shape = whole.shape[:lead] + (rows, nd, dr) + whole.shape[-1:]
        whole = jnp.moveaxis(whole.reshape(shape), lead + 1, 0)
        whole = whole.reshape((nd,) + grads[0].shape[1 : lead + 1] + (rows * dr, whole.shape[-1]))
        return [
            jnp.take(whole, jnp.bitwise_xor(jnp.asarray(m, jnp.int32), me), axis=0)
            for m in (even, odd)
        ]

    def images(v):
        return jnp.concatenate(
            [jnp.pad(v[i * SEQ : (i + 1) * SEQ], ((0, PAD - SEQ), (0, 0))) for i in range(nimg)]
        )

    chunk = jnp.concatenate([w_qkv, w_out.T[None]], axis=0)
    if direct:
        wide = [
            jnp.concatenate(
                [norm_gains, norm_biases, out_bias[None], w_router.T, down_bias, jnp.zeros((3, dr), BF)],
                axis=0,
            ),
            jnp.concatenate(
                [up_bias, jnp.pad(qv_bias, ((0, 0), (0, dr - qr))), jnp.zeros((10, dr), BF)], axis=0
            ),
        ]
        chunk = jnp.concatenate([chunk.reshape(4 * dr, LANES), jnp.concatenate(wide, axis=1)], axis=0)
    keep = jnp.where(slots >= 0, routes, -1).reshape(nt * nimg, SEQ, 2)
    keep = jnp.pad(keep, ((0, 0), (0, PAD - SEQ), (0, 0)), constant_values=-1)
    x = images(tokens)
    w_dn = w_down.transpose(0, 2, 1)
    def ring_all(v):
        out = [v]
        for s in range(1, nt):
            out.append(ring_step(out[-1], nt, False))
        return out

    cot = images(cotangent)
    chunk_z = [chunk] + [xor_send(chunk, "tensor", nt, m) for m in range(1, nt)]
    if direct:
        up_near = plane_first(after(w_up, chunk))
        chunk_z, up_near = lax.optimization_barrier((chunk_z, up_near))
        chunk_z = jnp.stack(chunk_z)
        cots = ring_all(after(cot, chunk_z))
        near = plane_first(chunk_z)
        quad = plane_stack(*near, lax.optimization_barrier((plane_far(*near), cots[2]))[0])
        up_far = lax.optimization_barrier((plane_far(*up_near), cots[1]))[0]
        up_quad = plane_stack(*up_near, up_far)
        dn_near = plane_first(after(w_dn, quad))
        quad = after(quad, x, keep, ids, up_quad)
        (_, quad), (_, other) = gather_cores(quad)
        full, rows = assemble(ids, [(CORE0, quad), (CORE1, other)], width)
        up_cores = gather_cores(after(up_quad, quad))
    else:
        cots = ring_all(cot)
        up, dn = (
            canonical(gather_dp(w[None], nd))[0][1][0, 0].transpose(1, 0, 2).reshape(width, EXPERTS * ff)
            for w in (w_up, w_dn)
        )
        full = canonical(gather_dp(jnp.stack(chunk_z), nd))[0][1][0]
        at = jnp.bitwise_xor(jnp.arange(nt), met)
        full = jnp.take(full, at, axis=0).transpose(1, 2, 0, 3).reshape(4, width, width)

        def whole(v):
            return lax.all_gather(v, "dp", axis=v.ndim - 1, tiled=True).astype(F4)

        qvb = lax.all_gather(whole(qv_bias), "tensor", axis=1, tiled=True)
        four = jnp.zeros((4, width), F4)
        rows = [whole(norm_gains), whole(norm_biases), whole(out_bias[None]), qvb]
        rows += [jnp.zeros((1, width), F4), whole(w_router.T), four, whole(down_bias), four]
        rows += [jnp.pad(whole(up_bias), ((0, 0), (0, width - nd * fr))), four]
        rows = jnp.concatenate(rows, axis=0)

    saved = attn_forward(x, rows, full, nimg)
    hn2s = [saved[0]]
    def shard(s, *first):
        hn2 = after(hn2s[s], *first)
        return expert_shard(ids, keep, hn2, cots[s], rows, up, dn, nimg, s)

    for s in range(1, nt):
        hn2s.append(ring_step(after(hn2s[-1], *(cots[-1:] if s == 1 else [])), nt, False))
    if direct:
        up = gather_experts(ids, [(m, after(a, hn2s[0])) for m, a in up_cores], width)
        dn_near = lax.optimization_barrier((dn_near, hn2s[0], cots[3]))[0]
        dn_quad = after(plane_stack(*dn_near, plane_far(*dn_near)), hn2s[1])
        dn = gather_experts(ids, gather_cores(dn_quad), width)
    shards = [None, shard(1)] + [None] * (nt - 2)
    total = past = shards[1][1]
    for s in range(2, nt):
        if s == nt - 1:
            shards[0] = shard(0, past)
            shards[s] = shard(s, shards[0][1])
        else:
            shards[s] = shard(s, shards[s - 1][1])
        total = ring_step(total, nt, False)
        past = total
        total = sums([[[(total, None), (shards[s][1], None)]]])[0]
        past = total if s < nt - 1 else past
    total = ring_step(total, nt, False)
    recv = total

    gubs, *egrads = expert_grads(
        ids,
        [hn2s[0], after(hn2s[1], past), *hn2s[2:]],
        cots,
        [r[2] for r in shards],
        [r[3] for r in shards],
        gmasks,
        dr if direct else width,
    )
    ms = [r[0] for r in shards]
    if direct:
        kept_x, kept_y, send_x, send_y = scatter_first(egrads[0], to(after(egrads[1], recv), 1))
        got_x, got_y = to(send_x, 2), to(send_y, 4)
        recv = after(recv, send_x)
    m_sum = ring_step(after(ms[1], recv), nt, False)

    res = attn_backward(
        ids,
        recv,
        shards[0][1],
        x,
        cots[0],
        saved[1:],
        rows,
        full,
        [gubs],
        [r[4] for r in shards],
        gmasks,
        direct,
        nt,
        dr if direct else width,
    )
    gtok, flat = res[0], res[-1]
    if direct:
        keeps, gots, m_sum = lax.optimization_barrier(
            ((kept_x, kept_y), (got_x, got_y), m_sum, gtok)
        )[:3]
        next_x, next_y, base_x, base_y = scatter_second(*keeps, *gots)
        far_x, far_y = to(next_x, 4), to(next_y, 2)
        m_sum = ring_step(sums([[[(m_sum, None), (ms[2], None)]]])[0], nt, False)
        a_odd = after(res[2], next_x)
        keeps = scatter_first(res[1], to(a_odd, 1))
        a_keep, a_send = keeps[:2], keeps[2:]
        a_got = to(a_send[0], 2), to(a_send[1], 4)
        m_sum = sums([[[(after(m_sum, a_send[0]), None), (ms[3], None)]]])[0]
        a_got, m_sum = lax.optimization_barrier((a_got, m_sum))
        m_sum = ring_step(m_sum, nt, False)
        a_next_x, a_next_y, a_base_x, a_base_y = scatter_second(*a_keep, *a_got)
        a_far = to(a_next_x, 4), to(a_next_y, 2)
        held = sums(
            [[[(b, j), (f, j)]] for b, f in ((a_base_x, a_far[0]), (a_base_y, a_far[1])) for j in (0, 1)]
        )
        far = lax.optimization_barrier(((far_x, far_y), held))[0]
        g_up, g_down = add_all([base_x, far[0]])[0], add_all([base_y, far[1]])[0]
        parts = [held[0]] + [xor_send(held[m], "tensor", nt, m) for m in range(1, nt)]
        g_qkv, g_out, g_gain, g_bias, g_outb, g_router, g_dbias, g_ub, g_qvb = finish(parts, dr, qr)
        g_outb, g_router = g_outb[0], g_router.T
    else:
        egrads = halves(egrads, 2, 1)
        g_up, g_down = add_all(scatter_dp(*egrads, nd))
        held = add_all(scatter_dp(*halves(res[1:-1], 1, 4), nd)).astype(BF)
        mine = add_all([held[0]] + [xor_send(held[m], "tensor", nt, m) for m in range(1, nt)])
        g_qkv, g_out = mine[: 3 * dr].reshape(3, dr, LANES), mine[3 * dr :]
        for s in range(2, nt):
            m_sum = ring_step(add_all([m_sum, ms[s]]).astype(BF), nt, False)
        g_ub = lax.dynamic_slice(lax.psum(flat, "dp"), (UBIAS, me * fr), (EXPERTS, fr))
        flat = lax.psum(flat, ("dp", "tensor"))
        cut = lax.dynamic_slice(flat, (0, me * dr), (NROWS, dr))
        g_gain, g_bias, g_outb = cut[0:2], cut[2:4], cut[4]
        g_router, g_dbias = cut[ROUTER : ROUTER + 4].T, cut[DBIAS : DBIAS + 4]
        g_qvb = lax.dynamic_slice(flat, (QVB, (met * nd + me) * qr), (2, qr))

    def rows_of(v):
        return jnp.concatenate([v[i * PAD : i * PAD + SEQ] for i in range(nimg)])

    layer_out = rows_of(saved[1] + (m_sum.astype(F4) + ms[0].astype(F4)))
    grad_tokens = rows_of(gtok)

    return (
        layer_out,
        grad_tokens,
        g_gain,
        g_bias,
        g_qkv,
        g_qvb,
        g_out.T,
        g_outb,
        g_router,
        g_up,
        g_ub,
        g_down.transpose(0, 2, 1),
        g_dbias,
    )


def solution(mesh):
    nd, nt = mesh.shape["dp"], mesh.shape["tensor"]
    placed = (
        P(("dp", "tensor"), None),
        P(("dp", "tensor"), None),
        P("dp", None),
        P("dp", None),
        P(None, "dp"),
        P(None, "dp"),
        P(None, "dp", "tensor"),
        P(None, ("tensor", "dp")),
        P("tensor", "dp"),
        P("dp"),
        P("dp", None),
        P(None, "dp", "tensor"),
        P(None, ("tensor", "dp")),
        P(None, "tensor", "dp"),
        P(None, "dp"),
    )
    return jax.shard_map(
        partial(per_device, nd, nt),
        mesh=mesh,
        in_specs=placed,
        out_specs=(
            P(("dp", "tensor"), None),
            P(("dp", "tensor"), None),
            P(None, "dp"),
            P(None, "dp"),
            P(None, "dp", "tensor"),
            P(None, ("tensor", "dp")),
            P("tensor", "dp"),
            P("dp"),
            P("dp", None),
            P(None, "dp", "tensor"),
            P(None, ("tensor", "dp")),
            P(None, "tensor", "dp"),
            P(None, "dp"),
        ),
        check_vma=False,
    )
```

profile of v0, /device:TPU:0, one launch (start us, length us, event | category | flops | bytes accessed | tf_op | source)
XLA Modules:
  0.0 174.7 jit_solution(17514262239317432409)
XLA Ops:
  0.7 0.8 pad_maximum_fusion.6
  1.5 2.2 %concatenate.42 = bf16[16,64]{1,0:T(8,128)(2,1)S(1)} concatenate(bf16[2,64]{1,0:T(2,128)(2,1)} %param.20, bf16[2,64]{1,0:T(2,128)(2,1)} %param.21, bf16[1,64]{1,0:T(2,128)(2,1)} %bitcast.59, bf16[4,64]{1,0:T(4,128)(2,1)} %bitcast.58, bf16[4,64]{1,0:T(4,128)(2,1)} %param.30, bf16[3,64]{1,0:T(4,128)(2,1)S(1)} %broadcast_in_dim.18), dimensions={0} | concatenate | bytes 4096 | tf_op jit(solution)/shard_map/concatenate | solution.py:794
  3.7 0.8 fusion.11
  4.5 5.1 %collective-permute-start.2 = (bf16[272,128]{1,0:T(8,128)(2,1)S(1)}, bf16[272,128]{1,0:T(8,128)(2,1)S(1)}, u32[]{:S(2)}, u32[]{:S(2)}) collective-permute-start(bf16[272,128]{1,0:T(8,128)(2,1)S(1)} %fusion.11), channel_id=1, source_target_pairs={{0,3},{1,2},{2,1},{3,0},{4,7},{5,6},{6,5},{7,4},{8,11},{9,10},{10,... | collective-permute-start | bytes 208904 | tf_op jit(solution)/shard_map/ppermute | solution.py:46
  10.2 1.7 collective-permute-start.4
  11.9 1.5 collective-permute-start.3
  13.4 1.0 slice.49
  14.4 1.1 slice_select_fusion
  15.6 2.3 %collective-permute-done.4 = bf16[4,64,512]{2,1,0:T(8,128)(2,1)S(1)} collective-permute-done((bf16[4,64,512]{2,1,0:T(8,128)(2,1)}, bf16[4,64,512]{2,1,0:T(8,128)(2,1)S(1)}, u32[]{:S(2)}, u32[]{:S(2)}) %collective-permute-start.4) | collective-permute-done | bytes 262176 | tf_op jit(solution)/shard_map/ppermute | solution.py:46
  17.9 1.2 collective-permute-done.3
  19.2 0.8 fusion.12
  20.0 1.4 collective-permute-start.9
  21.9 1.5 collective-permute-start.5
  25.3 1.5 collective-permute-start.11
  26.9 3.4 %collective-permute-done.9.cot_ref.refs_5_ = bf16[400,512]{1,0:T(8,128)(2,1)S(1)} collective-permute-done((bf16[400,512]{1,0:T(8,128)(2,1)S(1)}, bf16[400,512]{1,0:T(8,128)(2,1)S(1)}, u32[]{:S(2)}, u32[]{:S(2)}) %collective-permute-start.9) | collective-permute-done | bytes 409632 | tf_op jit(solution)/shard_map/ppermute | solution.py:56
  31.7 1.6 collective-permute-start.8
  33.8 1.0 maximum_bitcast_fusion.1
  35.0 1.8 %collective-permute-done.8 = bf16[2,272,128]{2,1,0:T(8,128)(2,1)S(1)} collective-permute-done((bf16[2,272,128]{2,1,0:T(8,128)(2,1)S(1)}, bf16[2,272,128]{2,1,0:T(8,128)(2,1)S(1)}, u32[]{:S(2)}, u32[]{:S(2)}) %collective-permute-start.8) | collective-permute-done | bytes 139296 | tf_op jit(solution)/shard_map/ppermute | solution.py:46
  36.8 1.6 collective-permute-done.7
  38.4 1.2 collective-permute-done.10.cot_ref.refs_6_
  39.9 1.9 %collective-permute-start.14 = (bf16[400,512]{1,0:T(8,128)(2,1)S(1)}, bf16[400,512]{1,0:T(8,128)(2,1)S(1)}, u32[]{:S(2)}, u32[]{:S(2)}) collective-permute-start(bf16[400,512]{1,0:T(8,128)(2,1)S(1)} %collective-permute-done.10.cot_ref.refs_6_), channel_id=1, source_target_pairs={{0,1},{1,3},{3,2},{2,0},{4,5},{5,7},{7,6},{6,4},{8,9},{9,11},{11,1... | collective-permute-start | bytes 1228808 | tf_op jit(solution)/shard_map/ppermute | solution.py:56
  43.0 2.9 %assemble.1 = (bf16[4,512,512]{2,1,0:T(8,128)(2,1)S(1)}, f32[32,512]{1,0:T(8,128)S(1)}) custom-call(s32[6]{0:T(128)S(1)} %pad_add_fusion.ids, bf16[4,4,272,128]{3,2,1,0:T(8,128)(2,1)S(1)} %pad_maximum_fusion.refs_0_, bf16[4,4,272,128]{3,2,1,0:T(8,128)(2,1)S(1)} %collective-permute-done.13.refs_1_), custom_call_target="tpu_custom_call" | custom-call | bytes 66000 | tf_op jit(solution)/shard_map/assemble/pallas_call | solution.py:336
  45.9 4.3 %attn_forward.1 = (bf16[400,512]{1,0:T(8,128)(2,1)S(1)}, f32[400,512]{1,0:T(8,128)}, bf16[400,512]{1,0:T(8,128)(2,1)}, bf16[400,512]{1,0:T(8,128)(2,1)}, bf16[40...) custom-call(bf16[400,512]{1,0:T(8,128)(2,1)S(1)} %fusion.2.x_ref.refs_2_, ...), custom_call_target="tpu_custom_call" | custom-call | bytes 297000 | tf_op jit(solution)/shard_map/attn_forward/pallas_call | solution.py:411
  50.3 2.4 %collective-permute-done.14.cot_ref.refs_7_ = bf16[400,512]{1,0:T(8,128)(2,1)S(1)} collective-permute-done((bf16[400,512]{1,0:T(8,128)(2,1)S(1)}, bf16[400,512]{1,0:T(8,128)(2,1)S(1)}, u32[]{:S(2)}, u32[]{:S(2)}) %collective-permute-start.14) | collective-permute-done | bytes 409632 | tf_op jit(solution)/shard_map/ppermute | solution.py:56
  52.7 1.0 collective-permute-start.15
  53.7 0.9 collective-permute-start.20
  55.3 3.4 %collective-permute-done.20 = bf16[2,64,512]{2,1,0:T(8,128)(2,1)S(1)} collective-permute-done((bf16[2,64,512]{2,1,0:T(8,128)(2,1)S(1)}, bf16[2,64,512]{2,1,0:T(8,128)(2,1)S(1)}, u32[]{:S(2)}, u32[]{:S(2)}) %collective-permute-start.20) | collective-permute-done | bytes 131104 | tf_op jit(solution)/shard_map/ppermute | solution.py:46
  58.7 0.9 collective-permute-done.19
  59.8 4.7 %collective-permute-done.15.hn2_ref.refs_1_ = bf16[400,512]{1,0:T(8,128)(2,1)S(1)} collective-permute-done((bf16[400,512]{1,0:T(8,128)(2,1)S(1)}, bf16[400,512]{1,0:T(8,128)(2,1)S(1)}, u32[]{:S(2)}, u32[]{:S(2)}) %collective-permute-start.15) | collective-permute-done | bytes 409632 | tf_op jit(solution)/shard_map/ppermute | solution.py:56
  64.9 1.2 gather_experts.2.up_ref
  66.1 1.0 collective-permute-done.21.refs_1_
  67.2 1.2 gather_experts.3.dn_ref
  68.4 7.7 %expert_shard.4 = (bf16[400,512]{1,0:T(8,128)(2,1)S(1)}, bf16[400,512]{1,0:T(8,128)(2,1)S(1)}, bf16[400,2048]{1,0:T(8,128)(2,1)S(1)}, bf16[400,2048]{1,0:T(8,128)(2,1)S(1)}, f32[16,512]{1,0:T(8,128)S(1)}) custom-call(s32[6]{0:T(128)S(1)} %pad_add_fusion.ids, s32[8,200,2]{2,1,0:T(8,128)S(1)} %pad.26.keep_ref, ...), custom_call_target="tpu_custom_call" | custom-call | bytes 231000 | tf_op jit(solution)/shard_map/expert_shard/pallas_call | solution.py:518
  76.1 2.4 %collective-permute-start.22 = (bf16[400,512]{1,0:T(8,128)(2,1)S(1)}, bf16[400,512]{1,0:T(8,128)(2,1)S(1)}, u32[]{:S(2)}, u32[]{:S(2)}) collective-permute-start(bf16[400,512]{1,0:T(8,128)(2,1)S(1)} %get-tuple-element.146), channel_id=1, source_target_pairs={{0,1},{1,3},{3,2},{2,0},{4,5},{5,7},{7,6},{6,4},{8,9},{9,11},{11,1... | collective-permute-start | bytes 1228808 | tf_op jit(solution)/shard_map/ppermute | solution.py:56
  78.5 1.4 collective-permute-start.25
  79.9 7.6 %expert_shard.5 = (bf16[400,512]{1,0:T(8,128)(2,1)S(1)}, bf16[400,512]{1,0:T(8,128)(2,1)S(1)}, bf16[400,2048]{1,0:T(8,128)(2,1)S(1)}, bf16[400,2048]{1,0:T(8,128)(2,1)S(1)}, f32[16,512]{1,0:T(8,128)S(1)}) custom-call(s32[6]{0:T(128)S(1)} %pad_add_fusion.ids, s32[8,200,2]{2,1,0:T(8,128)S(1)} %pad.26.keep_ref, ...), custom_call_target="tpu_custom_call" | custom-call | bytes 231000 | tf_op jit(solution)/shard_map/expert_shard/pallas_call | solution.py:518
  87.5 1.8 %collective-permute-done.22.refs_0_ = bf16[400,512]{1,0:T(8,128)(2,1)S(1)} collective-permute-done((bf16[400,512]{1,0:T(8,128)(2,1)S(1)}, bf16[400,512]{1,0:T(8,128)(2,1)S(1)}, u32[]{:S(2)}, u32[]{:S(2)}) %collective-permute-start.22) | collective-permute-done | bytes 409632 | tf_op jit(solution)/shard_map/ppermute | solution.py:56
  89.4 1.7 collective-permute-start.24
  91.2 7.8 %expert_shard.6 = (bf16[400,512]{1,0:T(8,128)(2,1)S(1)}, bf16[400,512]{1,0:T(8,128)(2,1)S(1)}, bf16[400,2048]{1,0:T(8,128)(2,1)S(1)}, bf16[400,2048]{1,0:T(8,128)(2,1)S(1)}, f32[16,512]{1,0:T(8,128)S(1)}) custom-call(s32[6]{0:T(128)S(1)} %pad_add_fusion.ids, s32[8,200,2]{2,1,0:T(8,128)S(1)} %pad.26.keep_ref, ...), custom_call_target="tpu_custom_call" | custom-call | bytes 231000 | tf_op jit(solution)/shard_map/expert_shard/pallas_call | solution.py:518
  99.0 7.6 %expert_shard.7 = (bf16[400,512]{1,0:T(8,128)(2,1)S(1)}, bf16[400,512]{1,0:T(8,128)(2,1)S(1)}, bf16[400,2048]{1,0:T(8,128)(2,1)S(1)}, bf16[400,2048]{1,0:T(8,128)(2,1)S(1)}, f32[16,512]{1,0:T(8,128)S(1)}) custom-call(s32[6]{0:T(128)S(1)} %pad_add_fusion.ids, s32[8,200,2]{2,1,0:T(8,128)S(1)} %pad.26.keep_ref, ...), custom_call_target="tpu_custom_call" | custom-call | bytes 231000 | tf_op jit(solution)/shard_map/expert_shard/pallas_call | solution.py:518
  106.7 2.4 %collective-permute-start.26 = (bf16[400,512]{1,0:T(8,128)(2,1)S(1)}, bf16[400,512]{1,0:T(8,128)(2,1)S(1)}, u32[]{:S(2)}, u32[]{:S(2)}) collective-permute-start(bf16[400,512]{1,0:T(8,128)(2,1)S(1)} %sums.10), channel_id=1, source_target_pairs={{0,1},{1,3},{3,2},{2,0},{4,5},{5,7},{7,6},{6,4},{8,9},{9,11},{11,1... | collective-permute-start | bytes 1228808 | tf_op jit(solution)/shard_map/ppermute | solution.py:56
  109.1 11.1 %expert_grads.1 = (f32[4,1,512]{2,1,0:T(1,128)S(1)}, bf16[4,2,4,64,512]{4,3,2,1,0:T(8,128)(2,1)S(1)}, bf16[4,2,4,64,512]{4,3,2,1,0:T(8,128)(2,1)S(1)}) custom-call(s32[6]{0:T(128)S(1)} %pad_add_fusion.ids, bf16[400,512]{1,0:T(8,128)(2,1)S(1)} %get-tuple-element.149.hn2_ref.refs_0_, bf16[400,512]{1,0:T(8,128)(2,1)S(1)} %collective-permute-done.15.hn2_ref.refs_1_, ...), custom_call_target="tpu_custom_call" | custom-call | bytes 297000 | tf_op jit(solution)/shard_map/expert_grads/pallas_call | solution.py:560
  120.2 4.1 %collective-permute-done.27.refs_1_ = bf16[4,2,4,64,512]{4,3,2,1,0:T(8,128)(2,1)S(1)} collective-permute-done((bf16[4,2,4,64,512]{4,3,2,1,0:T(8,128)(2,1)S(1)}, bf16[4,2,4,64,512]{4,3,2,1,0:T(8,128)(2,1)S(1)}, u32[]{:S(2)}, u32[]{:S(2)}) %collective-permute-start.27) | collective-permute-done | bytes 2097184 | tf_op jit(solution)/shard_map/ppermute | solution.py:46
  124.9 0.8 collective-permute-start.29
  125.7 1.5 collective-permute-start.28
  127.2 0.9 collective-permute-start.30
  128.1 10.2 %attn_backward.1 = (f32[400,512]{1,0:T(8,128)S(1)}, bf16[4,4,272,128]{3,2,1,0:T(8,128)(2,1)S(1)}, bf16[4,4,272,128]{3,2,1,0:T(8,128)(2,1)S(1)}, f32[32,512]{1,0:T(8,128)}) custom-call(s32[6]{0:T(128)S(1)} %pad_add_fusion.ids, bf16[400,512]{1,0:T(8,128)(2,1)S(1)} %collective-permute-done.26.refs_0_, bf16[400,512]{1,0:T(8,128)(2,1)S(1)} %get-tuple-element.150.refs_1_, ...), custom_call_target="tpu_custom_call" | custom-call | bytes 528000 | tf_op jit(solution)/shard_map/attn_backward/pallas_call | solution.py:713
  139.8 0.9 collective-permute-start.34
  140.8 1.7 collective-permute-done.31.refs_1_
  142.7 1.4 collective-permute-start.33
  144.1 1.5 collective-permute-start.32
  146.9 5.8 %collective-permute-done.34.refs_0_ = bf16[400,512]{1,0:T(8,128)(2,1)S(1)} collective-permute-done((bf16[400,512]{1,0:T(8,128)(2,1)S(1)}, bf16[400,512]{1,0:T(8,128)(2,1)S(1)}, u32[]{:S(2)}, u32[]{:S(2)}) %collective-permute-start.34) | collective-permute-done | bytes 409632 | tf_op jit(solution)/shard_map/ppermute | solution.py:56
  152.8 0.9 collective-permute-done.32.refs_1_
  153.8 0.8 collective-permute-start.36
  154.6 1.5 collective-permute-start.37
  156.0 0.9 collective-permute-start.35
  157.0 3.1 %collective-permute-done.36.refs_1_ = bf16[2,272,128]{2,1,0:T(8,128)(2,1)S(1)} collective-permute-done((bf16[2,272,128]{2,1,0:T(8,128)(2,1)S(1)}, bf16[2,272,128]{2,1,0:T(8,128)(2,1)S(1)}, u32[]{:S(2)}, u32[]{:S(2)}) %collective-permute-start.36) | collective-permute-done | bytes 139296 | tf_op jit(solution)/shard_map/ppermute | solution.py:46
  160.1 1.0 collective-permute-done.37.refs_3_
  161.2 1.0 collective-permute-start.38
  162.6 3.1 %collective-permute-start.40 = (bf16[272,128]{1,0:T(8,128)(2,1)S(1)}, bf16[272,128]{1,0:T(8,128)(2,1)S(1)}, u32[]{:S(2)}, u32[]{:S(2)}) collective-permute-start(bf16[272,128]{1,0:T(8,128)(2,1)S(1)} %get-tuple-element.210), channel_id=1, source_target_pairs={{0,3},{1,2},{2,1},{3,0},{4,7},{5,6},{6,5},{7,4},{8,11},{9,10},{10,... | collective-permute-start | bytes 208904 | tf_op jit(solution)/shard_map/ppermute | solution.py:46
  165.7 1.1 add_bitcast_fusion
  166.8 2.1 %collective-permute-done.38.refs_1_ = bf16[272,128]{1,0:T(8,128)(2,1)S(1)} collective-permute-done((bf16[272,128]{1,0:T(8,128)(2,1)S(1)}, bf16[272,128]{1,0:T(8,128)(2,1)S(1)}, u32[]{:S(2)}, u32[]{:S(2)}) %collective-permute-start.38) | collective-permute-done | bytes 69664 | tf_op jit(solution)/shard_map/ppermute | solution.py:46
  168.9 3.5 %collective-permute-done.39.refs_2_ = bf16[272,128]{1,0:T(8,128)(2,1)S(1)} collective-permute-done((bf16[272,128]{1,0:T(8,128)(2,1)S(1)}, bf16[272,128]{1,0:T(8,128)(2,1)S(1)}, u32[]{:S(2)}, u32[]{:S(2)}) %collective-permute-start.39) | collective-permute-done | bytes 69664 | tf_op jit(solution)/shard_map/ppermute | solution.py:46
  173.3 1.3 pad_maximum_fusion.3
  (96 shorter events, 13.4 us)
Async XLA Ops:
  0.6 20.7 %copy-start.9 = (s32[1576,2]{0,1:T(2,128)S(1)}, s32[1576,2]{0,1:T(2,128)}, u32[]{:S(2)}) copy-start(s32[1576,2]{0,1:T(2,128)} %param.19) | copy-start | bytes 37828
  0.7 20.7 %copy-start.8 = (s32[1576,2]{0,1:T(2,128)S(1)}, s32[1576,2]{0,1:T(2,128)}, u32[]{:S(2)}) copy-start(s32[1576,2]{0,1:T(2,128)} %param.18) | copy-start | bytes 37828
  4.5 11.1 %collective-permute-start.2 = (bf16[272,128]{1,0:T(8,128)(2,1)S(1)}, bf16[272,128]{1,0:T(8,128)(2,1)S(1)}, u32[]{:S(2)}, u32[]{:S(2)}) collective-permute-start(bf16[272,128]{1,0:T(8,128)(2,1)S(1)} %fusion.11), channel_id=1, source_target_pairs={{0,3},{1,2},{2,1},{3,0},{4,7},{5,6},{6,5},{7,4},{8,11},{9,10},{10,... | collective-permute-start | bytes 208904 | tf_op jit(solution)/shard_map/ppermute | solution.py:46
  9.6 6.0 %collective-permute-start.1 = (bf16[272,128]{1,0:T(8,128)(2,1)S(1)}, bf16[272,128]{1,0:T(8,128)(2,1)S(1)}, u32[]{:S(2)}, u32[]{:S(2)}) collective-permute-start(bf16[272,128]{1,0:T(8,128)(2,1)S(1)} %fusion.11), channel_id=1, source_target_pairs={{0,2},{1,3},{2,0},{3,1},{4,6},{5,7},{6,4},{7,5},{8,10},{9,11},{10,... | collective-permute-start | bytes 208904 | tf_op jit(solution)/shard_map/ppermute | solution.py:46
  9.6 6.0 %collective-permute-start = (bf16[272,128]{1,0:T(8,128)(2,1)S(1)}, bf16[272,128]{1,0:T(8,128)(2,1)S(1)}, u32[]{:S(2)}, u32[]{:S(2)}) collective-permute-start(bf16[272,128]{1,0:T(8,128)(2,1)S(1)} %fusion.11), channel_id=1, source_target_pairs={{0,1},{1,0},{2,3},{3,2},{4,5},{5,4},{6,7},{7,6},{8,9},{9,8},{10,11... | collective-permute-start | bytes 208904 | tf_op jit(solution)/shard_map/ppermute | solution.py:46
  10.2 7.7 %collective-permute-start.4 = (bf16[4,64,512]{2,1,0:T(8,128)(2,1)}, bf16[4,64,512]{2,1,0:T(8,128)(2,1)S(1)}, u32[]{:S(2)}, u32[]{:S(2)}) collective-permute-start(bf16[4,64,512]{2,1,0:T(8,128)(2,1)} %param.27), channel_id=1, source_target_pairs={{0,16},{4,20},{8,24},{12,28},{16,0},{20,4},{24,8},{28,12},{1,17},{... | collective-permute-start | bytes 786440 | tf_op jit(solution)/shard_map/ppermute | solution.py:46
  11.9 7.3 %collective-permute-start.3 = (bf16[4,64,512]{2,1,0:T(8,128)(2,1)}, bf16[4,64,512]{2,1,0:T(8,128)(2,1)S(1)}, u32[]{:S(2)}, u32[]{:S(2)}) collective-permute-start(bf16[4,64,512]{2,1,0:T(8,128)(2,1)} %param.27), channel_id=1, source_target_pairs={{0,8},{4,12},{8,0},{12,4},{16,24},{20,28},{24,16},{28,20},{1,9},{5... | collective-permute-start | bytes 786440 | tf_op jit(solution)/shard_map/ppermute | solution.py:46
  13.4 17.7 %copy-start.5 = (bf16[394,512]{1,0:T(8,128)(2,1)S(1)}, bf16[394,512]{1,0:T(8,128)(2,1)}, u32[]{:S(2)}) copy-start(bf16[394,512]{1,0:T(8,128)(2,1)} %param.16) | copy-start | bytes 1210372
  17.9 8.9 %copy-start.1 = (bf16[4,64,512]{2,1,0:T(8,128)(2,1)}, bf16[4,64,512]{2,1,0:T(8,128)(2,1)S(1)}, u32[]{:S(2)}) copy-start(bf16[4,64,512]{2,1,0:T(8,128)(2,1)S(1)} %collective-permute-done.4) | copy-start | bytes 786436
  19.2 7.7 %copy-start.3 = (bf16[4,64,512]{2,1,0:T(8,128)(2,1)}, bf16[4,64,512]{2,1,0:T(8,128)(2,1)S(1)}, u32[]{:S(2)}) copy-start(bf16[4,64,512]{2,1,0:T(8,128)(2,1)S(1)} %collective-permute-done.3) | copy-start | bytes 786436
  20.0 10.3 %collective-permute-start.9 = (bf16[400,512]{1,0:T(8,128)(2,1)S(1)}, bf16[400,512]{1,0:T(8,128)(2,1)S(1)}, u32[]{:S(2)}, u32[]{:S(2)}) collective-permute-start(bf16[400,512]{1,0:T(8,128)(2,1)S(1)} %fusion.3.cot_ref.refs_4_.refs_3_), channel_id=1, source_target_pairs={{0,1},{1,3},{3,2},{2,0},{4,5},{5,7},{7,6},{6,4},{8,9},{9,11},{11,1... | collective-permute-start | bytes 1228808 | tf_op jit(solution)/shard_map/ppermute | solution.py:56
  21.4 10.3 %collective-permute-start.6 = (bf16[4,272,128]{2,1,0:T(8,128)(2,1)}, bf16[4,272,128]{2,1,0:T(8,128)(2,1)S(1)}, u32[]{:S(2)}, u32[]{:S(2)}) collective-permute-start(bf16[4,272,128]{2,1,0:T(8,128)(2,1)} %get-tuple-element.230), channel_id=1, source_target_pairs={{0,16},{4,20},{8,24},{12,28},{16,0},{20,4},{24,8},{28,12},{1,17},{... | collective-permute-start | bytes 835592 | tf_op jit(solution)/shard_map/ppermute | solution.py:46
  21.9 11.3 %collective-permute-start.5 = (bf16[4,272,128]{2,1,0:T(8,128)(2,1)}, bf16[4,272,128]{2,1,0:T(8,128)(2,1)S(1)}, u32[]{:S(2)}, u32[]{:S(2)}) collective-permute-start(bf16[4,272,128]{2,1,0:T(8,128)(2,1)} %get-tuple-element.230), channel_id=1, source_target_pairs={{0,8},{4,12},{8,0},{12,4},{16,24},{20,28},{24,16},{28,20},{1,9},{5... | collective-permute-start | bytes 835592 | tf_op jit(solution)/shard_map/ppermute | solution.py:46
  24.8 9.0 %collective-permute-start.12 = (bf16[2,64,512]{2,1,0:T(8,128)(2,1)}, bf16[2,64,512]{2,1,0:T(8,128)(2,1)}, u32[]{:S(2)}, u32[]{:S(2)}) collective-permute-start(bf16[2,64,512]{2,1,0:T(8,128)(2,1)} %slice.51), channel_id=1, source_target_pairs={{0,8},{4,12},{8,0},{12,4},{16,24},{20,28},{24,16},{28,20},{1,9},{5... | collective-permute-start | bytes 393224 | tf_op jit(solution)/shard_map/ppermute | solution.py:46
  25.3 8.5 %collective-permute-start.11 = (bf16[2,64,512]{2,1,0:T(8,128)(2,1)S(1)}, bf16[2,64,512]{2,1,0:T(8,128)(2,1)}, u32[]{:S(2)}, u32[]{:S(2)}) collective-permute-start(bf16[2,64,512]{2,1,0:T(8,128)(2,1)S(1)} %slice.50), channel_id=1, source_target_pairs={{0,16},{4,20},{8,24},{12,28},{16,0},{20,4},{24,8},{28,12},{1,17},{... | collective-permute-start | bytes 393224 | tf_op jit(solution)/shard_map/ppermute | solution.py:46
  30.2 9.4 %collective-permute-start.10 = (bf16[400,512]{1,0:T(8,128)(2,1)S(1)}, bf16[400,512]{1,0:T(8,128)(2,1)S(1)}, u32[]{:S(2)}, u32[]{:S(2)}) collective-permute-start(bf16[400,512]{1,0:T(8,128)(2,1)S(1)} %collective-permute-done.9.cot_ref.refs_5_), channel_id=1, source_target_pairs={{0,1},{1,3},{3,2},{2,0},{4,5},{5,7},{7,6},{6,4},{8,9},{9,11},{11,1... | collective-permute-start | bytes 1228808 | tf_op jit(solution)/shard_map/ppermute | solution.py:56
  31.5 3.3 %copy-start.2 = (bf16[4,64,512]{2,1,0:T(8,128)(2,1)S(1)}, bf16[4,64,512]{2,1,0:T(8,128)(2,1)}, u32[]{:S(2)}) copy-start(bf16[4,64,512]{2,1,0:T(8,128)(2,1)} %copy-done.1) | copy-start | bytes 786436
  31.5 3.3 %copy-start.4 = (bf16[4,64,512]{2,1,0:T(8,128)(2,1)S(1)}, bf16[4,64,512]{2,1,0:T(8,128)(2,1)}, u32[]{:S(2)}) copy-start(bf16[4,64,512]{2,1,0:T(8,128)(2,1)} %copy-done.3) | copy-start | bytes 786436
  31.5 3.3 %copy-start.6 = (bf16[4,64,512]{2,1,0:T(8,128)(2,1)S(1)}, bf16[4,64,512]{2,1,0:T(8,128)(2,1)}, u32[]{:S(2)}) copy-start(bf16[4,64,512]{2,1,0:T(8,128)(2,1)} %param.27) | copy-start | bytes 786436
  31.7 5.1 %collective-permute-start.8 = (bf16[2,272,128]{2,1,0:T(8,128)(2,1)S(1)}, bf16[2,272,128]{2,1,0:T(8,128)(2,1)S(1)}, u32[]{:S(2)}, u32[]{:S(2)}) collective-permute-start(bf16[2,272,128]{2,1,0:T(8,128)(2,1)S(1)} %slice.59), channel_id=1, source_target_pairs={{0,8},{4,12},{8,0},{12,4},{16,24},{20,28},{24,16},{28,20},{1,9},{5... | collective-permute-start | bytes 417800 | tf_op jit(solution)/shard_map/ppermute | solution.py:46
  33.3 5.1 %collective-permute-start.7 = (bf16[2,272,128]{2,1,0:T(8,128)(2,1)S(1)}, bf16[2,272,128]{2,1,0:T(8,128)(2,1)S(1)}, u32[]{:S(2)}, u32[]{:S(2)}) collective-permute-start(bf16[2,272,128]{2,1,0:T(8,128)(2,1)S(1)} %slice.58), channel_id=1, source_target_pairs={{0,16},{4,20},{8,24},{12,28},{16,0},{20,4},{24,8},{28,12},{1,17},{... | collective-permute-start | bytes 417800 | tf_op jit(solution)/shard_map/ppermute | solution.py:46
  35.0 6.8 %copy-start.7 = (bf16[4,512,64]{1,2,0:T(8,128)(2,1)S(1)}, bf16[4,512,64]{1,2,0:T(8,128)(2,1)}, u32[]{:S(2)}) copy-start(bf16[4,512,64]{1,2,0:T(8,128)(2,1)} %param.29) | copy-start | bytes 786436
  39.8 3.2 %collective-permute-start.13 = (bf16[4,4,272,128]{3,2,1,0:T(8,128)(2,1)S(1)}, bf16[4,4,272,128]{3,2,1,0:T(8,128)(2,1)S(1)}, u32[]{:S(2)}, u32[]{:S(2)}) collective-permute-start(bf16[4,4,272,128]{3,2,1,0:T(8,128)(2,1)S(1)} %pad_maximum_fusion.refs_0_), channel_id=1, source_target_pairs={{0,4},{4,0},{8,12},{12,8},{16,20},{20,16},{24,28},{28,24},{1,5},{5... | collective-permute-start | bytes 3342344 | tf_op jit(solution)/shard_map/ppermute | solution.py:46
  39.9 12.8 %collective-permute-start.14 = (bf16[400,512]{1,0:T(8,128)(2,1)S(1)}, bf16[400,512]{1,0:T(8,128)(2,1)S(1)}, u32[]{:S(2)}, u32[]{:S(2)}) collective-permute-start(bf16[400,512]{1,0:T(8,128)(2,1)S(1)} %collective-permute-done.10.cot_ref.refs_6_), channel_id=1, source_target_pairs={{0,1},{1,3},{3,2},{2,0},{4,5},{5,7},{7,6},{6,4},{8,9},{9,11},{11,1... | collective-permute-start | bytes 1228808 | tf_op jit(solution)/shard_map/ppermute | solution.py:56
  41.8 11.8 %collective-permute-start.18 = (bf16[4,64,512]{2,1,0:T(8,128)(2,1)S(1)}, bf16[4,64,512]{2,1,0:T(8,128)(2,1)S(1)}, u32[]{:S(2)}, u32[]{:S(2)}) collective-permute-start(bf16[4,64,512]{2,1,0:T(8,128)(2,1)S(1)} %bitcast.51), channel_id=1, source_target_pairs={{0,16},{4,20},{8,24},{12,28},{16,0},{20,4},{24,8},{28,12},{1,17},{... | collective-permute-start | bytes 786440 | tf_op jit(solution)/shard_map/ppermute | solution.py:46
  42.4 11.2 %collective-permute-start.17 = (bf16[4,64,512]{2,1,0:T(8,128)(2,1)S(1)}, bf16[4,64,512]{2,1,0:T(8,128)(2,1)S(1)}, u32[]{:S(2)}, u32[]{:S(2)}) collective-permute-start(bf16[4,64,512]{2,1,0:T(8,128)(2,1)S(1)} %bitcast.52), channel_id=1, source_target_pairs={{0,8},{4,12},{8,0},{12,4},{16,24},{20,28},{24,16},{28,20},{1,9},{5... | collective-permute-start | bytes 786440 | tf_op jit(solution)/shard_map/ppermute | solution.py:46
  52.7 11.9 %collective-permute-start.15 = (bf16[400,512]{1,0:T(8,128)(2,1)S(1)}, bf16[400,512]{1,0:T(8,128)(2,1)S(1)}, u32[]{:S(2)}, u32[]{:S(2)}) collective-permute-start(bf16[400,512]{1,0:T(8,128)(2,1)S(1)} %get-tuple-element.149.hn2_ref.refs_0_), channel_id=1, source_target_pairs={{0,1},{1,3},{3,2},{2,0},{4,5},{5,7},{7,6},{6,4},{8,9},{9,11},{11,1... | collective-permute-start | bytes 1228808 | tf_op jit(solution)/shard_map/ppermute | solution.py:56
  53.7 5.0 %collective-permute-start.20 = (bf16[2,64,512]{2,1,0:T(8,128)(2,1)S(1)}, bf16[2,64,512]{2,1,0:T(8,128)(2,1)S(1)}, u32[]{:S(2)}, u32[]{:S(2)}) collective-permute-start(bf16[2,64,512]{2,1,0:T(8,128)(2,1)S(1)} %slice.53), channel_id=1, source_target_pairs={{0,8},{4,12},{8,0},{12,4},{16,24},{20,28},{24,16},{28,20},{1,9},{5... | collective-permute-start | bytes 393224 | tf_op jit(solution)/shard_map/ppermute | solution.py:46
  54.6 5.0 %collective-permute-start.19 = (bf16[2,64,512]{2,1,0:T(8,128)(2,1)S(1)}, bf16[2,64,512]{2,1,0:T(8,128)(2,1)S(1)}, u32[]{:S(2)}, u32[]{:S(2)}) collective-permute-start(bf16[2,64,512]{2,1,0:T(8,128)(2,1)S(1)} %slice.52), channel_id=1, source_target_pairs={{0,16},{4,20},{8,24},{12,28},{16,0},{20,4},{24,8},{28,12},{1,17},{... | collective-permute-start | bytes 393224 | tf_op jit(solution)/shard_map/ppermute | solution.py:46
  55.3 9.2 %collective-permute-start.16 = (bf16[4,4,64,512]{3,2,1,0:T(8,128)(2,1)S(1)}, bf16[4,4,64,512]{3,2,1,0:T(8,128)(2,1)S(1)}, u32[]{:S(2)}, u32[]{:S(2)}) collective-permute-start(bf16[4,4,64,512]{3,2,1,0:T(8,128)(2,1)S(1)} %pad_maximum_fusion.1.refs_0_), channel_id=1, source_target_pairs={{0,4},{4,0},{8,12},{12,8},{16,20},{20,16},{24,28},{28,24},{1,5},{5... | collective-permute-start | bytes 3145736 | tf_op jit(solution)/shard_map/ppermute | solution.py:46
  64.5 2.7 %collective-permute-start.21 = (bf16[4,4,64,512]{3,2,1,0:T(8,128)(2,1)S(1)}, bf16[4,4,64,512]{3,2,1,0:T(8,128)(2,1)S(1)}, u32[]{:S(2)}, u32[]{:S(2)}) collective-permute-start(bf16[4,4,64,512]{3,2,1,0:T(8,128)(2,1)S(1)} %pad_maximum_fusion.2.refs_0_), channel_id=1, source_target_pairs={{0,4},{4,0},{8,12},{12,8},{16,20},{20,16},{24,28},{28,24},{1,5},{5... | collective-permute-start | bytes 3145736 | tf_op jit(solution)/shard_map/ppermute | solution.py:46
  64.5 13.9 %collective-permute-start.23 = (bf16[400,512]{1,0:T(8,128)(2,1)S(1)}, bf16[400,512]{1,0:T(8,128)(2,1)S(1)}, u32[]{:S(2)}, u32[]{:S(2)}) collective-permute-start(bf16[400,512]{1,0:T(8,128)(2,1)S(1)} %collective-permute-done.15.hn2_ref.refs_1_), channel_id=1, source_target_pairs={{0,1},{1,3},{3,2},{2,0},{4,5},{5,7},{7,6},{6,4},{8,9},{9,11},{11,1... | collective-permute-start | bytes 1228808 | tf_op jit(solution)/shard_map/ppermute | solution.py:56
  76.1 13.3 %collective-permute-start.22 = (bf16[400,512]{1,0:T(8,128)(2,1)S(1)}, bf16[400,512]{1,0:T(8,128)(2,1)S(1)}, u32[]{:S(2)}, u32[]{:S(2)}) collective-permute-start(bf16[400,512]{1,0:T(8,128)(2,1)S(1)} %get-tuple-element.146), channel_id=1, source_target_pairs={{0,1},{1,3},{3,2},{2,0},{4,5},{5,7},{7,6},{6,4},{8,9},{9,11},{11,1... | collective-permute-start | bytes 1228808 | tf_op jit(solution)/shard_map/ppermute | solution.py:56
  78.5 20.5 %collective-permute-start.25 = (bf16[400,512]{1,0:T(8,128)(2,1)S(1)}, bf16[400,512]{1,0:T(8,128)(2,1)S(1)}, u32[]{:S(2)}, u32[]{:S(2)}) collective-permute-start(bf16[400,512]{1,0:T(8,128)(2,1)S(1)} %collective-permute-done.23.hn2_ref.refs_2_), channel_id=1, source_target_pairs={{0,1},{1,3},{3,2},{2,0},{4,5},{5,7},{7,6},{6,4},{8,9},{9,11},{11,1... | collective-permute-start | bytes 1228808 | tf_op jit(solution)/shard_map/ppermute | solution.py:56
  89.4 17.2 %collective-permute-start.24 = (bf16[400,512]{1,0:T(8,128)(2,1)S(1)}, bf16[400,512]{1,0:T(8,128)(2,1)S(1)}, u32[]{:S(2)}, u32[]{:S(2)}) collective-permute-start(bf16[400,512]{1,0:T(8,128)(2,1)S(1)} %sums.9), channel_id=1, source_target_pairs={{0,1},{1,3},{3,2},{2,0},{4,5},{5,7},{7,6},{6,4},{8,9},{9,11},{11,1... | collective-permute-start | bytes 1228808 | tf_op jit(solution)/shard_map/ppermute | solution.py:56
  106.7 13.4 %collective-permute-start.26 = (bf16[400,512]{1,0:T(8,128)(2,1)S(1)}, bf16[400,512]{1,0:T(8,128)(2,1)S(1)}, u32[]{:S(2)}, u32[]{:S(2)}) collective-permute-start(bf16[400,512]{1,0:T(8,128)(2,1)S(1)} %sums.10), channel_id=1, source_target_pairs={{0,1},{1,3},{3,2},{2,0},{4,5},{5,7},{7,6},{6,4},{8,9},{9,11},{11,1... | collective-permute-start | bytes 1228808 | tf_op jit(solution)/shard_map/ppermute | solution.py:56
  120.2 4.2 %collective-permute-start.27 = (bf16[4,2,4,64,512]{4,3,2,1,0:T(8,128)(2,1)S(1)}, bf16[4,2,4,64,512]{4,3,2,1,0:T(8,128)(2,1)S(1)}, u32[]{:S(2)}, u32[]{:S(2)}) collective-permute-start(bf16[4,2,4,64,512]{4,3,2,1,0:T(8,128)(2,1)S(1)} %get-tuple-element.164), channel_id=1, source_target_pairs={{0,4},{4,0},{8,12},{12,8},{16,20},{20,16},{24,28},{28,24},{1,5},{5... | collective-permute-start | bytes 6291464 | tf_op jit(solution)/shard_map/ppermute | solution.py:46
  124.9 14.1 %collective-permute-start.29 = (bf16[2,1,4,64,512]{4,3,2,1,0:T(8,128)(2,1)S(1)}, bf16[2,1,4,64,512]{4,3,2,1,0:T(8,128)(2,1)S(1)}, u32[]{:S(2)}, u32[]{:S(2)}) collective-permute-start(bf16[2,1,4,64,512]{4,3,2,1,0:T(8,128)(2,1)S(1)} %get-tuple-element.181), channel_id=1, source_target_pairs={{0,16},{4,20},{8,24},{12,28},{16,0},{20,4},{24,8},{28,12},{1,17},{... | collective-permute-start | bytes 1572872 | tf_op jit(solution)/shard_map/ppermute | solution.py:46
  125.7 13.7 %collective-permute-start.28 = (bf16[2,1,4,64,512]{4,3,2,1,0:T(8,128)(2,1)S(1)}, bf16[2,1,4,64,512]{4,3,2,1,0:T(8,128)(2,1)S(1)}, u32[]{:S(2)}, u32[]{:S(2)}) collective-permute-start(bf16[2,1,4,64,512]{4,3,2,1,0:T(8,128)(2,1)S(1)} %get-tuple-element.165), channel_id=1, source_target_pairs={{0,8},{4,12},{8,0},{12,4},{16,24},{20,28},{24,16},{28,20},{1,9},{5... | collective-permute-start | bytes 1572872 | tf_op jit(solution)/shard_map/ppermute | solution.py:46
  127.2 11.8 %collective-permute-start.30 = (bf16[400,512]{1,0:T(8,128)(2,1)S(1)}, bf16[400,512]{1,0:T(8,128)(2,1)S(1)}, u32[]{:S(2)}, u32[]{:S(2)}) collective-permute-start(bf16[400,512]{1,0:T(8,128)(2,1)S(1)} %get-tuple-element.183), channel_id=1, source_target_pairs={{0,1},{1,3},{3,2},{2,0},{4,5},{5,7},{7,6},{6,4},{8,9},{9,11},{11,1... | collective-permute-start | bytes 1228808 | tf_op jit(solution)/shard_map/ppermute | solution.py:56
  139.6 2.8 %collective-permute-start.31 = (bf16[4,4,272,128]{3,2,1,0:T(8,128)(2,1)S(1)}, bf16[4,4,272,128]{3,2,1,0:T(8,128)(2,1)S(1)}, u32[]{:S(2)}, u32[]{:S(2)}) collective-permute-start(bf16[4,4,272,128]{3,2,1,0:T(8,128)(2,1)S(1)} %get-tuple-element.190), channel_id=1, source_target_pairs={{0,4},{4,0},{8,12},{12,8},{16,20},{20,16},{24,28},{28,24},{1,5},{5... | collective-permute-start | bytes 3342344 | tf_op jit(solution)/shard_map/ppermute | solution.py:46
  139.8 12.8 %collective-permute-start.34 = (bf16[400,512]{1,0:T(8,128)(2,1)S(1)}, bf16[400,512]{1,0:T(8,128)(2,1)S(1)}, u32[]{:S(2)}, u32[]{:S(2)}) collective-permute-start(bf16[400,512]{1,0:T(8,128)(2,1)S(1)} %sums.14), channel_id=1, source_target_pairs={{0,1},{1,3},{3,2},{2,0},{4,5},{5,7},{7,6},{6,4},{8,9},{9,11},{11,1... | collective-permute-start | bytes 1228808 | tf_op jit(solution)/shard_map/ppermute | solution.py:56
  142.7 10.0 %collective-permute-start.33 = (bf16[2,2,272,128]{3,2,1,0:T(8,128)(2,1)S(1)}, bf16[2,2,272,128]{3,2,1,0:T(8,128)(2,1)S(1)}, u32[]{:S(2)}, u32[]{:S(2)}) collective-permute-start(bf16[2,2,272,128]{3,2,1,0:T(8,128)(2,1)S(1)} %get-tuple-element.192), channel_id=1, source_target_pairs={{0,16},{4,20},{8,24},{12,28},{16,0},{20,4},{24,8},{28,12},{1,17},{... | collective-permute-start | bytes 835592 | tf_op jit(solution)/shard_map/ppermute | solution.py:46
  144.1 9.5 %collective-permute-start.32 = (bf16[2,2,272,128]{3,2,1,0:T(8,128)(2,1)S(1)}, bf16[2,2,272,128]{3,2,1,0:T(8,128)(2,1)S(1)}, u32[]{:S(2)}, u32[]{:S(2)}) collective-permute-start(bf16[2,2,272,128]{3,2,1,0:T(8,128)(2,1)S(1)} %get-tuple-element.191), channel_id=1, source_target_pairs={{0,8},{4,12},{8,0},{12,4},{16,24},{20,28},{24,16},{28,20},{1,9},{5... | collective-permute-start | bytes 835592 | tf_op jit(solution)/shard_map/ppermute | solution.py:46
  145.6 17.0 %collective-permute-start.42 = (bf16[1,4,64,512]{3,2,1,0:T(8,128)(2,1)S(1)}, bf16[1,4,64,512]{3,2,1,0:T(8,128)(2,1)S(1)}, u32[]{:S(2)}, u32[]{:S(2)}) collective-permute-start(bf16[1,4,64,512]{3,2,1,0:T(8,128)(2,1)S(1)} %get-tuple-element.219), channel_id=1, source_target_pairs={{0,8},{4,12},{8,0},{12,4},{16,24},{20,28},{24,16},{28,20},{1,9},{5... | collective-permute-start | bytes 786440 | tf_op jit(solution)/shard_map/ppermute | solution.py:46
  146.2 19.5 %collective-permute-start.41 = (bf16[1,4,64,512]{3,2,1,0:T(8,128)(2,1)S(1)}, bf16[1,4,64,512]{3,2,1,0:T(8,128)(2,1)S(1)}, u32[]{:S(2)}, u32[]{:S(2)}) collective-permute-start(bf16[1,4,64,512]{3,2,1,0:T(8,128)(2,1)S(1)} %get-tuple-element.189), channel_id=1, source_target_pairs={{0,16},{4,20},{8,24},{12,28},{16,0},{20,4},{24,8},{28,12},{1,17},{... | collective-permute-start | bytes 786440 | tf_op jit(solution)/shard_map/ppermute | solution.py:46
  153.8 6.3 %collective-permute-start.36 = (bf16[2,272,128]{2,1,0:T(8,128)(2,1)S(1)}, bf16[2,272,128]{2,1,0:T(8,128)(2,1)S(1)}, u32[]{:S(2)}, u32[]{:S(2)}) collective-permute-start(bf16[2,272,128]{2,1,0:T(8,128)(2,1)S(1)} %get-tuple-element.204), channel_id=1, source_target_pairs={{0,16},{4,20},{8,24},{12,28},{16,0},{20,4},{24,8},{28,12},{1,17},{... | collective-permute-start | bytes 417800 | tf_op jit(solution)/shard_map/ppermute | solution.py:46
  154.6 6.6 %collective-permute-start.37 = (bf16[2,272,128]{2,1,0:T(8,128)(2,1)S(1)}, bf16[2,272,128]{2,1,0:T(8,128)(2,1)S(1)}, u32[]{:S(2)}, u32[]{:S(2)}) collective-permute-start(bf16[2,272,128]{2,1,0:T(8,128)(2,1)S(1)} %get-tuple-element.206), channel_id=1, source_target_pairs={{0,8},{4,12},{8,0},{12,4},{16,24},{20,28},{24,16},{28,20},{1,9},{5... | collective-permute-start | bytes 417800 | tf_op jit(solution)/shard_map/ppermute | solution.py:46
  156.0 17.0 %collective-permute-start.35 = (bf16[400,512]{1,0:T(8,128)(2,1)S(1)}, bf16[400,512]{1,0:T(8,128)(2,1)S(1)}, u32[]{:S(2)}, u32[]{:S(2)}) collective-permute-start(bf16[400,512]{1,0:T(8,128)(2,1)S(1)} %sums.15), channel_id=1, source_target_pairs={{0,1},{1,3},{3,2},{2,0},{4,5},{5,7},{7,6},{6,4},{8,9},{9,11},{11,1... | collective-permute-start | bytes 1228808 | tf_op jit(solution)/shard_map/ppermute | solution.py:56
  157.0 16.1 %copy-start = (f32[400,512]{1,0:T(8,128)S(1)}, f32[400,512]{1,0:T(8,128)}, u32[]{:S(2)}) copy-start(f32[400,512]{1,0:T(8,128)} %get-tuple-element.135.refs_4_) | copy-start | bytes 2457604
  161.2 7.7 %collective-permute-start.38 = (bf16[272,128]{1,0:T(8,128)(2,1)S(1)}, bf16[272,128]{1,0:T(8,128)(2,1)S(1)}, u32[]{:S(2)}, u32[]{:S(2)}) collective-permute-start(bf16[272,128]{1,0:T(8,128)(2,1)S(1)} %get-tuple-element.208), channel_id=1, source_target_pairs={{0,1},{1,0},{2,3},{3,2},{4,5},{5,4},{6,7},{7,6},{8,9},{9,8},{10,11... | collective-permute-start | bytes 208904 | tf_op jit(solution)/shard_map/ppermute | solution.py:46
  162.2 10.2 %collective-permute-start.39 = (bf16[272,128]{1,0:T(8,128)(2,1)S(1)}, bf16[272,128]{1,0:T(8,128)(2,1)S(1)}, u32[]{:S(2)}, u32[]{:S(2)}) collective-permute-start(bf16[272,128]{1,0:T(8,128)(2,1)S(1)} %get-tuple-element.209), channel_id=1, source_target_pairs={{0,2},{1,3},{2,0},{3,1},{4,6},{5,7},{6,4},{7,5},{8,10},{9,11},{10,... | collective-permute-start | bytes 208904 | tf_op jit(solution)/shard_map/ppermute | solution.py:46
  162.6 9.8 %collective-permute-start.40 = (bf16[272,128]{1,0:T(8,128)(2,1)S(1)}, bf16[272,128]{1,0:T(8,128)(2,1)S(1)}, u32[]{:S(2)}, u32[]{:S(2)}) collective-permute-start(bf16[272,128]{1,0:T(8,128)(2,1)S(1)} %get-tuple-element.210), channel_id=1, source_target_pairs={{0,3},{1,2},{2,1},{3,0},{4,7},{5,6},{6,5},{7,4},{8,11},{9,10},{10,... | collective-permute-start | bytes 208904 | tf_op jit(solution)/shard_map/ppermute | solution.py:46
where the time goes:
time: 175 us
  Pallas kernels  64.2 us (37%)
  waiting for transfers between devices  49.2 us (28%)
  starting transfers between devices  47.2 us (27%)
  other arithmetic  7.76 us (4%)
  local copies, waits for them, and re-layouts  5.31 us (3%)
    ppermute x31, starting transfers between devices, xor_send(): return lax.ppermute(x, axis, [(i, i ^ mask) for i in range(n)])  31.2 us
    pallas_call x4, Pallas kernels, expert_shard(): pl.pallas_call(partial(expert_kernel, nimg, shard), out_shape=[low, low,...  30.8 us
    ppermute x31, waiting for transfers between devices, xor_send(): return lax.ppermute(x, axis, [(i, i ^ mask) for i in range(n)])  29.1 us
    ppermute x12, waiting for transfers between devices, ring_step(): return lax.ppermute(x, 'tensor', pairs)  20.1 us
    ppermute x12, starting transfers between devices, ring_step(): return lax.ppermute(x, 'tensor', pairs)  16.1 us
    pallas_call x1, Pallas kernels, expert_grads(): pl.pallas_call(partial(expert_grad_kernel, nt, gmasks), grid=(EXPERTS,),...  11.1 us
    pallas_call x1, Pallas kernels, attn_backward(): pl.pallas_call(partial(attn_backward_kernel, nimg, len(sms), len(gubs), g...  10.2 us
    pallas_call x1, Pallas kernels, attn_forward(): pl.pallas_call(partial(attn_forward_kernel, nimg), out_shape=shapes, in_s...  4.32 us
  transfers between devices with their start and end apart: 43, of which 22 were waited for; matrix products, arithmetic and copies ran while one was open for 4% of the time, Pallas kernels for 36%

commit v1 on v0

--- a/solution.py
+++ b/solution.py
@@ -421,7 +421,7 @@
 
 
 def gather_experts_kernel(masks, ids, *refs):
-    pieces, (w_ref, sems) = refs[:-2], refs[-2:]
+    pieces, (up_ref, dn_ref, sems) = refs[:-3], refs[-3:]
     me = ids[0]
     pairs = []
     for group, ref in zip(masks, pieces):
@@ -429,7 +429,9 @@
         for idx, mask in enumerate(group):
             at = pl.ds(pl.multiple_of(jnp.bitwise_xor(me, mask) * dr, dr), dr)
             for e in range(EXPERTS):
-                pairs.append((ref.at[idx, e], w_ref.at[at, e * ff : (e + 1) * ff]))
+                cols = slice(e * ff, (e + 1) * ff)
+                pairs.append((ref.at[idx, e], up_ref.at[at, cols]))
+                pairs.append((ref.at[idx, EXPERTS + e], dn_ref.at[at, cols]))
     run_copies(pairs, sems)
 
 
@@ -437,12 +439,13 @@
     masks = [m for m, _ in weights]
     pieces = arrays(weights)
     nd = sum(len(m) for m in masks)
+    whole = jax.ShapeDtypeStruct((width, EXPERTS * pieces[0].shape[3]), BF)
     return pl.pallas_call(
         partial(gather_experts_kernel, masks),
-        out_shape=jax.ShapeDtypeStruct((width, EXPERTS * pieces[0].shape[3]), BF),
+        out_shape=[whole, whole],
         in_specs=[SM] + [ANY] * len(pieces),
-        out_specs=VM,
-        scratch_shapes=[pltpu.SemaphoreType.DMA((EXPERTS * nd,))],
+        out_specs=[VM, VM],
+        scratch_shapes=[pltpu.SemaphoreType.DMA((2 * EXPERTS * nd,))],
         compiler_params=params(8),
         cost_estimate=cost(3),
         name="gather_experts",
@@ -532,40 +535,39 @@
     grads = refs[4 * nt + 1 : 4 * nt + 1 + len(gmasks)]
     res_ref = refs[4 * nt + 1 + len(gmasks)]
     me = ids[0]
+    ff = gub_ref.shape[2]
     ones = jnp.ones((8, hn2s[0].shape[0]), BF)
-    sums = None
-    for s in range(nt):
-        part = mm(ones, dhps[s][...])
-        sums = part if sums is None else sums + part
-    for which in range(2):
-        lefts, rights = ((hn2s, dhps), (cots, hgs))[which]
-        left = jnp.concatenate([r[...] for r in lefts], axis=0)
-        right = jnp.concatenate([r[...] for r in rights], axis=0)
-        total = mm(left, right, TN)
-        res_ref[...] = total
-        for group, ref in zip(gmasks, grads):
-            dr = ref.shape[3]
-            for idx, mask in enumerate(group):
-                at = pl.ds(pl.multiple_of(jnp.bitwise_xor(me, mask) * dr, dr), dr)
-                ref[idx, which, 0] = res_ref[at, :].astype(BF)
-    gub_ref[...] = sums[0:1, :]
+
+    def expert(e, carry):
+        cols = pl.ds(pl.multiple_of(e * ff, ff), ff)
+        sums_ = [mm(ones, r[:, cols]) for r in dhps]
+        gub_ref[e] = sum(sums_[1:], sums_[0])[0:1, :]
+        for which in range(2):
+            lefts, rights = ((hn2s, dhps), (cots, hgs))[which]
+            left = jnp.concatenate([r[...] for r in lefts], axis=0)
+            right = jnp.concatenate([r[:, cols] for r in rights], axis=0)
+            res_ref[which] = mm(left, right, TN)
+            for group, ref in zip(gmasks, grads):
+                dr = ref.shape[3]
+                for idx, mask in enumerate(group):
+                    at = pl.ds(pl.multiple_of(jnp.bitwise_xor(me, mask) * dr, dr), dr)
+                    ref[idx, which, e] = res_ref[which, at, :].astype(BF)
+        return carry
+
+    lax.fori_loop(0, EXPERTS, expert, 0)
 
 
 def expert_grads(ids, hn2s, cots, hgs, dhps, gmasks, dr):
     nt = len(hn2s)
-    count, width = hn2s[0].shape
+    width = hn2s[0].shape[1]
     ff = hgs[0].shape[1] // EXPERTS
-    fixed = pl.BlockSpec((count, width), lambda e: (0, 0))
-    moving = pl.BlockSpec((count, ff), lambda e: (0, e))
     return pl.pallas_call(
         partial(expert_grad_kernel, nt, gmasks),
-        grid=(EXPERTS,),
         out_shape=[jax.ShapeDtypeStruct((EXPERTS, 1, ff), F4)]
         + [jax.ShapeDtypeStruct((len(m), 2, EXPERTS, dr, ff), BF) for m in gmasks],
-        in_specs=[SM] + [fixed] * (2 * nt) + [moving] * (2 * nt),
-        out_specs=[pl.BlockSpec((None, 1, ff), lambda e: (e, 0, 0))]
-        + [pl.BlockSpec((len(m), 2, 1, dr, ff), lambda e: (0, 0, e, 0, 0)) for m in gmasks],
-        scratch_shapes=[pltpu.VMEM((width, ff), F4)],
+        in_specs=[SM] + [VM] * (4 * nt),
+        out_specs=[VM] * (1 + len(gmasks)),
+        scratch_shapes=[pltpu.VMEM((2, width, ff), F4)],
         compiler_params=params(16),
         cost_estimate=cost(9),
         name="expert_grads",
@@ -609,31 +611,32 @@
     for c in copies[1:]:
         c.wait()
 
-    def pair(n, carry):
-        cols = pl.ds(pl.multiple_of(n * LANES, LANES), LANES)
-        for img in range(nimg):
-            at = slice(img * PAD, (img + 1) * PAD)
-            qp, kp, vp, dop = q_ref[at, cols], k_ref[at, cols], v_ref[at, cols], do_ref[at, cols]
-            zero = jnp.zeros_like(qp)
-            dq = jnp.zeros((PAD, LANES), F4)
-            dk = jnp.zeros((PAD, LANES), F4)
-            dv = jnp.zeros((PAD, LANES), F4)
-            for half in range(2):
-                mine = (lane < HD) if half == 0 else (lane >= HD)
-                pb = pb_ref[img * (width // HD) + 2 * n + half]
-                dom = jnp.where(mine, dop, zero)
-                dpb = mm(dom, vp, NT)
-                p = pb.astype(F4)
-                ds = (p * (dpb - jnp.sum(p * dpb, axis=-1, keepdims=True))).astype(BF)
-                dv = dv + mm(pb, dom, TN)
-                dq = dq + mm(ds, jnp.where(mine, kp, zero))
-                dk = dk + mm(ds, jnp.where(mine, qp, zero), TN)
-            dq_ref[at, cols] = (dq * scale).astype(BF)
-            dk_ref[at, cols] = (dk * scale).astype(BF)
-            dv_ref[at, cols] = dv.astype(BF)
+    def pairs(at_pair, carry):
+        for n in (2 * at_pair, 2 * at_pair + 1):
+            cols = pl.ds(pl.multiple_of(n * LANES, LANES), LANES)
+            for img in range(nimg):
+                at = slice(img * PAD, (img + 1) * PAD)
+                qp, kp, vp, dop = q_ref[at, cols], k_ref[at, cols], v_ref[at, cols], do_ref[at, cols]
+                zero = jnp.zeros_like(qp)
+                dq = jnp.zeros((PAD, LANES), F4)
+                dk = jnp.zeros((PAD, LANES), F4)
+                dv = jnp.zeros((PAD, LANES), F4)
+                for half in range(2):
+                    mine = (lane < HD) if half == 0 else (lane >= HD)
+                    pb = pb_ref[img * (width // HD) + 2 * n + half]
+                    dom = jnp.where(mine, dop, zero)
+                    dpb = mm(dom, vp, NT)
+                    p = pb.astype(F4)
+                    ds = (p * (dpb - jnp.sum(p * dpb, axis=-1, keepdims=True))).astype(BF)
+                    dv = dv + mm(pb, dom, TN)
+                    dq = dq + mm(ds, jnp.where(mine, kp, zero))
+                    dk = dk + mm(ds, jnp.where(mine, qp, zero), TN)
+                dq_ref[at, cols] = (dq * scale).astype(BF)
+                dk_ref[at, cols] = (dk * scale).astype(BF)
+                dv_ref[at, cols] = dv.astype(BF)
         return carry
 
-    lax.fori_loop(0, width // LANES, pair, 0)
+    lax.fori_loop(0, width // LANES // 2, pairs, 0)
     small_ref[QVB : QVB + 1, :] = jnp.sum(dq_ref[...].astype(F4), axis=0, keepdims=True)
     small_ref[QVB + 1 : QVB + 2, :] = jnp.sum(dv_ref[...].astype(F4), axis=0, keepdims=True)
     dh1 = (
@@ -813,19 +816,12 @@
     cot = images(cotangent)
     chunk_z = [chunk] + [xor_send(chunk, "tensor", nt, m) for m in range(1, nt)]
     if direct:
-        up_near = plane_first(after(w_up, chunk))
-        chunk_z, up_near = lax.optimization_barrier((chunk_z, up_near))
         chunk_z = jnp.stack(chunk_z)
         cots = ring_all(after(cot, chunk_z))
         near = plane_first(chunk_z)
-        quad = plane_stack(*near, lax.optimization_barrier((plane_far(*near), cots[2]))[0])
-        up_far = lax.optimization_barrier((plane_far(*up_near), cots[1]))[0]
-        up_quad = plane_stack(*up_near, up_far)
-        dn_near = plane_first(after(w_dn, quad))
-        quad = after(quad, x, keep, ids, up_quad)
-        (_, quad), (_, other) = gather_cores(quad)
-        full, rows = assemble(ids, [(CORE0, quad), (CORE1, other)], width)
-        up_cores = gather_cores(after(up_quad, quad))
+        quad = plane_stack(*near, lax.optimization_barrier((plane_far(*near), cots[1]))[0])
+        layers = plane_first(after(jnp.concatenate([w_up, w_dn]), quad))
+        full, rows = assemble(ids, gather_cores(after(quad, x, keep, ids)), width)
     else:
         cots = ring_all(cot)
         up, dn = (
@@ -853,12 +849,12 @@
         return expert_shard(ids, keep, hn2, cots[s], rows, up, dn, nimg, s)
 
     for s in range(1, nt):
-        hn2s.append(ring_step(after(hn2s[-1], *(cots[-1:] if s == 1 else [])), nt, False))
+        hn2s.append(ring_step(after(hn2s[-1], *(cots[2:] if s == nt - 1 else [])), nt, False))
     if direct:
-        up = gather_experts(ids, [(m, after(a, hn2s[0])) for m, a in up_cores], width)
-        dn_near = lax.optimization_barrier((dn_near, hn2s[0], cots[3]))[0]
-        dn_quad = after(plane_stack(*dn_near, plane_far(*dn_near)), hn2s[1])
-        dn = gather_experts(ids, gather_cores(dn_quad), width)
+        layers = lax.optimization_barrier((layers, hn2s[0], cots[2]))[0]
+        far = lax.optimization_barrier((plane_far(*layers), hn2s[1]))[0]
+        layers = plane_stack(*layers, far)
+        up, dn = gather_experts(ids, gather_cores(layers), width)
     shards = [None, shard(1)] + [None] * (nt - 2)
     total = past = shards[1][1]
     for s in range(2, nt):

time: 175 us -> 170 us (0.971)
  starting transfers between devices: 47.2 us -> 37 us
  waiting for transfers between devices: 49.2 us -> 58.5 us
  Pallas kernels: 64.2 us -> 62 us
    ppermute x12, starting transfers between devices: 16.1 us -> 8.63 us  [ring_step(): return lax.ppermute(x, 'tensor', pairs)]
    ppermute x31 -> x26, waiting for transfers between devices: 29.1 us -> 34.5 us  [xor_send(): return lax.ppermute(x, axis, [(i, i ^ mask) for i in range(n)])]
    ppermute x12, waiting for transfers between devices: 20.1 us -> 23.9 us  [ring_step(): return lax.ppermute(x, 'tensor', pairs)]
    ppermute x31 -> x26, starting transfers between devices: 31.2 us -> 28.3 us  [xor_send(): return lax.ppermute(x, axis, [(i, i ^ mask) for i in range(n)])]
    pallas_call x3 -> x2, Pallas kernels: 13.5 us -> 11.9 us  [the longest x1 10 us: expert_grads(): pl.pallas_call(partial(expert_grad_kernel, nt, gmasks), out_shape=[jax.Sh...]
  transfers between devices with their start and end apart: 43 -> 38, of which waited for: 22 -> 27; matrix products, arithmetic and copies ran while one was open for 4% -> 3% of each run, Pallas kernels for 36% -> 36%
where the time goes in v1:
time: 170 us; the launch traced here: 169 us
  Pallas kernels  62 us (36%)
  waiting for transfers between devices  58.5 us (34%)
  starting transfers between devices  37 us (22%)
  other arithmetic  6.22 us (4%)
  local copies, waits for them, and re-layouts  4.6 us (3%)
    ppermute x26, waiting for transfers between devices, xor_send(): return lax.ppermute(x, axis, [(i, i ^ mask) for i in range(n)])  34.5 us
    pallas_call x4, Pallas kernels, expert_shard(): pl.pallas_call(partial(expert_kernel, nimg, shard), out_shape=[low, low,...  30.8 us
    ppermute x26, starting transfers between devices, xor_send(): return lax.ppermute(x, axis, [(i, i ^ mask) for i in range(n)])  28.3 us
    ppermute x12, waiting for transfers between devices, ring_step(): return lax.ppermute(x, 'tensor', pairs)  23.9 us
    pallas_call x1, Pallas kernels, expert_grads(): pl.pallas_call(partial(expert_grad_kernel, nt, gmasks), out_shape=[jax.Sh...  10 us
    pallas_call x1, Pallas kernels, attn_backward(): pl.pallas_call(partial(attn_backward_kernel, nimg, len(sms), len(gubs), g...  9.65 us
    ppermute x12, starting transfers between devices, ring_step(): return lax.ppermute(x, 'tensor', pairs)  8.63 us
    pallas_call x1, Pallas kernels, attn_forward(): pl.pallas_call(partial(attn_forward_kernel, nimg), out_shape=shapes, in_s...  4.32 us
  transfers between devices with their start and end apart: 38, of which 27 were waited for; matrix products, arithmetic and copies ran while one was open for 3% of the time, Pallas kernels for 36%

profile of v1, /device:TPU:0, one launch (start us, length us, event | category | flops | bytes accessed | tf_op | source)
XLA Modules:
  0.0 169.3 jit_solution(6165429071219750221)
XLA Ops:
  0.7 0.8 pad_maximum_fusion.6
  1.5 2.2 %concatenate.42 = bf16[16,64]{1,0:T(8,128)(2,1)S(1)} concatenate(bf16[2,64]{1,0:T(2,128)(2,1)} %param.20, bf16[2,64]{1,0:T(2,128)(2,1)} %param.21, bf16[1,64]{1,0:T(2,128)(2,1)} %bitcast.51, bf16[4,64]{1,0:T(4,128)(2,1)} %bitcast.50, bf16[4,64]{1,0:T(4,128)(2,1)} %param.30, bf16[3,64]{1,0:T(4,128)(2,1)S(1)} %broadcast_in_dim.18), dimensions={0} | concatenate | bytes 4096 | tf_op jit(solution)/shard_map/concatenate | solution.py:797
  3.7 0.8 fusion.11
  4.5 4.1 %collective-permute-start.1 = (bf16[272,128]{1,0:T(8,128)(2,1)S(1)}, bf16[272,128]{1,0:T(8,128)(2,1)S(1)}, u32[]{:S(2)}, u32[]{:S(2)}) collective-permute-start(bf16[272,128]{1,0:T(8,128)(2,1)S(1)} %fusion.11), channel_id=1, source_target_pairs={{0,2},{1,3},{2,0},{3,1},{4,6},{5,7},{6,4},{7,5},{8,10},{9,11},{10,... | collective-permute-start | bytes 208904 | tf_op jit(solution)/shard_map/ppermute | solution.py:46
  8.6 1.6 collective-permute-start
  10.2 1.0 slice.43
  11.2 1.2 slice_select_fusion
  12.9 3.4 %collective-permute-done.2 = bf16[272,128]{1,0:T(8,128)(2,1)S(1)} collective-permute-done((bf16[272,128]{1,0:T(8,128)(2,1)S(1)}, bf16[272,128]{1,0:T(8,128)(2,1)S(1)}, u32[]{:S(2)}, u32[]{:S(2)}) %collective-permute-start.2) | collective-permute-done | bytes 69664 | tf_op jit(solution)/shard_map/ppermute | solution.py:46
  16.3 1.6 collective-permute-start.4
  17.9 1.5 collective-permute-start.3
  19.5 0.7 dynamic-slice_bitcast_fusion
  20.1 3.0 %collective-permute-done.4 = bf16[4,272,128]{2,1,0:T(8,128)(2,1)S(1)} collective-permute-done((bf16[4,272,128]{2,1,0:T(8,128)(2,1)S(1)}, bf16[4,272,128]{2,1,0:T(8,128)(2,1)S(1)}, u32[]{:S(2)}, u32[]{:S(2)}) %collective-permute-start.4) | collective-permute-done | bytes 278560 | tf_op jit(solution)/shard_map/ppermute | solution.py:46
  23.2 1.6 collective-permute-start.6
  24.8 0.9 collective-permute-done.3
  25.7 0.6 collective-permute-start.5
  27.0 2.8 %collective-permute-done.7.cot_ref.refs_5_ = bf16[400,512]{1,0:T(8,128)(2,1)S(1)} collective-permute-done((bf16[400,512]{1,0:T(8,128)(2,1)S(1)}, bf16[400,512]{1,0:T(8,128)(2,1)S(1)}, u32[]{:S(2)}, u32[]{:S(2)}) %collective-permute-start.7) | collective-permute-done | bytes 409632 | tf_op jit(solution)/shard_map/ppermute | solution.py:56
  29.8 1.0 collective-permute-done.5
  31.2 0.6 collective-permute-start.11
  31.8 1.0 collective-permute-start.10
  33.8 2.9 %assemble.1 = (bf16[4,512,512]{2,1,0:T(8,128)(2,1)S(1)}, f32[32,512]{1,0:T(8,128)S(1)}) custom-call(s32[6]{0:T(128)S(1)} %pad_add_fusion.ids, bf16[4,4,272,128]{3,2,1,0:T(8,128)(2,1)S(1)} %pad_maximum_fusion.1.refs_0_, bf16[4,4,272,128]{3,2,1,0:T(8,128)(2,1)S(1)} %collective-permute-done.8.refs_1_), custom_call_target="tpu_custom_call" | custom-call | bytes 66000 | tf_op jit(solution)/shard_map/assemble/pallas_call | solution.py:336
  36.8 4.3 %attn_forward.1 = (bf16[400,512]{1,0:T(8,128)(2,1)S(1)}, f32[400,512]{1,0:T(8,128)}, bf16[400,512]{1,0:T(8,128)(2,1)}, bf16[400,512]{1,0:T(8,128)(2,1)}, bf16[40...) custom-call(bf16[400,512]{1,0:T(8,128)(2,1)S(1)} %fusion.2.x_ref.refs_2_, ...), custom_call_target="tpu_custom_call" | custom-call | bytes 297000 | tf_op jit(solution)/shard_map/attn_forward/pallas_call | solution.py:411
  41.1 1.3 collective-permute-start.9
  42.4 3.3 %collective-permute-done.12.cot_ref.refs_6_ = bf16[400,512]{1,0:T(8,128)(2,1)S(1)} collective-permute-done((bf16[400,512]{1,0:T(8,128)(2,1)S(1)}, bf16[400,512]{1,0:T(8,128)(2,1)S(1)}, u32[]{:S(2)}, u32[]{:S(2)}) %collective-permute-start.12) | collective-permute-done | bytes 409632 | tf_op jit(solution)/shard_map/ppermute | solution.py:56
  45.9 1.3 collective-permute-start.14
  47.2 1.7 collective-permute-start.13
  48.9 4.6 %collective-permute-done.14 = bf16[4,64,512]{2,1,0:T(8,128)(2,1)S(1)} collective-permute-done((bf16[4,64,512]{2,1,0:T(8,128)(2,1)S(1)}, bf16[4,64,512]{2,1,0:T(8,128)(2,1)S(1)}, u32[]{:S(2)}, u32[]{:S(2)}) %collective-permute-start.14) | collective-permute-done | bytes 262176 | tf_op jit(solution)/shard_map/ppermute | solution.py:46
  53.5 1.3 collective-permute-done.13
  55.3 1.9 %collective-permute-start.17 = (bf16[400,512]{1,0:T(8,128)(2,1)S(1)}, bf16[400,512]{1,0:T(8,128)(2,1)S(1)}, u32[]{:S(2)}, u32[]{:S(2)}) collective-permute-start(bf16[400,512]{1,0:T(8,128)(2,1)S(1)} %collective-permute-done.9.hn2_ref.refs_1_), channel_id=1, source_target_pairs={{0,1},{1,3},{3,2},{2,0},{4,5},{5,7},{7,6},{6,4},{8,9},{9,11},{11,1... | collective-permute-start | bytes 1228808 | tf_op jit(solution)/shard_map/ppermute | solution.py:56
  57.2 2.1 %collective-permute-done.15.refs_1_ = bf16[4,8,64,512]{3,2,1,0:T(8,128)(2,1)S(1)} collective-permute-done((bf16[4,8,64,512]{3,2,1,0:T(8,128)(2,1)S(1)}, bf16[4,8,64,512]{3,2,1,0:T(8,128)(2,1)S(1)}, u32[]{:S(2)}, u32[]{:S(2)}) %collective-permute-start.15) | collective-permute-done | bytes 2097184 | tf_op jit(solution)/shard_map/ppermute | solution.py:46
  59.3 1.9 %gather_experts.1 = (bf16[512,2048]{1,0:T(8,128)(2,1)S(1)}, bf16[512,2048]{1,0:T(8,128)(2,1)S(1)}) custom-call(s32[6]{0:T(128)S(1)} %pad_add_fusion.ids, bf16[4,8,64,512]{3,2,1,0:T(8,128)(2,1)S(1)} %pad_maximum_fusion.refs_0_, bf16[4,8,64,512]{3,2,1,0:T(8,128)(2,1)S(1)} %collective-permute-done.15.refs_1_), custom_call_target="tpu_custom_call" | custom-call | bytes 99000 | tf_op jit(solution)/shard_map/gather_experts/pallas_call | solution.py:443
  61.3 7.7 %expert_shard.4 = (bf16[400,512]{1,0:T(8,128)(2,1)S(1)}, bf16[400,512]{1,0:T(8,128)(2,1)S(1)}, bf16[400,2048]{1,0:T(8,128)(2,1)S(1)}, bf16[400,2048]{1,0:T(8,128)(2,1)S(1)}, f32[16,512]{1,0:T(8,128)S(1)}) custom-call(s32[6]{0:T(128)S(1)} %pad_add_fusion.ids, s32[8,200,2]{2,1,0:T(8,128)S(1)} %pad.26.keep_ref, ...), custom_call_target="tpu_custom_call" | custom-call | bytes 231000 | tf_op jit(solution)/shard_map/expert_shard/pallas_call | solution.py:521
  69.0 8.3 %collective-permute-done.17.hn2_ref.refs_2_ = bf16[400,512]{1,0:T(8,128)(2,1)S(1)} collective-permute-done((bf16[400,512]{1,0:T(8,128)(2,1)S(1)}, bf16[400,512]{1,0:T(8,128)(2,1)S(1)}, u32[]{:S(2)}, u32[]{:S(2)}) %collective-permute-start.17) | collective-permute-done | bytes 409632 | tf_op jit(solution)/shard_map/ppermute | solution.py:56
  77.3 7.6 %expert_shard.5 = (bf16[400,512]{1,0:T(8,128)(2,1)S(1)}, bf16[400,512]{1,0:T(8,128)(2,1)S(1)}, bf16[400,2048]{1,0:T(8,128)(2,1)S(1)}, bf16[400,2048]{1,0:T(8,128)(2,1)S(1)}, f32[16,512]{1,0:T(8,128)S(1)}) custom-call(s32[6]{0:T(128)S(1)} %pad_add_fusion.ids, s32[8,200,2]{2,1,0:T(8,128)S(1)} %pad.26.keep_ref, ...), custom_call_target="tpu_custom_call" | custom-call | bytes 231000 | tf_op jit(solution)/shard_map/expert_shard/pallas_call | solution.py:521
  84.9 1.1 collective-permute-done.16.refs_0_
  86.1 1.1 collective-permute-start.18
  87.2 7.8 %expert_shard.6 = (bf16[400,512]{1,0:T(8,128)(2,1)S(1)}, bf16[400,512]{1,0:T(8,128)(2,1)S(1)}, bf16[400,2048]{1,0:T(8,128)(2,1)S(1)}, bf16[400,2048]{1,0:T(8,128)(2,1)S(1)}, f32[16,512]{1,0:T(8,128)S(1)}) custom-call(s32[6]{0:T(128)S(1)} %pad_add_fusion.ids, s32[8,200,2]{2,1,0:T(8,128)S(1)} %pad.26.keep_ref, ...), custom_call_target="tpu_custom_call" | custom-call | bytes 231000 | tf_op jit(solution)/shard_map/expert_shard/pallas_call | solution.py:521
  95.0 7.7 %expert_shard.7 = (bf16[400,512]{1,0:T(8,128)(2,1)S(1)}, bf16[400,512]{1,0:T(8,128)(2,1)S(1)}, bf16[400,2048]{1,0:T(8,128)(2,1)S(1)}, bf16[400,2048]{1,0:T(8,128)(2,1)S(1)}, f32[16,512]{1,0:T(8,128)S(1)}) custom-call(s32[6]{0:T(128)S(1)} %pad_add_fusion.ids, s32[8,200,2]{2,1,0:T(8,128)S(1)} %pad.26.keep_ref, ...), custom_call_target="tpu_custom_call" | custom-call | bytes 231000 | tf_op jit(solution)/shard_map/expert_shard/pallas_call | solution.py:521
  103.2 0.9 collective-permute-start.21
  104.1 10.0 %expert_grads.1 = (f32[4,1,512]{2,1,0:T(1,128)S(1)}, bf16[4,2,4,64,512]{4,3,2,1,0:T(8,128)(2,1)S(1)}, bf16[4,2,4,64,512]{4,3,2,1,0:T(8,128)(2,1)S(1)}) custom-call(s32[6]{0:T(128)S(1)} %pad_add_fusion.ids, bf16[400,512]{1,0:T(8,128)(2,1)S(1)} %get-tuple-element.129.hn2_ref.refs_0_, bf16[400,512]{1,0:T(8,128)(2,1)S(1)} %collective-permute-done.9.hn2_ref.refs_1_, ...), custom_call_target="tpu_custom_call" | custom-call | bytes 297000 | tf_op jit(solution)/shard_map/expert_grads/pallas_call | solution.py:564
  114.1 1.0 collective-permute-done.21.refs_0_
  115.1 4.2 %collective-permute-done.22.refs_1_ = bf16[4,2,4,64,512]{4,3,2,1,0:T(8,128)(2,1)S(1)} collective-permute-done((bf16[4,2,4,64,512]{4,3,2,1,0:T(8,128)(2,1)S(1)}, bf16[4,2,4,64,512]{4,3,2,1,0:T(8,128)(2,1)S(1)}, u32[]{:S(2)}, u32[]{:S(2)}) %collective-permute-start.22) | collective-permute-done | bytes 2097184 | tf_op jit(solution)/shard_map/ppermute | solution.py:46
  119.8 1.5 collective-permute-start.24
  121.8 0.8 collective-permute-start.25
  122.6 9.7 %attn_backward.1 = (f32[400,512]{1,0:T(8,128)S(1)}, bf16[4,4,272,128]{3,2,1,0:T(8,128)(2,1)S(1)}, bf16[4,4,272,128]{3,2,1,0:T(8,128)(2,1)S(1)}, f32[32,512]{1,0:T(8,128)}) custom-call(s32[6]{0:T(128)S(1)} %pad_add_fusion.ids, bf16[400,512]{1,0:T(8,128)(2,1)S(1)} %collective-permute-done.21.refs_0_, bf16[400,512]{1,0:T(8,128)(2,1)S(1)} %get-tuple-element.130.refs_1_, ...), custom_call_target="tpu_custom_call" | custom-call | bytes 528000 | tf_op jit(solution)/shard_map/attn_backward/pallas_call | solution.py:716
  132.3 1.3 collective-permute-done.25.refs_0_
  133.8 1.1 collective-permute-done.23.refs_1_
  135.4 0.9 collective-permute-start.29
  136.3 1.7 %collective-permute-done.26.refs_1_ = bf16[4,4,272,128]{3,2,1,0:T(8,128)(2,1)S(1)} collective-permute-done((bf16[4,4,272,128]{3,2,1,0:T(8,128)(2,1)S(1)}, bf16[4,4,272,128]{3,2,1,0:T(8,128)(2,1)S(1)}, u32[]{:S(2)}, u32[]{:S(2)}) %collective-permute-start.26) | collective-permute-done | bytes 1114144 | tf_op jit(solution)/shard_map/ppermute | solution.py:46
  138.3 0.7 collective-permute-start.28
  139.0 1.2 collective-permute-start.27
  140.2 0.8 collective-permute-start.37
  141.0 1.4 collective-permute-start.36
  142.4 5.8 %collective-permute-done.29.refs_0_ = bf16[400,512]{1,0:T(8,128)(2,1)S(1)} collective-permute-done((bf16[400,512]{1,0:T(8,128)(2,1)S(1)}, bf16[400,512]{1,0:T(8,128)(2,1)S(1)}, u32[]{:S(2)}, u32[]{:S(2)}) %collective-permute-start.29) | collective-permute-done | bytes 409632 | tf_op jit(solution)/shard_map/ppermute | solution.py:56
  148.7 1.5 collective-permute-start.31
  150.6 0.8 collective-permute-start.30
  151.6 4.1 %collective-permute-done.31.refs_1_ = bf16[2,272,128]{2,1,0:T(8,128)(2,1)S(1)} collective-permute-done((bf16[2,272,128]{2,1,0:T(8,128)(2,1)S(1)}, bf16[2,272,128]{2,1,0:T(8,128)(2,1)S(1)}, u32[]{:S(2)}, u32[]{:S(2)}) %collective-permute-start.31) | collective-permute-done | bytes 139296 | tf_op jit(solution)/shard_map/ppermute | solution.py:46
  156.1 0.9 collective-permute-start.33
  157.0 1.1 collective-permute-start.34
  158.1 2.4 %collective-permute-start.35 = (bf16[272,128]{1,0:T(8,128)(2,1)S(1)}, bf16[272,128]{1,0:T(8,128)(2,1)S(1)}, u32[]{:S(2)}, u32[]{:S(2)}) collective-permute-start(bf16[272,128]{1,0:T(8,128)(2,1)S(1)} %get-tuple-element.190), channel_id=1, source_target_pairs={{0,3},{1,2},{2,1},{3,0},{4,7},{5,6},{6,5},{7,4},{8,11},{9,10},{10,... | collective-permute-start | bytes 208904 | tf_op jit(solution)/shard_map/ppermute | solution.py:46
  160.5 1.1 add_bitcast_fusion
  161.7 2.2 %collective-permute-done.33.refs_1_ = bf16[272,128]{1,0:T(8,128)(2,1)S(1)} collective-permute-done((bf16[272,128]{1,0:T(8,128)(2,1)S(1)}, bf16[272,128]{1,0:T(8,128)(2,1)S(1)}, u32[]{:S(2)}, u32[]{:S(2)}) %collective-permute-start.33) | collective-permute-done | bytes 69664 | tf_op jit(solution)/shard_map/ppermute | solution.py:46
  163.9 3.1 %collective-permute-done.34.refs_2_ = bf16[272,128]{1,0:T(8,128)(2,1)S(1)} collective-permute-done((bf16[272,128]{1,0:T(8,128)(2,1)S(1)}, bf16[272,128]{1,0:T(8,128)(2,1)S(1)}, u32[]{:S(2)}, u32[]{:S(2)}) %collective-permute-start.34) | collective-permute-done | bytes 69664 | tf_op jit(solution)/shard_map/ppermute | solution.py:46
  167.0 0.7 finish.1
  167.9 1.3 pad_maximum_fusion.2
  (79 shorter events, 7.5 us)
Async XLA Ops:
  0.6 11.8 %copy-start.6 = (bf16[4,64]{1,0:T(4,128)(2,1)S(1)}, bf16[4,64]{1,0:T(4,128)(2,1)}, u32[]{:S(2)}) copy-start(bf16[4,64]{1,0:T(4,128)(2,1)} %param.28) | copy-start | bytes 1540
  0.7 11.8 %copy-start.7 = (bf16[2,16]{1,0:T(2,128)(2,1)S(1)}, bf16[2,16]{1,0:T(2,128)(2,1)}, u32[]{:S(2)}) copy-start(bf16[2,16]{1,0:T(2,128)(2,1)} %param.23) | copy-start | bytes 196
  0.7 18.8 %copy-start.4 = (s32[1576,2]{0,1:T(2,128)S(1)}, s32[1576,2]{0,1:T(2,128)}, u32[]{:S(2)}) copy-start(s32[1576,2]{0,1:T(2,128)} %param.18) | copy-start | bytes 37828
  0.7 18.7 %copy-start.5 = (s32[1576,2]{0,1:T(2,128)S(1)}, s32[1576,2]{0,1:T(2,128)}, u32[]{:S(2)}) copy-start(s32[1576,2]{0,1:T(2,128)} %param.19) | copy-start | bytes 37828
  4.5 8.0 %collective-permute-start.1 = (bf16[272,128]{1,0:T(8,128)(2,1)S(1)}, bf16[272,128]{1,0:T(8,128)(2,1)S(1)}, u32[]{:S(2)}, u32[]{:S(2)}) collective-permute-start(bf16[272,128]{1,0:T(8,128)(2,1)S(1)} %fusion.11), channel_id=1, source_target_pairs={{0,2},{1,3},{2,0},{3,1},{4,6},{5,7},{6,4},{7,5},{8,10},{9,11},{10,... | collective-permute-start | bytes 208904 | tf_op jit(solution)/shard_map/ppermute | solution.py:46
  8.6 4.3 %collective-permute-start = (bf16[272,128]{1,0:T(8,128)(2,1)S(1)}, bf16[272,128]{1,0:T(8,128)(2,1)S(1)}, u32[]{:S(2)}, u32[]{:S(2)}) collective-permute-start(bf16[272,128]{1,0:T(8,128)(2,1)S(1)} %fusion.11), channel_id=1, source_target_pairs={{0,1},{1,0},{2,3},{3,2},{4,5},{5,4},{6,7},{7,6},{8,9},{9,8},{10,11... | collective-permute-start | bytes 208904 | tf_op jit(solution)/shard_map/ppermute | solution.py:46
  10.2 6.1 %collective-permute-start.2 = (bf16[272,128]{1,0:T(8,128)(2,1)S(1)}, bf16[272,128]{1,0:T(8,128)(2,1)S(1)}, u32[]{:S(2)}, u32[]{:S(2)}) collective-permute-start(bf16[272,128]{1,0:T(8,128)(2,1)S(1)} %fusion.11), channel_id=1, source_target_pairs={{0,3},{1,2},{2,1},{3,0},{4,7},{5,6},{6,5},{7,4},{8,11},{9,10},{10,... | collective-permute-start | bytes 208904 | tf_op jit(solution)/shard_map/ppermute | solution.py:46
  11.2 15.3 %copy-start.1 = (bf16[394,512]{1,0:T(8,128)(2,1)S(1)}, bf16[394,512]{1,0:T(8,128)(2,1)}, u32[]{:S(2)}) copy-start(bf16[394,512]{1,0:T(8,128)(2,1)} %param.16) | copy-start | bytes 1210372
  16.3 6.9 %collective-permute-start.4 = (bf16[4,272,128]{2,1,0:T(8,128)(2,1)S(1)}, bf16[4,272,128]{2,1,0:T(8,128)(2,1)S(1)}, u32[]{:S(2)}, u32[]{:S(2)}) collective-permute-start(bf16[4,272,128]{2,1,0:T(8,128)(2,1)S(1)} %get-tuple-element.210), channel_id=1, source_target_pairs={{0,16},{4,20},{8,24},{12,28},{16,0},{20,4},{24,8},{28,12},{1,17},{... | collective-permute-start | bytes 835592 | tf_op jit(solution)/shard_map/ppermute | solution.py:46
  17.9 7.8 %collective-permute-start.3 = (bf16[4,272,128]{2,1,0:T(8,128)(2,1)S(1)}, bf16[4,272,128]{2,1,0:T(8,128)(2,1)S(1)}, u32[]{:S(2)}, u32[]{:S(2)}) collective-permute-start(bf16[4,272,128]{2,1,0:T(8,128)(2,1)S(1)} %get-tuple-element.210), channel_id=1, source_target_pairs={{0,8},{4,12},{8,0},{12,4},{16,24},{20,28},{24,16},{28,20},{1,9},{5... | collective-permute-start | bytes 835592 | tf_op jit(solution)/shard_map/ppermute | solution.py:46
  19.4 10.4 %collective-permute-start.7 = (bf16[400,512]{1,0:T(8,128)(2,1)S(1)}, bf16[400,512]{1,0:T(8,128)(2,1)S(1)}, u32[]{:S(2)}, u32[]{:S(2)}) collective-permute-start(bf16[400,512]{1,0:T(8,128)(2,1)S(1)} %fusion.3.cot_ref.refs_4_.refs_3_), channel_id=1, source_target_pairs={{0,1},{1,3},{3,2},{2,0},{4,5},{5,7},{7,6},{6,4},{8,9},{9,11},{11,1... | collective-permute-start | bytes 1228808 | tf_op jit(solution)/shard_map/ppermute | solution.py:56
  23.2 6.6 %collective-permute-start.6 = (bf16[2,272,128]{2,1,0:T(8,128)(2,1)S(1)}, bf16[2,272,128]{2,1,0:T(8,128)(2,1)S(1)}, u32[]{:S(2)}, u32[]{:S(2)}) collective-permute-start(bf16[2,272,128]{2,1,0:T(8,128)(2,1)S(1)} %slice.51), channel_id=1, source_target_pairs={{0,8},{4,12},{8,0},{12,4},{16,24},{20,28},{24,16},{28,20},{1,9},{5... | collective-permute-start | bytes 417800 | tf_op jit(solution)/shard_map/ppermute | solution.py:46
  25.7 5.1 %collective-permute-start.5 = (bf16[2,272,128]{2,1,0:T(8,128)(2,1)S(1)}, bf16[2,272,128]{2,1,0:T(8,128)(2,1)S(1)}, u32[]{:S(2)}, u32[]{:S(2)}) collective-permute-start(bf16[2,272,128]{2,1,0:T(8,128)(2,1)S(1)} %slice.50), channel_id=1, source_target_pairs={{0,16},{4,20},{8,24},{12,28},{16,0},{20,4},{24,8},{28,12},{1,17},{... | collective-permute-start | bytes 417800 | tf_op jit(solution)/shard_map/ppermute | solution.py:46
  27.0 4.1 %copy-start.2 = (bf16[4,512,64]{1,2,0:T(8,128)(2,1)S(1)}, bf16[4,512,64]{1,2,0:T(8,128)(2,1)}, u32[]{:S(2)}) copy-start(bf16[4,512,64]{1,2,0:T(8,128)(2,1)} %param.29) | copy-start | bytes 786436
  27.0 4.1 %copy-start.3 = (bf16[4,64,512]{2,1,0:T(8,128)(2,1)S(1)}, bf16[4,64,512]{2,1,0:T(8,128)(2,1)}, u32[]{:S(2)}) copy-start(bf16[4,64,512]{2,1,0:T(8,128)(2,1)} %param.27) | copy-start | bytes 786436
  31.0 2.8 %collective-permute-start.8 = (bf16[4,4,272,128]{3,2,1,0:T(8,128)(2,1)S(1)}, bf16[4,4,272,128]{3,2,1,0:T(8,128)(2,1)S(1)}, u32[]{:S(2)}, u32[]{:S(2)}) collective-permute-start(bf16[4,4,272,128]{3,2,1,0:T(8,128)(2,1)S(1)} %pad_maximum_fusion.1.refs_0_), channel_id=1, source_target_pairs={{0,4},{4,0},{8,12},{12,8},{16,20},{20,16},{24,28},{28,24},{1,5},{5... | collective-permute-start | bytes 3342344 | tf_op jit(solution)/shard_map/ppermute | solution.py:46
  31.2 14.6 %collective-permute-start.11 = (bf16[8,64,512]{2,1,0:T(8,128)(2,1)S(1)}, bf16[8,64,512]{2,1,0:T(8,128)(2,1)S(1)}, u32[]{:S(2)}, u32[]{:S(2)}) collective-permute-start(bf16[8,64,512]{2,1,0:T(8,128)(2,1)S(1)} %pad_maximum_fusion.4), channel_id=1, source_target_pairs={{0,16},{4,20},{8,24},{12,28},{16,0},{20,4},{24,8},{28,12},{1,17},{... | collective-permute-start | bytes 1572872 | tf_op jit(solution)/shard_map/ppermute | solution.py:46
  31.8 14.0 %collective-permute-start.10 = (bf16[8,64,512]{2,1,0:T(8,128)(2,1)S(1)}, bf16[8,64,512]{2,1,0:T(8,128)(2,1)S(1)}, u32[]{:S(2)}, u32[]{:S(2)}) collective-permute-start(bf16[8,64,512]{2,1,0:T(8,128)(2,1)S(1)} %pad_maximum_fusion.4), channel_id=1, source_target_pairs={{0,8},{4,12},{8,0},{12,4},{16,24},{20,28},{24,16},{28,20},{1,9},{5... | collective-permute-start | bytes 1572872 | tf_op jit(solution)/shard_map/ppermute | solution.py:46
  32.8 12.9 %collective-permute-start.12 = (bf16[400,512]{1,0:T(8,128)(2,1)S(1)}, bf16[400,512]{1,0:T(8,128)(2,1)S(1)}, u32[]{:S(2)}, u32[]{:S(2)}) collective-permute-start(bf16[400,512]{1,0:T(8,128)(2,1)S(1)} %collective-permute-done.7.cot_ref.refs_5_), channel_id=1, source_target_pairs={{0,1},{1,3},{3,2},{2,0},{4,5},{5,7},{7,6},{6,4},{8,9},{9,11},{11,1... | collective-permute-start | bytes 1228808 | tf_op jit(solution)/shard_map/ppermute | solution.py:56
  41.1 13.7 %collective-permute-start.9 = (bf16[400,512]{1,0:T(8,128)(2,1)S(1)}, bf16[400,512]{1,0:T(8,128)(2,1)S(1)}, u32[]{:S(2)}, u32[]{:S(2)}) collective-permute-start(bf16[400,512]{1,0:T(8,128)(2,1)S(1)} %get-tuple-element.129.hn2_ref.refs_0_), channel_id=1, source_target_pairs={{0,1},{1,3},{3,2},{2,0},{4,5},{5,7},{7,6},{6,4},{8,9},{9,11},{11,1... | collective-permute-start | bytes 1228808 | tf_op jit(solution)/shard_map/ppermute | solution.py:56
  45.9 7.6 %collective-permute-start.14 = (bf16[4,64,512]{2,1,0:T(8,128)(2,1)S(1)}, bf16[4,64,512]{2,1,0:T(8,128)(2,1)S(1)}, u32[]{:S(2)}, u32[]{:S(2)}) collective-permute-start(bf16[4,64,512]{2,1,0:T(8,128)(2,1)S(1)} %slice.45), channel_id=1, source_target_pairs={{0,8},{4,12},{8,0},{12,4},{16,24},{20,28},{24,16},{28,20},{1,9},{5... | collective-permute-start | bytes 786440 | tf_op jit(solution)/shard_map/ppermute | solution.py:46
  47.2 7.6 %collective-permute-start.13 = (bf16[4,64,512]{2,1,0:T(8,128)(2,1)S(1)}, bf16[4,64,512]{2,1,0:T(8,128)(2,1)S(1)}, u32[]{:S(2)}, u32[]{:S(2)}) collective-permute-start(bf16[4,64,512]{2,1,0:T(8,128)(2,1)S(1)} %slice.44), channel_id=1, source_target_pairs={{0,16},{4,20},{8,24},{12,28},{16,0},{20,4},{24,8},{28,12},{1,17},{... | collective-permute-start | bytes 786440 | tf_op jit(solution)/shard_map/ppermute | solution.py:46
  55.1 4.2 %collective-permute-start.15 = (bf16[4,8,64,512]{3,2,1,0:T(8,128)(2,1)S(1)}, bf16[4,8,64,512]{3,2,1,0:T(8,128)(2,1)S(1)}, u32[]{:S(2)}, u32[]{:S(2)}) collective-permute-start(bf16[4,8,64,512]{3,2,1,0:T(8,128)(2,1)S(1)} %pad_maximum_fusion.refs_0_), channel_id=1, source_target_pairs={{0,4},{4,0},{8,12},{12,8},{16,20},{20,16},{24,28},{28,24},{1,5},{5... | collective-permute-start | bytes 6291464 | tf_op jit(solution)/shard_map/ppermute | solution.py:46
  55.2 13.8 %collective-permute-start.19 = (bf16[400,512]{1,0:T(8,128)(2,1)S(1)}, bf16[400,512]{1,0:T(8,128)(2,1)S(1)}, u32[]{:S(2)}, u32[]{:S(2)}) collective-permute-start(bf16[400,512]{1,0:T(8,128)(2,1)S(1)} %collective-permute-done.12.cot_ref.refs_6_), channel_id=1, source_target_pairs={{0,1},{1,3},{3,2},{2,0},{4,5},{5,7},{7,6},{6,4},{8,9},{9,11},{11,1... | collective-permute-start | bytes 1228808 | tf_op jit(solution)/shard_map/ppermute | solution.py:56
  55.3 22.0 %collective-permute-start.17 = (bf16[400,512]{1,0:T(8,128)(2,1)S(1)}, bf16[400,512]{1,0:T(8,128)(2,1)S(1)}, u32[]{:S(2)}, u32[]{:S(2)}) collective-permute-start(bf16[400,512]{1,0:T(8,128)(2,1)S(1)} %collective-permute-done.9.hn2_ref.refs_1_), channel_id=1, source_target_pairs={{0,1},{1,3},{3,2},{2,0},{4,5},{5,7},{7,6},{6,4},{8,9},{9,11},{11,1... | collective-permute-start | bytes 1228808 | tf_op jit(solution)/shard_map/ppermute | solution.py:56
  68.9 17.1 %collective-permute-start.16 = (bf16[400,512]{1,0:T(8,128)(2,1)S(1)}, bf16[400,512]{1,0:T(8,128)(2,1)S(1)}, u32[]{:S(2)}, u32[]{:S(2)}) collective-permute-start(bf16[400,512]{1,0:T(8,128)(2,1)S(1)} %get-tuple-element.125), channel_id=1, source_target_pairs={{0,1},{1,3},{3,2},{2,0},{4,5},{5,7},{7,6},{6,4},{8,9},{9,11},{11,1... | collective-permute-start | bytes 1228808 | tf_op jit(solution)/shard_map/ppermute | solution.py:56
  77.3 17.8 %collective-permute-start.20 = (bf16[400,512]{1,0:T(8,128)(2,1)S(1)}, bf16[400,512]{1,0:T(8,128)(2,1)S(1)}, u32[]{:S(2)}, u32[]{:S(2)}) collective-permute-start(bf16[400,512]{1,0:T(8,128)(2,1)S(1)} %collective-permute-done.17.hn2_ref.refs_2_), channel_id=1, source_target_pairs={{0,1},{1,3},{3,2},{2,0},{4,5},{5,7},{7,6},{6,4},{8,9},{9,11},{11,1... | collective-permute-start | bytes 1228808 | tf_op jit(solution)/shard_map/ppermute | solution.py:56
  86.1 16.9 %collective-permute-start.18 = (bf16[400,512]{1,0:T(8,128)(2,1)S(1)}, bf16[400,512]{1,0:T(8,128)(2,1)S(1)}, u32[]{:S(2)}, u32[]{:S(2)}) collective-permute-start(bf16[400,512]{1,0:T(8,128)(2,1)S(1)} %sums.9), channel_id=1, source_target_pairs={{0,1},{1,3},{3,2},{2,0},{4,5},{5,7},{7,6},{6,4},{8,9},{9,11},{11,1... | collective-permute-start | bytes 1228808 | tf_op jit(solution)/shard_map/ppermute | solution.py:56
  103.2 11.9 %collective-permute-start.21 = (bf16[400,512]{1,0:T(8,128)(2,1)S(1)}, bf16[400,512]{1,0:T(8,128)(2,1)S(1)}, u32[]{:S(2)}, u32[]{:S(2)}) collective-permute-start(bf16[400,512]{1,0:T(8,128)(2,1)S(1)} %sums.10), channel_id=1, source_target_pairs={{0,1},{1,3},{3,2},{2,0},{4,5},{5,7},{7,6},{6,4},{8,9},{9,11},{11,1... | collective-permute-start | bytes 1228808 | tf_op jit(solution)/shard_map/ppermute | solution.py:56
  115.1 4.2 %collective-permute-start.22 = (bf16[4,2,4,64,512]{4,3,2,1,0:T(8,128)(2,1)S(1)}, bf16[4,2,4,64,512]{4,3,2,1,0:T(8,128)(2,1)S(1)}, u32[]{:S(2)}, u32[]{:S(2)}) collective-permute-start(bf16[4,2,4,64,512]{4,3,2,1,0:T(8,128)(2,1)S(1)} %get-tuple-element.144), channel_id=1, source_target_pairs={{0,4},{4,0},{8,12},{12,8},{16,20},{20,16},{24,28},{28,24},{1,5},{5... | collective-permute-start | bytes 6291464 | tf_op jit(solution)/shard_map/ppermute | solution.py:46
  119.8 14.0 %collective-permute-start.24 = (bf16[2,1,4,64,512]{4,3,2,1,0:T(8,128)(2,1)S(1)}, bf16[2,1,4,64,512]{4,3,2,1,0:T(8,128)(2,1)S(1)}, u32[]{:S(2)}, u32[]{:S(2)}) collective-permute-start(bf16[2,1,4,64,512]{4,3,2,1,0:T(8,128)(2,1)S(1)} %get-tuple-element.161), channel_id=1, source_target_pairs={{0,16},{4,20},{8,24},{12,28},{16,0},{20,4},{24,8},{28,12},{1,17},{... | collective-permute-start | bytes 1572872 | tf_op jit(solution)/shard_map/ppermute | solution.py:46
  121.2 13.7 %collective-permute-start.23 = (bf16[2,1,4,64,512]{4,3,2,1,0:T(8,128)(2,1)S(1)}, bf16[2,1,4,64,512]{4,3,2,1,0:T(8,128)(2,1)S(1)}, u32[]{:S(2)}, u32[]{:S(2)}) collective-permute-start(bf16[2,1,4,64,512]{4,3,2,1,0:T(8,128)(2,1)S(1)} %get-tuple-element.145), channel_id=1, source_target_pairs={{0,8},{4,12},{8,0},{12,4},{16,24},{20,28},{24,16},{28,20},{1,9},{5... | collective-permute-start | bytes 1572872 | tf_op jit(solution)/shard_map/ppermute | solution.py:46
  121.8 11.8 %collective-permute-start.25 = (bf16[400,512]{1,0:T(8,128)(2,1)S(1)}, bf16[400,512]{1,0:T(8,128)(2,1)S(1)}, u32[]{:S(2)}, u32[]{:S(2)}) collective-permute-start(bf16[400,512]{1,0:T(8,128)(2,1)S(1)} %get-tuple-element.163), channel_id=1, source_target_pairs={{0,1},{1,3},{3,2},{2,0},{4,5},{5,7},{7,6},{6,4},{8,9},{9,11},{11,1... | collective-permute-start | bytes 1228808 | tf_op jit(solution)/shard_map/ppermute | solution.py:56
  135.2 2.8 %collective-permute-start.26 = (bf16[4,4,272,128]{3,2,1,0:T(8,128)(2,1)S(1)}, bf16[4,4,272,128]{3,2,1,0:T(8,128)(2,1)S(1)}, u32[]{:S(2)}, u32[]{:S(2)}) collective-permute-start(bf16[4,4,272,128]{3,2,1,0:T(8,128)(2,1)S(1)} %get-tuple-element.170), channel_id=1, source_target_pairs={{0,4},{4,0},{8,12},{12,8},{16,20},{20,16},{24,28},{28,24},{1,5},{5... | collective-permute-start | bytes 3342344 | tf_op jit(solution)/shard_map/ppermute | solution.py:46
  135.4 12.8 %collective-permute-start.29 = (bf16[400,512]{1,0:T(8,128)(2,1)S(1)}, bf16[400,512]{1,0:T(8,128)(2,1)S(1)}, u32[]{:S(2)}, u32[]{:S(2)}) collective-permute-start(bf16[400,512]{1,0:T(8,128)(2,1)S(1)} %sums.14), channel_id=1, source_target_pairs={{0,1},{1,3},{3,2},{2,0},{4,5},{5,7},{7,6},{6,4},{8,9},{9,11},{11,1... | collective-permute-start | bytes 1228808 | tf_op jit(solution)/shard_map/ppermute | solution.py:56
  138.3 10.0 %collective-permute-start.28 = (bf16[2,2,272,128]{3,2,1,0:T(8,128)(2,1)S(1)}, bf16[2,2,272,128]{3,2,1,0:T(8,128)(2,1)S(1)}, u32[]{:S(2)}, u32[]{:S(2)}) collective-permute-start(bf16[2,2,272,128]{3,2,1,0:T(8,128)(2,1)S(1)} %get-tuple-element.172), channel_id=1, source_target_pairs={{0,16},{4,20},{8,24},{12,28},{16,0},{20,4},{24,8},{28,12},{1,17},{... | collective-permute-start | bytes 835592 | tf_op jit(solution)/shard_map/ppermute | solution.py:46
  139.0 9.5 %collective-permute-start.27 = (bf16[2,2,272,128]{3,2,1,0:T(8,128)(2,1)S(1)}, bf16[2,2,272,128]{3,2,1,0:T(8,128)(2,1)S(1)}, u32[]{:S(2)}, u32[]{:S(2)}) collective-permute-start(bf16[2,2,272,128]{3,2,1,0:T(8,128)(2,1)S(1)} %get-tuple-element.171), channel_id=1, source_target_pairs={{0,8},{4,12},{8,0},{12,4},{16,24},{20,28},{24,16},{28,20},{1,9},{5... | collective-permute-start | bytes 835592 | tf_op jit(solution)/shard_map/ppermute | solution.py:46
  140.2 17.9 %collective-permute-start.37 = (bf16[1,4,64,512]{3,2,1,0:T(8,128)(2,1)S(1)}, bf16[1,4,64,512]{3,2,1,0:T(8,128)(2,1)S(1)}, u32[]{:S(2)}, u32[]{:S(2)}) collective-permute-start(bf16[1,4,64,512]{3,2,1,0:T(8,128)(2,1)S(1)} %get-tuple-element.199), channel_id=1, source_target_pairs={{0,8},{4,12},{8,0},{12,4},{16,24},{20,28},{24,16},{28,20},{1,9},{5... | collective-permute-start | bytes 786440 | tf_op jit(solution)/shard_map/ppermute | solution.py:46
  141.0 19.5 %collective-permute-start.36 = (bf16[1,4,64,512]{3,2,1,0:T(8,128)(2,1)S(1)}, bf16[1,4,64,512]{3,2,1,0:T(8,128)(2,1)S(1)}, u32[]{:S(2)}, u32[]{:S(2)}) collective-permute-start(bf16[1,4,64,512]{3,2,1,0:T(8,128)(2,1)S(1)} %get-tuple-element.169), channel_id=1, source_target_pairs={{0,16},{4,20},{8,24},{12,28},{16,0},{20,4},{24,8},{28,12},{1,17},{... | collective-permute-start | bytes 786440 | tf_op jit(solution)/shard_map/ppermute | solution.py:46
  148.7 7.0 %collective-permute-start.31 = (bf16[2,272,128]{2,1,0:T(8,128)(2,1)S(1)}, bf16[2,272,128]{2,1,0:T(8,128)(2,1)S(1)}, u32[]{:S(2)}, u32[]{:S(2)}) collective-permute-start(bf16[2,272,128]{2,1,0:T(8,128)(2,1)S(1)} %get-tuple-element.184), channel_id=1, source_target_pairs={{0,16},{4,20},{8,24},{12,28},{16,0},{20,4},{24,8},{28,12},{1,17},{... | collective-permute-start | bytes 417800 | tf_op jit(solution)/shard_map/ppermute | solution.py:46
  150.1 5.9 %collective-permute-start.32 = (bf16[2,272,128]{2,1,0:T(8,128)(2,1)S(1)}, bf16[2,272,128]{2,1,0:T(8,128)(2,1)S(1)}, u32[]{:S(2)}, u32[]{:S(2)}) collective-permute-start(bf16[2,272,128]{2,1,0:T(8,128)(2,1)S(1)} %get-tuple-element.186), channel_id=1, source_target_pairs={{0,8},{4,12},{8,0},{12,4},{16,24},{20,28},{24,16},{28,20},{1,9},{5... | collective-permute-start | bytes 417800 | tf_op jit(solution)/shard_map/ppermute | solution.py:46
  150.6 17.0 %collective-permute-start.30 = (bf16[400,512]{1,0:T(8,128)(2,1)S(1)}, bf16[400,512]{1,0:T(8,128)(2,1)S(1)}, u32[]{:S(2)}, u32[]{:S(2)}) collective-permute-start(bf16[400,512]{1,0:T(8,128)(2,1)S(1)} %sums.15), channel_id=1, source_target_pairs={{0,1},{1,3},{3,2},{2,0},{4,5},{5,7},{7,6},{6,4},{8,9},{9,11},{11,1... | collective-permute-start | bytes 1228808 | tf_op jit(solution)/shard_map/ppermute | solution.py:56
  151.6 16.1 %copy-start = (f32[400,512]{1,0:T(8,128)S(1)}, f32[400,512]{1,0:T(8,128)}, u32[]{:S(2)}) copy-start(f32[400,512]{1,0:T(8,128)} %get-tuple-element.115.refs_4_) | copy-start | bytes 2457604
  156.1 7.8 %collective-permute-start.33 = (bf16[272,128]{1,0:T(8,128)(2,1)S(1)}, bf16[272,128]{1,0:T(8,128)(2,1)S(1)}, u32[]{:S(2)}, u32[]{:S(2)}) collective-permute-start(bf16[272,128]{1,0:T(8,128)(2,1)S(1)} %get-tuple-element.188), channel_id=1, source_target_pairs={{0,1},{1,0},{2,3},{3,2},{4,5},{5,4},{6,7},{7,6},{8,9},{9,8},{10,11... | collective-permute-start | bytes 208904 | tf_op jit(solution)/shard_map/ppermute | solution.py:46
  157.0 10.0 %collective-permute-start.34 = (bf16[272,128]{1,0:T(8,128)(2,1)S(1)}, bf16[272,128]{1,0:T(8,128)(2,1)S(1)}, u32[]{:S(2)}, u32[]{:S(2)}) collective-permute-start(bf16[272,128]{1,0:T(8,128)(2,1)S(1)} %get-tuple-element.189), channel_id=1, source_target_pairs={{0,2},{1,3},{2,0},{3,1},{4,6},{5,7},{6,4},{7,5},{8,10},{9,11},{10,... | collective-permute-start | bytes 208904 | tf_op jit(solution)/shard_map/ppermute | solution.py:46
  158.1 8.8 %collective-permute-start.35 = (bf16[272,128]{1,0:T(8,128)(2,1)S(1)}, bf16[272,128]{1,0:T(8,128)(2,1)S(1)}, u32[]{:S(2)}, u32[]{:S(2)}) collective-permute-start(bf16[272,128]{1,0:T(8,128)(2,1)S(1)} %get-tuple-element.190), channel_id=1, source_target_pairs={{0,3},{1,2},{2,1},{3,0},{4,7},{5,6},{6,5},{7,4},{8,11},{9,10},{10,... | collective-permute-start | bytes 208904 | tf_op jit(solution)/shard_map/ppermute | solution.py:46

commit v2 on v1

--- a/solution.py
+++ b/solution.py
@@ -209,7 +209,7 @@
 
 
 def finish_kernel(dr, qr, *refs):
-    parts, outs = refs[:4], refs[4:]
+    parts, outs = refs[:2], refs[2:]
     g_qkv, g_out, g_gain, g_bias, g_outb, g_router, g_dbias, g_ub, g_qvb = outs
     total = parts[0][...].astype(F4)
     for ref in parts[1:]:
@@ -234,7 +234,7 @@
     return pl.pallas_call(
         partial(finish_kernel, dr, qr),
         out_shape=[jax.ShapeDtypeStruct(v, F4) for v in shapes],
-        in_specs=[VM] * 4,
+        in_specs=[VM] * 2,
         out_specs=[VM] * len(shapes),
         compiler_params=params(),
         cost_estimate=cost(1),
@@ -851,8 +851,8 @@
     for s in range(1, nt):
         hn2s.append(ring_step(after(hn2s[-1], *(cots[2:] if s == nt - 1 else [])), nt, False))
     if direct:
-        layers = lax.optimization_barrier((layers, hn2s[0], cots[2]))[0]
-        far = lax.optimization_barrier((plane_far(*layers), hn2s[1]))[0]
+        layers = lax.optimization_barrier((layers, hn2s[0]))[0]
+        far = lax.optimization_barrier((plane_far(*layers), hn2s[1], cots[2]))[0]
         layers = plane_stack(*layers, far)
         up, dn = gather_experts(ids, gather_cores(layers), width)
     shards = [None, shard(1)] + [None] * (nt - 2)
@@ -881,9 +881,7 @@
     )
     ms = [r[0] for r in shards]
     if direct:
-        kept_x, kept_y, send_x, send_y = scatter_first(egrads[0], to(after(egrads[1], recv), 1))
-        got_x, got_y = to(send_x, 2), to(send_y, 4)
-        recv = after(recv, send_x)
+        other = to(after(egrads[1], recv), 1)
     m_sum = ring_step(after(ms[1], recv), nt, False)
 
     res = attn_backward(
@@ -903,29 +901,34 @@
         dr if direct else width,
     )
     gtok, flat = res[0], res[-1]
+    def rows_of(v):
+        return jnp.concatenate([v[i * PAD : i * PAD + SEQ] for i in range(nimg)])
+
+    grad_tokens = rows_of(gtok)
     if direct:
-        keeps, gots, m_sum = lax.optimization_barrier(
-            ((kept_x, kept_y), (got_x, got_y), m_sum, gtok)
-        )[:3]
-        next_x, next_y, base_x, base_y = scatter_second(*keeps, *gots)
-        far_x, far_y = to(next_x, 4), to(next_y, 2)
+        other, m_sum, odd = lax.optimization_barrier((other, m_sum, res[2]))
+        a_other = to(odd, 1)
         m_sum = ring_step(sums([[[(m_sum, None), (ms[2], None)]]])[0], nt, False)
-        a_odd = after(res[2], next_x)
-        keeps = scatter_first(res[1], to(a_odd, 1))
-        a_keep, a_send = keeps[:2], keeps[2:]
-        a_got = to(a_send[0], 2), to(a_send[1], 4)
-        m_sum = sums([[[(after(m_sum, a_send[0]), None), (ms[3], None)]]])[0]
-        a_got, m_sum = lax.optimization_barrier((a_got, m_sum))
-        m_sum = ring_step(m_sum, nt, False)
-        a_next_x, a_next_y, a_base_x, a_base_y = scatter_second(*a_keep, *a_got)
+        a_kept_x, a_kept_y, a_send_x, a_send_y = scatter_first(res[1], a_other)
+        a_got = to(a_send_x, 2), to(a_send_y, 4)
+        kept_x, kept_y, send_x, send_y = scatter_first(egrads[0], after(other, a_send_x))
+        a_got = lax.optimization_barrier((a_got, send_x))[0]
+        a_next_x, a_next_y, a_base_x, a_base_y = scatter_second(a_kept_x, a_kept_y, *a_got)
         a_far = to(a_next_x, 4), to(a_next_y, 2)
-        held = sums(
-            [[[(b, j), (f, j)]] for b, f in ((a_base_x, a_far[0]), (a_base_y, a_far[1])) for j in (0, 1)]
-        )
-        far = lax.optimization_barrier(((far_x, far_y), held))[0]
+        send_x, send_y, m_sum = lax.optimization_barrier((send_x, send_y, m_sum, a_next_x))[:3]
+        got = to(send_x, 2), to(send_y, 4)
+        m_sum = ring_step(sums([[[(m_sum, None), (ms[3], None)]]])[0], nt, False)
+        keep_z, send_z = sums([[[(v, None), (f, None)]] for v, f in zip((a_base_x, a_base_y), a_far)])
+        got_z = xor_send(send_z, "tensor", nt, 2)
+        got, got_z = lax.optimization_barrier((got, got_z))
+        mine, next_z = sums([[[(keep_z, j), (got_z, j)]] for j in (0, 1)])
+        next_x, next_y, base_x, base_y = scatter_second(kept_x, kept_y, *got)
+        far = to(next_x, 4), to(next_y, 2)
+        parts = [mine, xor_send(next_z, "tensor", nt, 1)]
+        layer_out = rows_of(saved[1] + (m_sum.astype(F4) + ms[0].astype(F4)))
+        parts = lax.optimization_barrier((parts, layer_out, grad_tokens))[0]
+        g_qkv, g_out, g_gain, g_bias, g_outb, g_router, g_dbias, g_ub, g_qvb = finish(parts, dr, qr)
         g_up, g_down = add_all([base_x, far[0]])[0], add_all([base_y, far[1]])[0]
-        parts = [held[0]] + [xor_send(held[m], "tensor", nt, m) for m in range(1, nt)]
-        g_qkv, g_out, g_gain, g_bias, g_outb, g_router, g_dbias, g_ub, g_qvb = finish(parts, dr, qr)
         g_outb, g_router = g_outb[0], g_router.T
     else:
         egrads = halves(egrads, 2, 1)
@@ -935,18 +938,13 @@
         g_qkv, g_out = mine[: 3 * dr].reshape(3, dr, LANES), mine[3 * dr :]
         for s in range(2, nt):
             m_sum = ring_step(add_all([m_sum, ms[s]]).astype(BF), nt, False)
+        layer_out = rows_of(saved[1] + (m_sum.astype(F4) + ms[0].astype(F4)))
         g_ub = lax.dynamic_slice(lax.psum(flat, "dp"), (UBIAS, me * fr), (EXPERTS, fr))
         flat = lax.psum(flat, ("dp", "tensor"))
         cut = lax.dynamic_slice(flat, (0, me * dr), (NROWS, dr))
         g_gain, g_bias, g_outb = cut[0:2], cut[2:4], cut[4]
         g_router, g_dbias = cut[ROUTER : ROUTER + 4].T, cut[DBIAS : DBIAS + 4]
         g_qvb = lax.dynamic_slice(flat, (QVB, (met * nd + me) * qr), (2, qr))
-
-    def rows_of(v):
-        return jnp.concatenate([v[i * PAD : i * PAD + SEQ] for i in range(nimg)])
-
-    layer_out = rows_of(saved[1] + (m_sum.astype(F4) + ms[0].astype(F4)))
-    grad_tokens = rows_of(gtok)
 
     return (
         layer_out,

time: 170 us -> 169 us (level)
    ppermute x26 -> x25, waiting for transfers between devices: 34.5 us -> 37.7 us  [xor_send(): return lax.ppermute(x, axis, [(i, i ^ mask) for i in range(n)])]
    ppermute x12, waiting for transfers between devices: 23.9 us -> 20.8 us  [ring_step(): return lax.ppermute(x, 'tensor', pairs)]
    ppermute x26 -> x25, starting transfers between devices: 28.3 us -> 28.4 us  [xor_send(): return lax.ppermute(x, axis, [(i, i ^ mask) for i in range(n)])]
  transfers between devices with their start and end apart: 38 -> 37, of which waited for: 27 -> 26; matrix products, arithmetic and copies ran while one was open for 3% -> 4% of each run, Pallas kernels for 36% -> 36%
where the time goes in v2:
time: 169 us
  Pallas kernels  61.9 us (37%)
  waiting for transfers between devices  58.5 us (35%)
  starting transfers between devices  35.7 us (21%)
  other arithmetic  6.88 us (4%)
  local copies, waits for them, and re-layouts  4.6 us (3%)
    ppermute x25, waiting for transfers between devices, xor_send(): return lax.ppermute(x, axis, [(i, i ^ mask) for i in range(n)])  37.7 us
    pallas_call x4, Pallas kernels, expert_shard(): pl.pallas_call(partial(expert_kernel, nimg, shard), out_shape=[low, low,...  30.8 us
    ppermute x25, starting transfers between devices, xor_send(): return lax.ppermute(x, axis, [(i, i ^ mask) for i in range(n)])  28.4 us
    ppermute x12, waiting for transfers between devices, ring_step(): return lax.ppermute(x, 'tensor', pairs)  20.8 us
    pallas_call x1, Pallas kernels, expert_grads(): pl.pallas_call(partial(expert_grad_kernel, nt, gmasks), out_shape=[jax.Sh...  10 us
    pallas_call x1, Pallas kernels, attn_backward(): pl.pallas_call(partial(attn_backward_kernel, nimg, len(sms), len(gubs), g...  9.66 us
    ppermute x12, starting transfers between devices, ring_step(): return lax.ppermute(x, 'tensor', pairs)  7.32 us
    pallas_call x1, Pallas kernels, attn_forward(): pl.pallas_call(partial(attn_forward_kernel, nimg), out_shape=shapes, in_s...  4.32 us
  transfers between devices with their start and end apart: 37, of which 26 were waited for; matrix products, arithmetic and copies ran while one was open for 4% of the time, Pallas kernels for 36%

profile of v2, /device:TPU:0, one launch (start us, length us, event | category | flops | bytes accessed | tf_op | source)
XLA Modules:
  0.0 168.6 jit_solution(8578318595288765843)
XLA Ops:
  0.7 0.8 pad_maximum_fusion.6
  1.5 2.2 %concatenate.42 = bf16[16,64]{1,0:T(8,128)(2,1)S(1)} concatenate(bf16[2,64]{1,0:T(2,128)(2,1)} %param.20, bf16[2,64]{1,0:T(2,128)(2,1)} %param.21, bf16[1,64]{1,0:T(2,128)(2,1)} %bitcast.51, bf16[4,64]{1,0:T(4,128)(2,1)} %bitcast.50, bf16[4,64]{1,0:T(4,128)(2,1)} %param.30, bf16[3,64]{1,0:T(4,128)(2,1)S(1)} %broadcast_in_dim.18), dimensions={0} | concatenate | bytes 4096 | tf_op jit(solution)/shard_map/concatenate | solution.py:797
  3.7 0.8 fusion.11
  4.5 4.1 %collective-permute-start.1 = (bf16[272,128]{1,0:T(8,128)(2,1)S(1)}, bf16[272,128]{1,0:T(8,128)(2,1)S(1)}, u32[]{:S(2)}, u32[]{:S(2)}) collective-permute-start(bf16[272,128]{1,0:T(8,128)(2,1)S(1)} %fusion.11), channel_id=1, source_target_pairs={{0,2},{1,3},{2,0},{3,1},{4,6},{5,7},{6,4},{7,5},{8,10},{9,11},{10,... | collective-permute-start | bytes 208904 | tf_op jit(solution)/shard_map/ppermute | solution.py:46
  8.6 1.6 collective-permute-start
  10.2 1.0 slice.43
  11.2 1.2 slice_select_fusion
  12.9 3.4 %collective-permute-done.2 = bf16[272,128]{1,0:T(8,128)(2,1)S(1)} collective-permute-done((bf16[272,128]{1,0:T(8,128)(2,1)S(1)}, bf16[272,128]{1,0:T(8,128)(2,1)S(1)}, u32[]{:S(2)}, u32[]{:S(2)}) %collective-permute-start.2) | collective-permute-done | bytes 69664 | tf_op jit(solution)/shard_map/ppermute | solution.py:46
  16.3 1.6 collective-permute-start.4
  17.9 1.5 collective-permute-start.3
  19.5 0.7 dynamic-slice_bitcast_fusion
  20.1 3.0 %collective-permute-done.4 = bf16[4,272,128]{2,1,0:T(8,128)(2,1)S(1)} collective-permute-done((bf16[4,272,128]{2,1,0:T(8,128)(2,1)S(1)}, bf16[4,272,128]{2,1,0:T(8,128)(2,1)S(1)}, u32[]{:S(2)}, u32[]{:S(2)}) %collective-permute-start.4) | collective-permute-done | bytes 278560 | tf_op jit(solution)/shard_map/ppermute | solution.py:46
  23.2 1.6 collective-permute-start.6
  24.8 0.9 collective-permute-done.3
  25.7 0.6 collective-permute-start.5
  27.0 2.8 %collective-permute-done.7.cot_ref.refs_5_ = bf16[400,512]{1,0:T(8,128)(2,1)S(1)} collective-permute-done((bf16[400,512]{1,0:T(8,128)(2,1)S(1)}, bf16[400,512]{1,0:T(8,128)(2,1)S(1)}, u32[]{:S(2)}, u32[]{:S(2)}) %collective-permute-start.7) | collective-permute-done | bytes 409632 | tf_op jit(solution)/shard_map/ppermute | solution.py:56
  29.8 1.0 collective-permute-done.5
  31.2 0.6 collective-permute-start.11
  31.8 1.0 collective-permute-start.10
  33.8 2.9 %assemble.1 = (bf16[4,512,512]{2,1,0:T(8,128)(2,1)S(1)}, f32[32,512]{1,0:T(8,128)S(1)}) custom-call(s32[6]{0:T(128)S(1)} %pad_add_fusion.ids, bf16[4,4,272,128]{3,2,1,0:T(8,128)(2,1)S(1)} %pad_maximum_fusion.1.refs_0_, bf16[4,4,272,128]{3,2,1,0:T(8,128)(2,1)S(1)} %collective-permute-done.8.refs_1_), custom_call_target="tpu_custom_call" | custom-call | bytes 66000 | tf_op jit(solution)/shard_map/assemble/pallas_call | solution.py:336
  36.8 4.3 %attn_forward.1 = (bf16[400,512]{1,0:T(8,128)(2,1)S(1)}, f32[400,512]{1,0:T(8,128)}, bf16[400,512]{1,0:T(8,128)(2,1)}, bf16[400,512]{1,0:T(8,128)(2,1)}, bf16[40...) custom-call(bf16[400,512]{1,0:T(8,128)(2,1)S(1)} %fusion.2.x_ref.refs_2_, ...), custom_call_target="tpu_custom_call" | custom-call | bytes 297000 | tf_op jit(solution)/shard_map/attn_forward/pallas_call | solution.py:411
  41.1 1.3 collective-permute-start.9
  42.4 3.1 %collective-permute-done.11 = bf16[8,64,512]{2,1,0:T(8,128)(2,1)S(1)} collective-permute-done((bf16[8,64,512]{2,1,0:T(8,128)(2,1)S(1)}, bf16[8,64,512]{2,1,0:T(8,128)(2,1)S(1)}, u32[]{:S(2)}, u32[]{:S(2)}) %collective-permute-start.11) | collective-permute-done | bytes 524320 | tf_op jit(solution)/shard_map/ppermute | solution.py:46
  45.9 1.3 collective-permute-start.13
  47.2 1.7 collective-permute-start.12
  48.9 4.6 %collective-permute-done.13 = bf16[4,64,512]{2,1,0:T(8,128)(2,1)S(1)} collective-permute-done((bf16[4,64,512]{2,1,0:T(8,128)(2,1)S(1)}, bf16[4,64,512]{2,1,0:T(8,128)(2,1)S(1)}, u32[]{:S(2)}, u32[]{:S(2)}) %collective-permute-start.13) | collective-permute-done | bytes 262176 | tf_op jit(solution)/shard_map/ppermute | solution.py:46
  53.5 1.3 collective-permute-done.12
  55.3 1.9 %collective-permute-start.17 = (bf16[400,512]{1,0:T(8,128)(2,1)S(1)}, bf16[400,512]{1,0:T(8,128)(2,1)S(1)}, u32[]{:S(2)}, u32[]{:S(2)}) collective-permute-start(bf16[400,512]{1,0:T(8,128)(2,1)S(1)} %collective-permute-done.9.hn2_ref.refs_1_), channel_id=1, source_target_pairs={{0,1},{1,3},{3,2},{2,0},{4,5},{5,7},{7,6},{6,4},{8,9},{9,11},{11,1... | collective-permute-start | bytes 1228808 | tf_op jit(solution)/shard_map/ppermute | solution.py:56
  57.2 2.1 %collective-permute-done.15.refs_1_ = bf16[4,8,64,512]{3,2,1,0:T(8,128)(2,1)S(1)} collective-permute-done((bf16[4,8,64,512]{3,2,1,0:T(8,128)(2,1)S(1)}, bf16[4,8,64,512]{3,2,1,0:T(8,128)(2,1)S(1)}, u32[]{:S(2)}, u32[]{:S(2)}) %collective-permute-start.15) | collective-permute-done | bytes 2097184 | tf_op jit(solution)/shard_map/ppermute | solution.py:46
  59.3 1.9 %gather_experts.1 = (bf16[512,2048]{1,0:T(8,128)(2,1)S(1)}, bf16[512,2048]{1,0:T(8,128)(2,1)S(1)}) custom-call(s32[6]{0:T(128)S(1)} %pad_add_fusion.ids, bf16[4,8,64,512]{3,2,1,0:T(8,128)(2,1)S(1)} %pad_maximum_fusion.refs_0_, bf16[4,8,64,512]{3,2,1,0:T(8,128)(2,1)S(1)} %collective-permute-done.15.refs_1_), custom_call_target="tpu_custom_call" | custom-call | bytes 99000 | tf_op jit(solution)/shard_map/gather_experts/pallas_call | solution.py:443
  61.3 7.7 %expert_shard.4 = (bf16[400,512]{1,0:T(8,128)(2,1)S(1)}, bf16[400,512]{1,0:T(8,128)(2,1)S(1)}, bf16[400,2048]{1,0:T(8,128)(2,1)S(1)}, bf16[400,2048]{1,0:T(8,128)(2,1)S(1)}, f32[16,512]{1,0:T(8,128)S(1)}) custom-call(s32[6]{0:T(128)S(1)} %pad_add_fusion.ids, s32[8,200,2]{2,1,0:T(8,128)S(1)} %pad.26.keep_ref, ...), custom_call_target="tpu_custom_call" | custom-call | bytes 231000 | tf_op jit(solution)/shard_map/expert_shard/pallas_call | solution.py:521
  69.0 8.3 %collective-permute-done.17.hn2_ref.refs_2_ = bf16[400,512]{1,0:T(8,128)(2,1)S(1)} collective-permute-done((bf16[400,512]{1,0:T(8,128)(2,1)S(1)}, bf16[400,512]{1,0:T(8,128)(2,1)S(1)}, u32[]{:S(2)}, u32[]{:S(2)}) %collective-permute-start.17) | collective-permute-done | bytes 409632 | tf_op jit(solution)/shard_map/ppermute | solution.py:56
  77.3 7.6 %expert_shard.5 = (bf16[400,512]{1,0:T(8,128)(2,1)S(1)}, bf16[400,512]{1,0:T(8,128)(2,1)S(1)}, bf16[400,2048]{1,0:T(8,128)(2,1)S(1)}, bf16[400,2048]{1,0:T(8,128)(2,1)S(1)}, f32[16,512]{1,0:T(8,128)S(1)}) custom-call(s32[6]{0:T(128)S(1)} %pad_add_fusion.ids, s32[8,200,2]{2,1,0:T(8,128)S(1)} %pad.26.keep_ref, ...), custom_call_target="tpu_custom_call" | custom-call | bytes 231000 | tf_op jit(solution)/shard_map/expert_shard/pallas_call | solution.py:521
  84.9 1.1 collective-permute-done.16.refs_0_
  86.1 1.1 collective-permute-start.18
  87.2 7.8 %expert_shard.6 = (bf16[400,512]{1,0:T(8,128)(2,1)S(1)}, bf16[400,512]{1,0:T(8,128)(2,1)S(1)}, bf16[400,2048]{1,0:T(8,128)(2,1)S(1)}, bf16[400,2048]{1,0:T(8,128)(2,1)S(1)}, f32[16,512]{1,0:T(8,128)S(1)}) custom-call(s32[6]{0:T(128)S(1)} %pad_add_fusion.ids, s32[8,200,2]{2,1,0:T(8,128)S(1)} %pad.26.keep_ref, ...), custom_call_target="tpu_custom_call" | custom-call | bytes 231000 | tf_op jit(solution)/shard_map/expert_shard/pallas_call | solution.py:521
  95.0 7.7 %expert_shard.7 = (bf16[400,512]{1,0:T(8,128)(2,1)S(1)}, bf16[400,512]{1,0:T(8,128)(2,1)S(1)}, bf16[400,2048]{1,0:T(8,128)(2,1)S(1)}, bf16[400,2048]{1,0:T(8,128)(2,1)S(1)}, f32[16,512]{1,0:T(8,128)S(1)}) custom-call(s32[6]{0:T(128)S(1)} %pad_add_fusion.ids, s32[8,200,2]{2,1,0:T(8,128)S(1)} %pad.26.keep_ref, ...), custom_call_target="tpu_custom_call" | custom-call | bytes 231000 | tf_op jit(solution)/shard_map/expert_shard/pallas_call | solution.py:521
  103.2 0.9 collective-permute-start.21
  104.1 10.0 %expert_grads.1 = (f32[4,1,512]{2,1,0:T(1,128)S(1)}, bf16[4,2,4,64,512]{4,3,2,1,0:T(8,128)(2,1)S(1)}, bf16[4,2,4,64,512]{4,3,2,1,0:T(8,128)(2,1)S(1)}) custom-call(s32[6]{0:T(128)S(1)} %pad_add_fusion.ids, bf16[400,512]{1,0:T(8,128)(2,1)S(1)} %get-tuple-element.131.hn2_ref.refs_0_, bf16[400,512]{1,0:T(8,128)(2,1)S(1)} %collective-permute-done.9.hn2_ref.refs_1_, ...), custom_call_target="tpu_custom_call" | custom-call | bytes 297000 | tf_op jit(solution)/shard_map/expert_grads/pallas_call | solution.py:564
  114.1 1.0 collective-permute-done.21.refs_0_
  115.1 1.2 collective-permute-start.23
  116.3 9.7 %attn_backward.1 = (f32[400,512]{1,0:T(8,128)S(1)}, bf16[4,4,272,128]{3,2,1,0:T(8,128)(2,1)S(1)}, bf16[4,4,272,128]{3,2,1,0:T(8,128)(2,1)S(1)}, f32[32,512]{1,0:T(8,128)}) custom-call(s32[6]{0:T(128)S(1)} %pad_add_fusion.ids, bf16[400,512]{1,0:T(8,128)(2,1)S(1)} %collective-permute-done.21.refs_0_, bf16[400,512]{1,0:T(8,128)(2,1)S(1)} %get-tuple-element.135.refs_1_, ...), custom_call_target="tpu_custom_call" | custom-call | bytes 528000 | tf_op jit(solution)/shard_map/attn_backward/pallas_call | solution.py:716
  125.9 1.9 %collective-permute-done.23.refs_0_ = bf16[400,512]{1,0:T(8,128)(2,1)S(1)} collective-permute-done((bf16[400,512]{1,0:T(8,128)(2,1)S(1)}, bf16[400,512]{1,0:T(8,128)(2,1)S(1)}, u32[]{:S(2)}, u32[]{:S(2)}) %collective-permute-start.23) | collective-permute-done | bytes 409632 | tf_op jit(solution)/shard_map/ppermute | solution.py:56
  128.0 2.6 %collective-permute-done.24.refs_1_ = bf16[4,4,272,128]{3,2,1,0:T(8,128)(2,1)S(1)} collective-permute-done((bf16[4,4,272,128]{3,2,1,0:T(8,128)(2,1)S(1)}, bf16[4,4,272,128]{3,2,1,0:T(8,128)(2,1)S(1)}, u32[]{:S(2)}, u32[]{:S(2)}) %collective-permute-start.24) | collective-permute-done | bytes 1114144 | tf_op jit(solution)/shard_map/ppermute | solution.py:46
  130.9 1.5 collective-permute-start.27
  133.4 6.3 %collective-permute-done.27.refs_3_ = bf16[2,2,272,128]{3,2,1,0:T(8,128)(2,1)S(1)} collective-permute-done((bf16[2,2,272,128]{3,2,1,0:T(8,128)(2,1)S(1)}, bf16[2,2,272,128]{3,2,1,0:T(8,128)(2,1)S(1)}, u32[]{:S(2)}, u32[]{:S(2)}) %collective-permute-start.27) | collective-permute-done | bytes 278560 | tf_op jit(solution)/shard_map/ppermute | solution.py:46
  139.7 1.1 collective-permute-done.26.refs_1_
  141.1 1.3 collective-permute-start.29
  142.4 0.6 collective-permute-start.30
  143.0 1.4 collective-permute-start.31
  144.4 0.8 collective-permute-start.32
  145.3 3.7 %collective-permute-done.30.refs_3_ = bf16[2,272,128]{2,1,0:T(8,128)(2,1)S(1)} collective-permute-done((bf16[2,272,128]{2,1,0:T(8,128)(2,1)S(1)}, bf16[2,272,128]{2,1,0:T(8,128)(2,1)S(1)}, u32[]{:S(2)}, u32[]{:S(2)}) %collective-permute-start.30) | collective-permute-done | bytes 139296 | tf_op jit(solution)/shard_map/ppermute | solution.py:46
  149.0 2.9 %collective-permute-start.33 = (bf16[2,272,128]{2,1,0:T(8,128)(2,1)S(1)}, bf16[2,272,128]{2,1,0:T(8,128)(2,1)S(1)}, u32[]{:S(2)}, u32[]{:S(2)}) collective-permute-start(bf16[2,272,128]{2,1,0:T(8,128)(2,1)S(1)} %get-tuple-element.184), channel_id=1, source_target_pairs={{0,2},{1,3},{2,0},{3,1},{4,6},{5,7},{6,4},{7,5},{8,10},{9,11},{10,... | collective-permute-start | bytes 417800 | tf_op jit(solution)/shard_map/ppermute | solution.py:46
  151.9 5.4 %collective-permute-done.28 = bf16[400,512]{1,0:T(8,128)(2,1)S(1)} collective-permute-done((bf16[400,512]{1,0:T(8,128)(2,1)S(1)}, bf16[400,512]{1,0:T(8,128)(2,1)S(1)}, u32[]{:S(2)}, u32[]{:S(2)}) %collective-permute-start.28) | collective-permute-done | bytes 409632 | tf_op jit(solution)/shard_map/ppermute | solution.py:56
  157.5 1.3 collective-permute-done.33.refs_1_
  159.1 1.5 collective-permute-start.35
  160.6 0.7 collective-permute-start.34
  161.3 1.5 collective-permute-start.36
  162.8 1.3 pad_maximum_fusion.2
  164.2 0.9 collective-permute-done.34.refs_1_
  165.0 0.7 finish.1
  166.0 0.9 add_bitcast_fusion.1
  166.9 0.8 collective-permute-done.36
  167.7 0.9 add_bitcast_fusion
  (79 shorter events, 6.7 us)
Async XLA Ops:
  0.6 11.8 %copy-start.6 = (bf16[4,64]{1,0:T(4,128)(2,1)S(1)}, bf16[4,64]{1,0:T(4,128)(2,1)}, u32[]{:S(2)}) copy-start(bf16[4,64]{1,0:T(4,128)(2,1)} %param.28) | copy-start | bytes 1540
  0.7 11.8 %copy-start.7 = (bf16[2,16]{1,0:T(2,128)(2,1)S(1)}, bf16[2,16]{1,0:T(2,128)(2,1)}, u32[]{:S(2)}) copy-start(bf16[2,16]{1,0:T(2,128)(2,1)} %param.23) | copy-start | bytes 196
  0.7 18.8 %copy-start.4 = (s32[1576,2]{0,1:T(2,128)S(1)}, s32[1576,2]{0,1:T(2,128)}, u32[]{:S(2)}) copy-start(s32[1576,2]{0,1:T(2,128)} %param.18) | copy-start | bytes 37828
  0.7 18.7 %copy-start.5 = (s32[1576,2]{0,1:T(2,128)S(1)}, s32[1576,2]{0,1:T(2,128)}, u32[]{:S(2)}) copy-start(s32[1576,2]{0,1:T(2,128)} %param.19) | copy-start | bytes 37828
  4.5 8.0 %collective-permute-start.1 = (bf16[272,128]{1,0:T(8,128)(2,1)S(1)}, bf16[272,128]{1,0:T(8,128)(2,1)S(1)}, u32[]{:S(2)}, u32[]{:S(2)}) collective-permute-start(bf16[272,128]{1,0:T(8,128)(2,1)S(1)} %fusion.11), channel_id=1, source_target_pairs={{0,2},{1,3},{2,0},{3,1},{4,6},{5,7},{6,4},{7,5},{8,10},{9,11},{10,... | collective-permute-start | bytes 208904 | tf_op jit(solution)/shard_map/ppermute | solution.py:46
  8.6 4.3 %collective-permute-start = (bf16[272,128]{1,0:T(8,128)(2,1)S(1)}, bf16[272,128]{1,0:T(8,128)(2,1)S(1)}, u32[]{:S(2)}, u32[]{:S(2)}) collective-permute-start(bf16[272,128]{1,0:T(8,128)(2,1)S(1)} %fusion.11), channel_id=1, source_target_pairs={{0,1},{1,0},{2,3},{3,2},{4,5},{5,4},{6,7},{7,6},{8,9},{9,8},{10,11... | collective-permute-start | bytes 208904 | tf_op jit(solution)/shard_map/ppermute | solution.py:46
  10.2 6.1 %collective-permute-start.2 = (bf16[272,128]{1,0:T(8,128)(2,1)S(1)}, bf16[272,128]{1,0:T(8,128)(2,1)S(1)}, u32[]{:S(2)}, u32[]{:S(2)}) collective-permute-start(bf16[272,128]{1,0:T(8,128)(2,1)S(1)} %fusion.11), channel_id=1, source_target_pairs={{0,3},{1,2},{2,1},{3,0},{4,7},{5,6},{6,5},{7,4},{8,11},{9,10},{10,... | collective-permute-start | bytes 208904 | tf_op jit(solution)/shard_map/ppermute | solution.py:46
  11.2 15.3 %copy-start.1 = (bf16[394,512]{1,0:T(8,128)(2,1)S(1)}, bf16[394,512]{1,0:T(8,128)(2,1)}, u32[]{:S(2)}) copy-start(bf16[394,512]{1,0:T(8,128)(2,1)} %param.16) | copy-start | bytes 1210372
  16.3 6.9 %collective-permute-start.4 = (bf16[4,272,128]{2,1,0:T(8,128)(2,1)S(1)}, bf16[4,272,128]{2,1,0:T(8,128)(2,1)S(1)}, u32[]{:S(2)}, u32[]{:S(2)}) collective-permute-start(bf16[4,272,128]{2,1,0:T(8,128)(2,1)S(1)} %get-tuple-element.212), channel_id=1, source_target_pairs={{0,16},{4,20},{8,24},{12,28},{16,0},{20,4},{24,8},{28,12},{1,17},{... | collective-permute-start | bytes 835592 | tf_op jit(solution)/shard_map/ppermute | solution.py:46
  17.9 7.8 %collective-permute-start.3 = (bf16[4,272,128]{2,1,0:T(8,128)(2,1)S(1)}, bf16[4,272,128]{2,1,0:T(8,128)(2,1)S(1)}, u32[]{:S(2)}, u32[]{:S(2)}) collective-permute-start(bf16[4,272,128]{2,1,0:T(8,128)(2,1)S(1)} %get-tuple-element.212), channel_id=1, source_target_pairs={{0,8},{4,12},{8,0},{12,4},{16,24},{20,28},{24,16},{28,20},{1,9},{5... | collective-permute-start | bytes 835592 | tf_op jit(solution)/shard_map/ppermute | solution.py:46
  19.4 10.4 %collective-permute-start.7 = (bf16[400,512]{1,0:T(8,128)(2,1)S(1)}, bf16[400,512]{1,0:T(8,128)(2,1)S(1)}, u32[]{:S(2)}, u32[]{:S(2)}) collective-permute-start(bf16[400,512]{1,0:T(8,128)(2,1)S(1)} %fusion.3.cot_ref.refs_4_.refs_3_), channel_id=1, source_target_pairs={{0,1},{1,3},{3,2},{2,0},{4,5},{5,7},{7,6},{6,4},{8,9},{9,11},{11,1... | collective-permute-start | bytes 1228808 | tf_op jit(solution)/shard_map/ppermute | solution.py:56
  23.2 6.6 %collective-permute-start.6 = (bf16[2,272,128]{2,1,0:T(8,128)(2,1)S(1)}, bf16[2,272,128]{2,1,0:T(8,128)(2,1)S(1)}, u32[]{:S(2)}, u32[]{:S(2)}) collective-permute-start(bf16[2,272,128]{2,1,0:T(8,128)(2,1)S(1)} %slice.51), channel_id=1, source_target_pairs={{0,8},{4,12},{8,0},{12,4},{16,24},{20,28},{24,16},{28,20},{1,9},{5... | collective-permute-start | bytes 417800 | tf_op jit(solution)/shard_map/ppermute | solution.py:46
  25.7 5.1 %collective-permute-start.5 = (bf16[2,272,128]{2,1,0:T(8,128)(2,1)S(1)}, bf16[2,272,128]{2,1,0:T(8,128)(2,1)S(1)}, u32[]{:S(2)}, u32[]{:S(2)}) collective-permute-start(bf16[2,272,128]{2,1,0:T(8,128)(2,1)S(1)} %slice.50), channel_id=1, source_target_pairs={{0,16},{4,20},{8,24},{12,28},{16,0},{20,4},{24,8},{28,12},{1,17},{... | collective-permute-start | bytes 417800 | tf_op jit(solution)/shard_map/ppermute | solution.py:46
  27.0 4.1 %copy-start.2 = (bf16[4,512,64]{1,2,0:T(8,128)(2,1)S(1)}, bf16[4,512,64]{1,2,0:T(8,128)(2,1)}, u32[]{:S(2)}) copy-start(bf16[4,512,64]{1,2,0:T(8,128)(2,1)} %param.29) | copy-start | bytes 786436
  27.0 4.1 %copy-start.3 = (bf16[4,64,512]{2,1,0:T(8,128)(2,1)S(1)}, bf16[4,64,512]{2,1,0:T(8,128)(2,1)}, u32[]{:S(2)}) copy-start(bf16[4,64,512]{2,1,0:T(8,128)(2,1)} %param.27) | copy-start | bytes 786436
  31.0 2.8 %collective-permute-start.8 = (bf16[4,4,272,128]{3,2,1,0:T(8,128)(2,1)S(1)}, bf16[4,4,272,128]{3,2,1,0:T(8,128)(2,1)S(1)}, u32[]{:S(2)}, u32[]{:S(2)}) collective-permute-start(bf16[4,4,272,128]{3,2,1,0:T(8,128)(2,1)S(1)} %pad_maximum_fusion.1.refs_0_), channel_id=1, source_target_pairs={{0,4},{4,0},{8,12},{12,8},{16,20},{20,16},{24,28},{28,24},{1,5},{5... | collective-permute-start | bytes 3342344 | tf_op jit(solution)/shard_map/ppermute | solution.py:46
  31.2 14.4 %collective-permute-start.11 = (bf16[8,64,512]{2,1,0:T(8,128)(2,1)S(1)}, bf16[8,64,512]{2,1,0:T(8,128)(2,1)S(1)}, u32[]{:S(2)}, u32[]{:S(2)}) collective-permute-start(bf16[8,64,512]{2,1,0:T(8,128)(2,1)S(1)} %pad_maximum_fusion.4), channel_id=1, source_target_pairs={{0,16},{4,20},{8,24},{12,28},{16,0},{20,4},{24,8},{28,12},{1,17},{... | collective-permute-start | bytes 1572872 | tf_op jit(solution)/shard_map/ppermute | solution.py:46
  31.8 14.0 %collective-permute-start.10 = (bf16[8,64,512]{2,1,0:T(8,128)(2,1)S(1)}, bf16[8,64,512]{2,1,0:T(8,128)(2,1)S(1)}, u32[]{:S(2)}, u32[]{:S(2)}) collective-permute-start(bf16[8,64,512]{2,1,0:T(8,128)(2,1)S(1)} %pad_maximum_fusion.4), channel_id=1, source_target_pairs={{0,8},{4,12},{8,0},{12,4},{16,24},{20,28},{24,16},{28,20},{1,9},{5... | collective-permute-start | bytes 1572872 | tf_op jit(solution)/shard_map/ppermute | solution.py:46
  32.8 16.1 %collective-permute-start.14 = (bf16[400,512]{1,0:T(8,128)(2,1)S(1)}, bf16[400,512]{1,0:T(8,128)(2,1)S(1)}, u32[]{:S(2)}, u32[]{:S(2)}) collective-permute-start(bf16[400,512]{1,0:T(8,128)(2,1)S(1)} %collective-permute-done.7.cot_ref.refs_5_), channel_id=1, source_target_pairs={{0,1},{1,3},{3,2},{2,0},{4,5},{5,7},{7,6},{6,4},{8,9},{9,11},{11,1... | collective-permute-start | bytes 1228808 | tf_op jit(solution)/shard_map/ppermute | solution.py:56
  41.1 13.7 %collective-permute-start.9 = (bf16[400,512]{1,0:T(8,128)(2,1)S(1)}, bf16[400,512]{1,0:T(8,128)(2,1)S(1)}, u32[]{:S(2)}, u32[]{:S(2)}) collective-permute-start(bf16[400,512]{1,0:T(8,128)(2,1)S(1)} %get-tuple-element.131.hn2_ref.refs_0_), channel_id=1, source_target_pairs={{0,1},{1,3},{3,2},{2,0},{4,5},{5,7},{7,6},{6,4},{8,9},{9,11},{11,1... | collective-permute-start | bytes 1228808 | tf_op jit(solution)/shard_map/ppermute | solution.py:56
  45.9 7.6 %collective-permute-start.13 = (bf16[4,64,512]{2,1,0:T(8,128)(2,1)S(1)}, bf16[4,64,512]{2,1,0:T(8,128)(2,1)S(1)}, u32[]{:S(2)}, u32[]{:S(2)}) collective-permute-start(bf16[4,64,512]{2,1,0:T(8,128)(2,1)S(1)} %slice.45), channel_id=1, source_target_pairs={{0,8},{4,12},{8,0},{12,4},{16,24},{20,28},{24,16},{28,20},{1,9},{5... | collective-permute-start | bytes 786440 | tf_op jit(solution)/shard_map/ppermute | solution.py:46
  47.2 7.6 %collective-permute-start.12 = (bf16[4,64,512]{2,1,0:T(8,128)(2,1)S(1)}, bf16[4,64,512]{2,1,0:T(8,128)(2,1)S(1)}, u32[]{:S(2)}, u32[]{:S(2)}) collective-permute-start(bf16[4,64,512]{2,1,0:T(8,128)(2,1)S(1)} %slice.44), channel_id=1, source_target_pairs={{0,16},{4,20},{8,24},{12,28},{16,0},{20,4},{24,8},{28,12},{1,17},{... | collective-permute-start | bytes 786440 | tf_op jit(solution)/shard_map/ppermute | solution.py:46
  55.1 4.2 %collective-permute-start.15 = (bf16[4,8,64,512]{3,2,1,0:T(8,128)(2,1)S(1)}, bf16[4,8,64,512]{3,2,1,0:T(8,128)(2,1)S(1)}, u32[]{:S(2)}, u32[]{:S(2)}) collective-permute-start(bf16[4,8,64,512]{3,2,1,0:T(8,128)(2,1)S(1)} %pad_maximum_fusion.refs_0_), channel_id=1, source_target_pairs={{0,4},{4,0},{8,12},{12,8},{16,20},{20,16},{24,28},{28,24},{1,5},{5... | collective-permute-start | bytes 6291464 | tf_op jit(solution)/shard_map/ppermute | solution.py:46
  55.2 13.8 %collective-permute-start.19 = (bf16[400,512]{1,0:T(8,128)(2,1)S(1)}, bf16[400,512]{1,0:T(8,128)(2,1)S(1)}, u32[]{:S(2)}, u32[]{:S(2)}) collective-permute-start(bf16[400,512]{1,0:T(8,128)(2,1)S(1)} %collective-permute-done.14.cot_ref.refs_6_), channel_id=1, source_target_pairs={{0,1},{1,3},{3,2},{2,0},{4,5},{5,7},{7,6},{6,4},{8,9},{9,11},{11,1... | collective-permute-start | bytes 1228808 | tf_op jit(solution)/shard_map/ppermute | solution.py:56
  55.3 22.0 %collective-permute-start.17 = (bf16[400,512]{1,0:T(8,128)(2,1)S(1)}, bf16[400,512]{1,0:T(8,128)(2,1)S(1)}, u32[]{:S(2)}, u32[]{:S(2)}) collective-permute-start(bf16[400,512]{1,0:T(8,128)(2,1)S(1)} %collective-permute-done.9.hn2_ref.refs_1_), channel_id=1, source_target_pairs={{0,1},{1,3},{3,2},{2,0},{4,5},{5,7},{7,6},{6,4},{8,9},{9,11},{11,1... | collective-permute-start | bytes 1228808 | tf_op jit(solution)/shard_map/ppermute | solution.py:56
  68.9 17.1 %collective-permute-start.16 = (bf16[400,512]{1,0:T(8,128)(2,1)S(1)}, bf16[400,512]{1,0:T(8,128)(2,1)S(1)}, u32[]{:S(2)}, u32[]{:S(2)}) collective-permute-start(bf16[400,512]{1,0:T(8,128)(2,1)S(1)} %get-tuple-element.126), channel_id=1, source_target_pairs={{0,1},{1,3},{3,2},{2,0},{4,5},{5,7},{7,6},{6,4},{8,9},{9,11},{11,1... | collective-permute-start | bytes 1228808 | tf_op jit(solution)/shard_map/ppermute | solution.py:56
  77.3 17.8 %collective-permute-start.20 = (bf16[400,512]{1,0:T(8,128)(2,1)S(1)}, bf16[400,512]{1,0:T(8,128)(2,1)S(1)}, u32[]{:S(2)}, u32[]{:S(2)}) collective-permute-start(bf16[400,512]{1,0:T(8,128)(2,1)S(1)} %collective-permute-done.17.hn2_ref.refs_2_), channel_id=1, source_target_pairs={{0,1},{1,3},{3,2},{2,0},{4,5},{5,7},{7,6},{6,4},{8,9},{9,11},{11,1... | collective-permute-start | bytes 1228808 | tf_op jit(solution)/shard_map/ppermute | solution.py:56
  86.1 16.9 %collective-permute-start.18 = (bf16[400,512]{1,0:T(8,128)(2,1)S(1)}, bf16[400,512]{1,0:T(8,128)(2,1)S(1)}, u32[]{:S(2)}, u32[]{:S(2)}) collective-permute-start(bf16[400,512]{1,0:T(8,128)(2,1)S(1)} %sums.10), channel_id=1, source_target_pairs={{0,1},{1,3},{3,2},{2,0},{4,5},{5,7},{7,6},{6,4},{8,9},{9,11},{11,1... | collective-permute-start | bytes 1228808 | tf_op jit(solution)/shard_map/ppermute | solution.py:56
  103.2 11.9 %collective-permute-start.21 = (bf16[400,512]{1,0:T(8,128)(2,1)S(1)}, bf16[400,512]{1,0:T(8,128)(2,1)S(1)}, u32[]{:S(2)}, u32[]{:S(2)}) collective-permute-start(bf16[400,512]{1,0:T(8,128)(2,1)S(1)} %sums.11), channel_id=1, source_target_pairs={{0,1},{1,3},{3,2},{2,0},{4,5},{5,7},{7,6},{6,4},{8,9},{9,11},{11,1... | collective-permute-start | bytes 1228808 | tf_op jit(solution)/shard_map/ppermute | solution.py:56
  115.1 12.8 %collective-permute-start.22 = (bf16[4,2,4,64,512]{4,3,2,1,0:T(8,128)(2,1)S(1)}, bf16[4,2,4,64,512]{4,3,2,1,0:T(8,128)(2,1)S(1)}, u32[]{:S(2)}, u32[]{:S(2)}) collective-permute-start(bf16[4,2,4,64,512]{4,3,2,1,0:T(8,128)(2,1)S(1)} %get-tuple-element.145), channel_id=1, source_target_pairs={{0,4},{4,0},{8,12},{12,8},{16,20},{20,16},{24,28},{28,24},{1,5},{5... | collective-permute-start | bytes 6291464 | tf_op jit(solution)/shard_map/ppermute | solution.py:46
  115.1 12.8 %collective-permute-start.23 = (bf16[400,512]{1,0:T(8,128)(2,1)S(1)}, bf16[400,512]{1,0:T(8,128)(2,1)S(1)}, u32[]{:S(2)}, u32[]{:S(2)}) collective-permute-start(bf16[400,512]{1,0:T(8,128)(2,1)S(1)} %get-tuple-element.147), channel_id=1, source_target_pairs={{0,1},{1,3},{3,2},{2,0},{4,5},{5,7},{7,6},{6,4},{8,9},{9,11},{11,1... | collective-permute-start | bytes 1228808 | tf_op jit(solution)/shard_map/ppermute | solution.py:56
  127.9 2.8 %collective-permute-start.24 = (bf16[4,4,272,128]{3,2,1,0:T(8,128)(2,1)S(1)}, bf16[4,4,272,128]{3,2,1,0:T(8,128)(2,1)S(1)}, u32[]{:S(2)}, u32[]{:S(2)}) collective-permute-start(bf16[4,4,272,128]{3,2,1,0:T(8,128)(2,1)S(1)} %get-tuple-element.161), channel_id=1, source_target_pairs={{0,4},{4,0},{8,12},{12,8},{16,20},{20,16},{24,28},{28,24},{1,5},{5... | collective-permute-start | bytes 3342344 | tf_op jit(solution)/shard_map/ppermute | solution.py:46
  128.0 12.9 %collective-permute-start.25 = (bf16[400,512]{1,0:T(8,128)(2,1)S(1)}, bf16[400,512]{1,0:T(8,128)(2,1)S(1)}, u32[]{:S(2)}, u32[]{:S(2)}) collective-permute-start(bf16[400,512]{1,0:T(8,128)(2,1)S(1)} %sums.14), channel_id=1, source_target_pairs={{0,1},{1,3},{3,2},{2,0},{4,5},{5,7},{7,6},{6,4},{8,9},{9,11},{11,1... | collective-permute-start | bytes 1228808 | tf_op jit(solution)/shard_map/ppermute | solution.py:56
  130.9 8.8 %collective-permute-start.27 = (bf16[2,2,272,128]{3,2,1,0:T(8,128)(2,1)S(1)}, bf16[2,2,272,128]{3,2,1,0:T(8,128)(2,1)S(1)}, u32[]{:S(2)}, u32[]{:S(2)}) collective-permute-start(bf16[2,2,272,128]{3,2,1,0:T(8,128)(2,1)S(1)} %get-tuple-element.169), channel_id=1, source_target_pairs={{0,16},{4,20},{8,24},{12,28},{16,0},{20,4},{24,8},{28,12},{1,17},{... | collective-permute-start | bytes 835592 | tf_op jit(solution)/shard_map/ppermute | solution.py:46
  132.4 8.4 %collective-permute-start.26 = (bf16[2,2,272,128]{3,2,1,0:T(8,128)(2,1)S(1)}, bf16[2,2,272,128]{3,2,1,0:T(8,128)(2,1)S(1)}, u32[]{:S(2)}, u32[]{:S(2)}) collective-permute-start(bf16[2,2,272,128]{3,2,1,0:T(8,128)(2,1)S(1)} %get-tuple-element.162), channel_id=1, source_target_pairs={{0,8},{4,12},{8,0},{12,4},{16,24},{20,28},{24,16},{28,20},{1,9},{5... | collective-permute-start | bytes 835592 | tf_op jit(solution)/shard_map/ppermute | solution.py:46
  140.9 16.4 %copy-start = (f32[400,512]{1,0:T(8,128)S(1)}, f32[400,512]{1,0:T(8,128)}, u32[]{:S(2)}) copy-start(f32[400,512]{1,0:T(8,128)} %get-tuple-element.116.refs_4_) | copy-start | bytes 2457604
  141.0 16.3 %collective-permute-start.28 = (bf16[400,512]{1,0:T(8,128)(2,1)S(1)}, bf16[400,512]{1,0:T(8,128)(2,1)S(1)}, u32[]{:S(2)}, u32[]{:S(2)}) collective-permute-start(bf16[400,512]{1,0:T(8,128)(2,1)S(1)} %sums.16), channel_id=1, source_target_pairs={{0,1},{1,3},{3,2},{2,0},{4,5},{5,7},{7,6},{6,4},{8,9},{9,11},{11,1... | collective-permute-start | bytes 1228808 | tf_op jit(solution)/shard_map/ppermute | solution.py:56
  141.1 7.9 %collective-permute-start.29 = (bf16[2,272,128]{2,1,0:T(8,128)(2,1)S(1)}, bf16[2,272,128]{2,1,0:T(8,128)(2,1)S(1)}, u32[]{:S(2)}, u32[]{:S(2)}) collective-permute-start(bf16[2,272,128]{2,1,0:T(8,128)(2,1)S(1)} %get-tuple-element.173), channel_id=1, source_target_pairs={{0,16},{4,20},{8,24},{12,28},{16,0},{20,4},{24,8},{28,12},{1,17},{... | collective-permute-start | bytes 417800 | tf_op jit(solution)/shard_map/ppermute | solution.py:46
  142.4 6.5 %collective-permute-start.30 = (bf16[2,272,128]{2,1,0:T(8,128)(2,1)S(1)}, bf16[2,272,128]{2,1,0:T(8,128)(2,1)S(1)}, u32[]{:S(2)}, u32[]{:S(2)}) collective-permute-start(bf16[2,272,128]{2,1,0:T(8,128)(2,1)S(1)} %get-tuple-element.180), channel_id=1, source_target_pairs={{0,8},{4,12},{8,0},{12,4},{16,24},{20,28},{24,16},{28,20},{1,9},{5... | collective-permute-start | bytes 417800 | tf_op jit(solution)/shard_map/ppermute | solution.py:46
  143.0 15.8 %collective-permute-start.31 = (bf16[2,1,4,64,512]{4,3,2,1,0:T(8,128)(2,1)S(1)}, bf16[2,1,4,64,512]{4,3,2,1,0:T(8,128)(2,1)S(1)}, u32[]{:S(2)}, u32[]{:S(2)}) collective-permute-start(bf16[2,1,4,64,512]{4,3,2,1,0:T(8,128)(2,1)S(1)} %get-tuple-element.182), channel_id=1, source_target_pairs={{0,8},{4,12},{8,0},{12,4},{16,24},{20,28},{24,16},{28,20},{1,9},{5... | collective-permute-start | bytes 1572872 | tf_op jit(solution)/shard_map/ppermute | solution.py:46
  144.4 14.4 %collective-permute-start.32 = (bf16[2,1,4,64,512]{4,3,2,1,0:T(8,128)(2,1)S(1)}, bf16[2,1,4,64,512]{4,3,2,1,0:T(8,128)(2,1)S(1)}, u32[]{:S(2)}, u32[]{:S(2)}) collective-permute-start(bf16[2,1,4,64,512]{4,3,2,1,0:T(8,128)(2,1)S(1)} %get-tuple-element.183), channel_id=1, source_target_pairs={{0,16},{4,20},{8,24},{12,28},{16,0},{20,4},{24,8},{28,12},{1,17},{... | collective-permute-start | bytes 1572872 | tf_op jit(solution)/shard_map/ppermute | solution.py:46
  149.0 9.8 %collective-permute-start.33 = (bf16[2,272,128]{2,1,0:T(8,128)(2,1)S(1)}, bf16[2,272,128]{2,1,0:T(8,128)(2,1)S(1)}, u32[]{:S(2)}, u32[]{:S(2)}) collective-permute-start(bf16[2,272,128]{2,1,0:T(8,128)(2,1)S(1)} %get-tuple-element.184), channel_id=1, source_target_pairs={{0,2},{1,3},{2,0},{3,1},{4,6},{5,7},{6,4},{7,5},{8,10},{9,11},{10,... | collective-permute-start | bytes 417800 | tf_op jit(solution)/shard_map/ppermute | solution.py:46
  159.1 6.9 %collective-permute-start.35 = (bf16[1,4,64,512]{3,2,1,0:T(8,128)(2,1)S(1)}, bf16[1,4,64,512]{3,2,1,0:T(8,128)(2,1)S(1)}, u32[]{:S(2)}, u32[]{:S(2)}) collective-permute-start(bf16[1,4,64,512]{3,2,1,0:T(8,128)(2,1)S(1)} %get-tuple-element.202), channel_id=1, source_target_pairs={{0,16},{4,20},{8,24},{12,28},{16,0},{20,4},{24,8},{28,12},{1,17},{... | collective-permute-start | bytes 786440 | tf_op jit(solution)/shard_map/ppermute | solution.py:46
  160.6 4.4 %collective-permute-start.34 = (bf16[272,128]{1,0:T(8,128)(2,1)S(1)}, bf16[272,128]{1,0:T(8,128)(2,1)S(1)}, u32[]{:S(2)}, u32[]{:S(2)}) collective-permute-start(bf16[272,128]{1,0:T(8,128)(2,1)S(1)} %get-tuple-element.187), channel_id=1, source_target_pairs={{0,1},{1,0},{2,3},{3,2},{4,5},{5,4},{6,7},{7,6},{8,9},{9,8},{10,11... | collective-permute-start | bytes 208904 | tf_op jit(solution)/shard_map/ppermute | solution.py:46
  161.3 6.4 %collective-permute-start.36 = (bf16[1,4,64,512]{3,2,1,0:T(8,128)(2,1)S(1)}, bf16[1,4,64,512]{3,2,1,0:T(8,128)(2,1)S(1)}, u32[]{:S(2)}, u32[]{:S(2)}) collective-permute-start(bf16[1,4,64,512]{3,2,1,0:T(8,128)(2,1)S(1)} %get-tuple-element.205), channel_id=1, source_target_pairs={{0,8},{4,12},{8,0},{12,4},{16,24},{20,28},{24,16},{28,20},{1,9},{5... | collective-permute-start | bytes 786440 | tf_op jit(solution)/shard_map/ppermute | solution.py:46

commit v3 on v2

--- a/solution.py
+++ b/solution.py
@@ -291,10 +291,8 @@
                 j = jnp.bitwise_xor(met, jm)
                 rows_at = pl.ds(pl.multiple_of(i * dr, dr), dr)
                 lanes_at = pl.ds(pl.multiple_of(j * LANES, LANES), LANES)
-                for s in range(4):
-                    pairs.append(
-                        (ref.at[idx, jm, s * dr : (s + 1) * dr], w_ref.at[s, rows_at, lanes_at])
-                    )
+                whole = ref.at[idx, jm, 0 : 4 * dr].reshape(4, dr, LANES)
+                pairs.append((whole, w_ref.at[:, rows_at, lanes_at]))
                 pairs.append((ref.at[idx, jm, 4 * dr : 4 * dr + SMALL], small_ref.at[mask, jm]))
     run_copies(pairs, sems)
     rows_ref[...] = jnp.zeros(rows_ref.shape, F4)
@@ -343,7 +341,7 @@
         out_specs=[VM, VM],
         scratch_shapes=[
             pltpu.VMEM((nd, nt, SMALL, LANES), BF),
-            pltpu.SemaphoreType.DMA((5 * nd * nt,)),
+            pltpu.SemaphoreType.DMA((2 * nd * nt,)),
         ],
         compiler_params=params(8),
         cost_estimate=cost(2),

time: 169 us -> 169 us (level)
  waiting for transfers between devices: 58.5 us -> 60.6 us
  transfers between devices with their start and end apart: 37 -> 37, of which waited for: 26 -> 27; matrix products, arithmetic and copies ran while one was open for 4% -> 4% of each run, Pallas kernels for 36% -> 36%
where the time goes in v3:
time: 169 us; the launch traced here: 168 us
  Pallas kernels  60.8 us (36%)
  waiting for transfers between devices  60.6 us (36%)
  starting transfers between devices  34.5 us (20%)
  other arithmetic  6.88 us (4%)
  local copies, waits for them, and re-layouts  4.6 us (3%)
    ppermute x25, waiting for transfers between devices, xor_send(): return lax.ppermute(x, axis, [(i, i ^ mask) for i in range(n)])  38.9 us
    pallas_call x4, Pallas kernels, expert_shard(): pl.pallas_call(partial(expert_kernel, nimg, shard), out_shape=[low, low,...  30.8 us
    ppermute x25, starting transfers between devices, xor_send(): return lax.ppermute(x, axis, [(i, i ^ mask) for i in range(n)])  28.1 us
    ppermute x12, waiting for transfers between devices, ring_step(): return lax.ppermute(x, 'tensor', pairs)  21.6 us
    pallas_call x1, Pallas kernels, expert_grads(): pl.pallas_call(partial(expert_grad_kernel, nt, gmasks), out_shape=[jax.Sh...  10 us
    pallas_call x1, Pallas kernels, attn_backward(): pl.pallas_call(partial(attn_backward_kernel, nimg, len(sms), len(gubs), g...  9.65 us
    ppermute x12, starting transfers between devices, ring_step(): return lax.ppermute(x, 'tensor', pairs)  6.37 us
    pallas_call x1, Pallas kernels, attn_forward(): pl.pallas_call(partial(attn_forward_kernel, nimg), out_shape=shapes, in_s...  4.32 us
  transfers between devices with their start and end apart: 37, of which 27 were waited for; matrix products, arithmetic and copies ran while one was open for 4% of the time, Pallas kernels for 36%

profile of v3, /device:TPU:0, one launch (start us, length us, event | category | flops | bytes accessed | tf_op | source)
XLA Modules:
  0.0 168.4 jit_solution(17354902494806420967)
XLA Ops:
  0.7 0.8 pad_maximum_fusion.6
  1.5 2.2 %concatenate.42 = bf16[16,64]{1,0:T(8,128)(2,1)S(1)} concatenate(bf16[2,64]{1,0:T(2,128)(2,1)} %param.20, bf16[2,64]{1,0:T(2,128)(2,1)} %param.21, bf16[1,64]{1,0:T(2,128)(2,1)} %bitcast.51, bf16[4,64]{1,0:T(4,128)(2,1)} %bitcast.50, bf16[4,64]{1,0:T(4,128)(2,1)} %param.30, bf16[3,64]{1,0:T(4,128)(2,1)S(1)} %broadcast_in_dim.18), dimensions={0} | concatenate | bytes 4096 | tf_op jit(solution)/shard_map/concatenate | solution.py:795
  3.7 0.8 fusion.11
  4.5 4.1 %collective-permute-start.1 = (bf16[272,128]{1,0:T(8,128)(2,1)S(1)}, bf16[272,128]{1,0:T(8,128)(2,1)S(1)}, u32[]{:S(2)}, u32[]{:S(2)}) collective-permute-start(bf16[272,128]{1,0:T(8,128)(2,1)S(1)} %fusion.11), channel_id=1, source_target_pairs={{0,2},{1,3},{2,0},{3,1},{4,6},{5,7},{6,4},{7,5},{8,10},{9,11},{10,... | collective-permute-start | bytes 208904 | tf_op jit(solution)/shard_map/ppermute | solution.py:46
  8.6 1.6 collective-permute-start
  10.2 1.0 slice.43
  11.2 1.2 slice_select_fusion
  12.9 3.4 %collective-permute-done.2 = bf16[272,128]{1,0:T(8,128)(2,1)S(1)} collective-permute-done((bf16[272,128]{1,0:T(8,128)(2,1)S(1)}, bf16[272,128]{1,0:T(8,128)(2,1)S(1)}, u32[]{:S(2)}, u32[]{:S(2)}) %collective-permute-start.2) | collective-permute-done | bytes 69664 | tf_op jit(solution)/shard_map/ppermute | solution.py:46
  16.3 1.6 collective-permute-start.4
  17.9 1.5 collective-permute-start.3
  19.5 0.7 dynamic-slice_bitcast_fusion
  20.1 3.0 %collective-permute-done.4 = bf16[4,272,128]{2,1,0:T(8,128)(2,1)S(1)} collective-permute-done((bf16[4,272,128]{2,1,0:T(8,128)(2,1)S(1)}, bf16[4,272,128]{2,1,0:T(8,128)(2,1)S(1)}, u32[]{:S(2)}, u32[]{:S(2)}) %collective-permute-start.4) | collective-permute-done | bytes 278560 | tf_op jit(solution)/shard_map/ppermute | solution.py:46
  23.2 1.6 collective-permute-start.6
  24.8 0.9 collective-permute-done.3
  25.7 0.6 collective-permute-start.5
  27.0 2.8 %collective-permute-done.7.cot_ref.refs_5_ = bf16[400,512]{1,0:T(8,128)(2,1)S(1)} collective-permute-done((bf16[400,512]{1,0:T(8,128)(2,1)S(1)}, bf16[400,512]{1,0:T(8,128)(2,1)S(1)}, u32[]{:S(2)}, u32[]{:S(2)}) %collective-permute-start.7) | collective-permute-done | bytes 409632 | tf_op jit(solution)/shard_map/ppermute | solution.py:56
  29.8 1.0 collective-permute-done.5
  31.2 0.6 collective-permute-start.11
  31.8 1.0 collective-permute-start.10
  33.8 1.9 %assemble.1 = (bf16[4,512,512]{2,1,0:T(8,128)(2,1)S(1)}, f32[32,512]{1,0:T(8,128)S(1)}) custom-call(s32[6]{0:T(128)S(1)} %pad_add_fusion.ids, bf16[4,4,272,128]{3,2,1,0:T(8,128)(2,1)S(1)} %pad_maximum_fusion.1.refs_0_, bf16[4,4,272,128]{3,2,1,0:T(8,128)(2,1)S(1)} %collective-permute-done.8.refs_1_), custom_call_target="tpu_custom_call" | custom-call | bytes 66000 | tf_op jit(solution)/shard_map/assemble/pallas_call | solution.py:334
  35.7 4.3 %attn_forward.1 = (bf16[400,512]{1,0:T(8,128)(2,1)S(1)}, f32[400,512]{1,0:T(8,128)}, bf16[400,512]{1,0:T(8,128)(2,1)}, bf16[400,512]{1,0:T(8,128)(2,1)}, bf16[40...) custom-call(bf16[400,512]{1,0:T(8,128)(2,1)S(1)} %fusion.2.x_ref.refs_2_, ...), custom_call_target="tpu_custom_call" | custom-call | bytes 297000 | tf_op jit(solution)/shard_map/attn_forward/pallas_call | solution.py:409
  40.1 1.3 collective-permute-start.9
  41.4 4.2 %collective-permute-done.11 = bf16[8,64,512]{2,1,0:T(8,128)(2,1)S(1)} collective-permute-done((bf16[8,64,512]{2,1,0:T(8,128)(2,1)S(1)}, bf16[8,64,512]{2,1,0:T(8,128)(2,1)S(1)}, u32[]{:S(2)}, u32[]{:S(2)}) %collective-permute-start.11) | collective-permute-done | bytes 524320 | tf_op jit(solution)/shard_map/ppermute | solution.py:46
  45.9 1.3 collective-permute-start.13
  47.2 1.7 collective-permute-start.12
  48.9 4.6 %collective-permute-done.13 = bf16[4,64,512]{2,1,0:T(8,128)(2,1)S(1)} collective-permute-done((bf16[4,64,512]{2,1,0:T(8,128)(2,1)S(1)}, bf16[4,64,512]{2,1,0:T(8,128)(2,1)S(1)}, u32[]{:S(2)}, u32[]{:S(2)}) %collective-permute-start.13) | collective-permute-done | bytes 262176 | tf_op jit(solution)/shard_map/ppermute | solution.py:46
  53.5 1.3 collective-permute-done.12
  55.3 1.8 %collective-permute-start.17 = (bf16[400,512]{1,0:T(8,128)(2,1)S(1)}, bf16[400,512]{1,0:T(8,128)(2,1)S(1)}, u32[]{:S(2)}, u32[]{:S(2)}) collective-permute-start(bf16[400,512]{1,0:T(8,128)(2,1)S(1)} %collective-permute-done.9.hn2_ref.refs_1_), channel_id=1, source_target_pairs={{0,1},{1,3},{3,2},{2,0},{4,5},{5,7},{7,6},{6,4},{8,9},{9,11},{11,1... | collective-permute-start | bytes 1228808 | tf_op jit(solution)/shard_map/ppermute | solution.py:56
  57.1 2.3 %collective-permute-done.15.refs_1_ = bf16[4,8,64,512]{3,2,1,0:T(8,128)(2,1)S(1)} collective-permute-done((bf16[4,8,64,512]{3,2,1,0:T(8,128)(2,1)S(1)}, bf16[4,8,64,512]{3,2,1,0:T(8,128)(2,1)S(1)}, u32[]{:S(2)}, u32[]{:S(2)}) %collective-permute-start.15) | collective-permute-done | bytes 2097184 | tf_op jit(solution)/shard_map/ppermute | solution.py:46
  59.3 1.9 %gather_experts.1 = (bf16[512,2048]{1,0:T(8,128)(2,1)S(1)}, bf16[512,2048]{1,0:T(8,128)(2,1)S(1)}) custom-call(s32[6]{0:T(128)S(1)} %pad_add_fusion.ids, bf16[4,8,64,512]{3,2,1,0:T(8,128)(2,1)S(1)} %pad_maximum_fusion.refs_0_, bf16[4,8,64,512]{3,2,1,0:T(8,128)(2,1)S(1)} %collective-permute-done.15.refs_1_), custom_call_target="tpu_custom_call" | custom-call | bytes 99000 | tf_op jit(solution)/shard_map/gather_experts/pallas_call | solution.py:441
  61.3 7.7 %expert_shard.4 = (bf16[400,512]{1,0:T(8,128)(2,1)S(1)}, bf16[400,512]{1,0:T(8,128)(2,1)S(1)}, bf16[400,2048]{1,0:T(8,128)(2,1)S(1)}, bf16[400,2048]{1,0:T(8,128)(2,1)S(1)}, f32[16,512]{1,0:T(8,128)S(1)}) custom-call(s32[6]{0:T(128)S(1)} %pad_add_fusion.ids, s32[8,200,2]{2,1,0:T(8,128)S(1)} %pad.26.keep_ref, ...), custom_call_target="tpu_custom_call" | custom-call | bytes 231000 | tf_op jit(solution)/shard_map/expert_shard/pallas_call | solution.py:519
  69.0 8.3 %collective-permute-done.17.hn2_ref.refs_2_ = bf16[400,512]{1,0:T(8,128)(2,1)S(1)} collective-permute-done((bf16[400,512]{1,0:T(8,128)(2,1)S(1)}, bf16[400,512]{1,0:T(8,128)(2,1)S(1)}, u32[]{:S(2)}, u32[]{:S(2)}) %collective-permute-start.17) | collective-permute-done | bytes 409632 | tf_op jit(solution)/shard_map/ppermute | solution.py:56
  77.3 7.6 %expert_shard.5 = (bf16[400,512]{1,0:T(8,128)(2,1)S(1)}, bf16[400,512]{1,0:T(8,128)(2,1)S(1)}, bf16[400,2048]{1,0:T(8,128)(2,1)S(1)}, bf16[400,2048]{1,0:T(8,128)(2,1)S(1)}, f32[16,512]{1,0:T(8,128)S(1)}) custom-call(s32[6]{0:T(128)S(1)} %pad_add_fusion.ids, s32[8,200,2]{2,1,0:T(8,128)S(1)} %pad.26.keep_ref, ...), custom_call_target="tpu_custom_call" | custom-call | bytes 231000 | tf_op jit(solution)/shard_map/expert_shard/pallas_call | solution.py:519
  84.9 1.1 collective-permute-done.16.refs_0_
  86.1 0.7 collective-permute-start.18
  86.9 7.8 %expert_shard.6 = (bf16[400,512]{1,0:T(8,128)(2,1)S(1)}, bf16[400,512]{1,0:T(8,128)(2,1)S(1)}, bf16[400,2048]{1,0:T(8,128)(2,1)S(1)}, bf16[400,2048]{1,0:T(8,128)(2,1)S(1)}, f32[16,512]{1,0:T(8,128)S(1)}) custom-call(s32[6]{0:T(128)S(1)} %pad_add_fusion.ids, s32[8,200,2]{2,1,0:T(8,128)S(1)} %pad.26.keep_ref, ...), custom_call_target="tpu_custom_call" | custom-call | bytes 231000 | tf_op jit(solution)/shard_map/expert_shard/pallas_call | solution.py:519
  94.8 7.6 %expert_shard.7 = (bf16[400,512]{1,0:T(8,128)(2,1)S(1)}, bf16[400,512]{1,0:T(8,128)(2,1)S(1)}, bf16[400,2048]{1,0:T(8,128)(2,1)S(1)}, bf16[400,2048]{1,0:T(8,128)(2,1)S(1)}, f32[16,512]{1,0:T(8,128)S(1)}) custom-call(s32[6]{0:T(128)S(1)} %pad_add_fusion.ids, s32[8,200,2]{2,1,0:T(8,128)S(1)} %pad.26.keep_ref, ...), custom_call_target="tpu_custom_call" | custom-call | bytes 231000 | tf_op jit(solution)/shard_map/expert_shard/pallas_call | solution.py:519
  102.5 0.6 collective-permute-done.18.refs_0_
  103.2 0.7 collective-permute-start.21
  103.9 10.0 %expert_grads.1 = (f32[4,1,512]{2,1,0:T(1,128)S(1)}, bf16[4,2,4,64,512]{4,3,2,1,0:T(8,128)(2,1)S(1)}, bf16[4,2,4,64,512]{4,3,2,1,0:T(8,128)(2,1)S(1)}) custom-call(s32[6]{0:T(128)S(1)} %pad_add_fusion.ids, bf16[400,512]{1,0:T(8,128)(2,1)S(1)} %get-tuple-element.131.hn2_ref.refs_0_, bf16[400,512]{1,0:T(8,128)(2,1)S(1)} %collective-permute-done.9.hn2_ref.refs_1_, ...), custom_call_target="tpu_custom_call" | custom-call | bytes 297000 | tf_op jit(solution)/shard_map/expert_grads/pallas_call | solution.py:562
  113.9 1.2 collective-permute-done.21.refs_0_
  115.1 0.9 collective-permute-start.23
  116.0 9.7 %attn_backward.1 = (f32[400,512]{1,0:T(8,128)S(1)}, bf16[4,4,272,128]{3,2,1,0:T(8,128)(2,1)S(1)}, bf16[4,4,272,128]{3,2,1,0:T(8,128)(2,1)S(1)}, f32[32,512]{1,0:T(8,128)}) custom-call(s32[6]{0:T(128)S(1)} %pad_add_fusion.ids, bf16[400,512]{1,0:T(8,128)(2,1)S(1)} %collective-permute-done.21.refs_0_, bf16[400,512]{1,0:T(8,128)(2,1)S(1)} %get-tuple-element.135.refs_1_, ...), custom_call_target="tpu_custom_call" | custom-call | bytes 528000 | tf_op jit(solution)/shard_map/attn_backward/pallas_call | solution.py:714
  125.7 2.2 %collective-permute-done.23.refs_0_ = bf16[400,512]{1,0:T(8,128)(2,1)S(1)} collective-permute-done((bf16[400,512]{1,0:T(8,128)(2,1)S(1)}, bf16[400,512]{1,0:T(8,128)(2,1)S(1)}, u32[]{:S(2)}, u32[]{:S(2)}) %collective-permute-start.23) | collective-permute-done | bytes 409632 | tf_op jit(solution)/shard_map/ppermute | solution.py:56
  128.0 2.6 %collective-permute-done.24.refs_1_ = bf16[4,4,272,128]{3,2,1,0:T(8,128)(2,1)S(1)} collective-permute-done((bf16[4,4,272,128]{3,2,1,0:T(8,128)(2,1)S(1)}, bf16[4,4,272,128]{3,2,1,0:T(8,128)(2,1)S(1)}, u32[]{:S(2)}, u32[]{:S(2)}) %collective-permute-start.24) | collective-permute-done | bytes 1114144 | tf_op jit(solution)/shard_map/ppermute | solution.py:46
  130.9 1.5 collective-permute-start.27
  133.4 6.3 %collective-permute-done.27.refs_3_ = bf16[2,2,272,128]{3,2,1,0:T(8,128)(2,1)S(1)} collective-permute-done((bf16[2,2,272,128]{3,2,1,0:T(8,128)(2,1)S(1)}, bf16[2,2,272,128]{3,2,1,0:T(8,128)(2,1)S(1)}, u32[]{:S(2)}, u32[]{:S(2)}) %collective-permute-start.27) | collective-permute-done | bytes 278560 | tf_op jit(solution)/shard_map/ppermute | solution.py:46
  139.7 1.1 collective-permute-done.26.refs_1_
  141.1 1.3 collective-permute-start.29
  142.4 0.6 collective-permute-start.30
  143.0 1.4 collective-permute-start.31
  144.4 0.8 collective-permute-start.32
  145.3 3.7 %collective-permute-done.30.refs_3_ = bf16[2,272,128]{2,1,0:T(8,128)(2,1)S(1)} collective-permute-done((bf16[2,272,128]{2,1,0:T(8,128)(2,1)S(1)}, bf16[2,272,128]{2,1,0:T(8,128)(2,1)S(1)}, u32[]{:S(2)}, u32[]{:S(2)}) %collective-permute-start.30) | collective-permute-done | bytes 139296 | tf_op jit(solution)/shard_map/ppermute | solution.py:46
  149.0 2.9 %collective-permute-start.33 = (bf16[2,272,128]{2,1,0:T(8,128)(2,1)S(1)}, bf16[2,272,128]{2,1,0:T(8,128)(2,1)S(1)}, u32[]{:S(2)}, u32[]{:S(2)}) collective-permute-start(bf16[2,272,128]{2,1,0:T(8,128)(2,1)S(1)} %get-tuple-element.184), channel_id=1, source_target_pairs={{0,2},{1,3},{2,0},{3,1},{4,6},{5,7},{6,4},{7,5},{8,10},{9,11},{10,... | collective-permute-start | bytes 417800 | tf_op jit(solution)/shard_map/ppermute | solution.py:46
  151.9 5.4 %collective-permute-done.28 = bf16[400,512]{1,0:T(8,128)(2,1)S(1)} collective-permute-done((bf16[400,512]{1,0:T(8,128)(2,1)S(1)}, bf16[400,512]{1,0:T(8,128)(2,1)S(1)}, u32[]{:S(2)}, u32[]{:S(2)}) %collective-permute-start.28) | collective-permute-done | bytes 409632 | tf_op jit(solution)/shard_map/ppermute | solution.py:56
  157.5 1.3 collective-permute-done.33.refs_1_
  159.1 1.5 collective-permute-start.35
  161.2 1.4 collective-permute-start.36
  162.6 1.3 pad_maximum_fusion.2
  163.9 1.1 collective-permute-done.34.refs_1_
  165.0 0.7 finish.1
  166.0 0.9 add_bitcast_fusion.1
  166.9 0.7 collective-permute-done.36
  167.6 0.9 add_bitcast_fusion
  (79 shorter events, 7.0 us)
Async XLA Ops:
  0.6 11.8 %copy-start.6 = (bf16[4,64]{1,0:T(4,128)(2,1)S(1)}, bf16[4,64]{1,0:T(4,128)(2,1)}, u32[]{:S(2)}) copy-start(bf16[4,64]{1,0:T(4,128)(2,1)} %param.28) | copy-start | bytes 1540
  0.7 11.8 %copy-start.7 = (bf16[2,16]{1,0:T(2,128)(2,1)S(1)}, bf16[2,16]{1,0:T(2,128)(2,1)}, u32[]{:S(2)}) copy-start(bf16[2,16]{1,0:T(2,128)(2,1)} %param.23) | copy-start | bytes 196
  0.7 18.8 %copy-start.4 = (s32[1576,2]{0,1:T(2,128)S(1)}, s32[1576,2]{0,1:T(2,128)}, u32[]{:S(2)}) copy-start(s32[1576,2]{0,1:T(2,128)} %param.18) | copy-start | bytes 37828
  0.7 18.7 %copy-start.5 = (s32[1576,2]{0,1:T(2,128)S(1)}, s32[1576,2]{0,1:T(2,128)}, u32[]{:S(2)}) copy-start(s32[1576,2]{0,1:T(2,128)} %param.19) | copy-start | bytes 37828
  4.5 8.0 %collective-permute-start.1 = (bf16[272,128]{1,0:T(8,128)(2,1)S(1)}, bf16[272,128]{1,0:T(8,128)(2,1)S(1)}, u32[]{:S(2)}, u32[]{:S(2)}) collective-permute-start(bf16[272,128]{1,0:T(8,128)(2,1)S(1)} %fusion.11), channel_id=1, source_target_pairs={{0,2},{1,3},{2,0},{3,1},{4,6},{5,7},{6,4},{7,5},{8,10},{9,11},{10,... | collective-permute-start | bytes 208904 | tf_op jit(solution)/shard_map/ppermute | solution.py:46
  8.6 4.3 %collective-permute-start = (bf16[272,128]{1,0:T(8,128)(2,1)S(1)}, bf16[272,128]{1,0:T(8,128)(2,1)S(1)}, u32[]{:S(2)}, u32[]{:S(2)}) collective-permute-start(bf16[272,128]{1,0:T(8,128)(2,1)S(1)} %fusion.11), channel_id=1, source_target_pairs={{0,1},{1,0},{2,3},{3,2},{4,5},{5,4},{6,7},{7,6},{8,9},{9,8},{10,11... | collective-permute-start | bytes 208904 | tf_op jit(solution)/shard_map/ppermute | solution.py:46
  10.2 6.1 %collective-permute-start.2 = (bf16[272,128]{1,0:T(8,128)(2,1)S(1)}, bf16[272,128]{1,0:T(8,128)(2,1)S(1)}, u32[]{:S(2)}, u32[]{:S(2)}) collective-permute-start(bf16[272,128]{1,0:T(8,128)(2,1)S(1)} %fusion.11), channel_id=1, source_target_pairs={{0,3},{1,2},{2,1},{3,0},{4,7},{5,6},{6,5},{7,4},{8,11},{9,10},{10,... | collective-permute-start | bytes 208904 | tf_op jit(solution)/shard_map/ppermute | solution.py:46
  11.2 15.3 %copy-start.1 = (bf16[394,512]{1,0:T(8,128)(2,1)S(1)}, bf16[394,512]{1,0:T(8,128)(2,1)}, u32[]{:S(2)}) copy-start(bf16[394,512]{1,0:T(8,128)(2,1)} %param.16) | copy-start | bytes 1210372
  16.3 6.9 %collective-permute-start.4 = (bf16[4,272,128]{2,1,0:T(8,128)(2,1)S(1)}, bf16[4,272,128]{2,1,0:T(8,128)(2,1)S(1)}, u32[]{:S(2)}, u32[]{:S(2)}) collective-permute-start(bf16[4,272,128]{2,1,0:T(8,128)(2,1)S(1)} %get-tuple-element.212), channel_id=1, source_target_pairs={{0,16},{4,20},{8,24},{12,28},{16,0},{20,4},{24,8},{28,12},{1,17},{... | collective-permute-start | bytes 835592 | tf_op jit(solution)/shard_map/ppermute | solution.py:46
  17.9 7.8 %collective-permute-start.3 = (bf16[4,272,128]{2,1,0:T(8,128)(2,1)S(1)}, bf16[4,272,128]{2,1,0:T(8,128)(2,1)S(1)}, u32[]{:S(2)}, u32[]{:S(2)}) collective-permute-start(bf16[4,272,128]{2,1,0:T(8,128)(2,1)S(1)} %get-tuple-element.212), channel_id=1, source_target_pairs={{0,8},{4,12},{8,0},{12,4},{16,24},{20,28},{24,16},{28,20},{1,9},{5... | collective-permute-start | bytes 835592 | tf_op jit(solution)/shard_map/ppermute | solution.py:46
  19.4 10.4 %collective-permute-start.7 = (bf16[400,512]{1,0:T(8,128)(2,1)S(1)}, bf16[400,512]{1,0:T(8,128)(2,1)S(1)}, u32[]{:S(2)}, u32[]{:S(2)}) collective-permute-start(bf16[400,512]{1,0:T(8,128)(2,1)S(1)} %fusion.3.cot_ref.refs_4_.refs_3_), channel_id=1, source_target_pairs={{0,1},{1,3},{3,2},{2,0},{4,5},{5,7},{7,6},{6,4},{8,9},{9,11},{11,1... | collective-permute-start | bytes 1228808 | tf_op jit(solution)/shard_map/ppermute | solution.py:56
  23.2 6.6 %collective-permute-start.6 = (bf16[2,272,128]{2,1,0:T(8,128)(2,1)S(1)}, bf16[2,272,128]{2,1,0:T(8,128)(2,1)S(1)}, u32[]{:S(2)}, u32[]{:S(2)}) collective-permute-start(bf16[2,272,128]{2,1,0:T(8,128)(2,1)S(1)} %slice.51), channel_id=1, source_target_pairs={{0,8},{4,12},{8,0},{12,4},{16,24},{20,28},{24,16},{28,20},{1,9},{5... | collective-permute-start | bytes 417800 | tf_op jit(solution)/shard_map/ppermute | solution.py:46
  25.7 5.1 %collective-permute-start.5 = (bf16[2,272,128]{2,1,0:T(8,128)(2,1)S(1)}, bf16[2,272,128]{2,1,0:T(8,128)(2,1)S(1)}, u32[]{:S(2)}, u32[]{:S(2)}) collective-permute-start(bf16[2,272,128]{2,1,0:T(8,128)(2,1)S(1)} %slice.50), channel_id=1, source_target_pairs={{0,16},{4,20},{8,24},{12,28},{16,0},{20,4},{24,8},{28,12},{1,17},{... | collective-permute-start | bytes 417800 | tf_op jit(solution)/shard_map/ppermute | solution.py:46
  27.0 4.1 %copy-start.2 = (bf16[4,512,64]{1,2,0:T(8,128)(2,1)S(1)}, bf16[4,512,64]{1,2,0:T(8,128)(2,1)}, u32[]{:S(2)}) copy-start(bf16[4,512,64]{1,2,0:T(8,128)(2,1)} %param.29) | copy-start | bytes 786436
  27.0 4.1 %copy-start.3 = (bf16[4,64,512]{2,1,0:T(8,128)(2,1)S(1)}, bf16[4,64,512]{2,1,0:T(8,128)(2,1)}, u32[]{:S(2)}) copy-start(bf16[4,64,512]{2,1,0:T(8,128)(2,1)} %param.27) | copy-start | bytes 786436
  31.0 2.8 %collective-permute-start.8 = (bf16[4,4,272,128]{3,2,1,0:T(8,128)(2,1)S(1)}, bf16[4,4,272,128]{3,2,1,0:T(8,128)(2,1)S(1)}, u32[]{:S(2)}, u32[]{:S(2)}) collective-permute-start(bf16[4,4,272,128]{3,2,1,0:T(8,128)(2,1)S(1)} %pad_maximum_fusion.1.refs_0_), channel_id=1, source_target_pairs={{0,4},{4,0},{8,12},{12,8},{16,20},{20,16},{24,28},{28,24},{1,5},{5... | collective-permute-start | bytes 3342344 | tf_op jit(solution)/shard_map/ppermute | solution.py:46
  31.2 14.4 %collective-permute-start.11 = (bf16[8,64,512]{2,1,0:T(8,128)(2,1)S(1)}, bf16[8,64,512]{2,1,0:T(8,128)(2,1)S(1)}, u32[]{:S(2)}, u32[]{:S(2)}) collective-permute-start(bf16[8,64,512]{2,1,0:T(8,128)(2,1)S(1)} %pad_maximum_fusion.4), channel_id=1, source_target_pairs={{0,16},{4,20},{8,24},{12,28},{16,0},{20,4},{24,8},{28,12},{1,17},{... | collective-permute-start | bytes 1572872 | tf_op jit(solution)/shard_map/ppermute | solution.py:46
  31.8 14.0 %collective-permute-start.10 = (bf16[8,64,512]{2,1,0:T(8,128)(2,1)S(1)}, bf16[8,64,512]{2,1,0:T(8,128)(2,1)S(1)}, u32[]{:S(2)}, u32[]{:S(2)}) collective-permute-start(bf16[8,64,512]{2,1,0:T(8,128)(2,1)S(1)} %pad_maximum_fusion.4), channel_id=1, source_target_pairs={{0,8},{4,12},{8,0},{12,4},{16,24},{20,28},{24,16},{28,20},{1,9},{5... | collective-permute-start | bytes 1572872 | tf_op jit(solution)/shard_map/ppermute | solution.py:46
  32.8 16.1 %collective-permute-start.14 = (bf16[400,512]{1,0:T(8,128)(2,1)S(1)}, bf16[400,512]{1,0:T(8,128)(2,1)S(1)}, u32[]{:S(2)}, u32[]{:S(2)}) collective-permute-start(bf16[400,512]{1,0:T(8,128)(2,1)S(1)} %collective-permute-done.7.cot_ref.refs_5_), channel_id=1, source_target_pairs={{0,1},{1,3},{3,2},{2,0},{4,5},{5,7},{7,6},{6,4},{8,9},{9,11},{11,1... | collective-permute-start | bytes 1228808 | tf_op jit(solution)/shard_map/ppermute | solution.py:56
  40.1 14.7 %collective-permute-start.9 = (bf16[400,512]{1,0:T(8,128)(2,1)S(1)}, bf16[400,512]{1,0:T(8,128)(2,1)S(1)}, u32[]{:S(2)}, u32[]{:S(2)}) collective-permute-start(bf16[400,512]{1,0:T(8,128)(2,1)S(1)} %get-tuple-element.131.hn2_ref.refs_0_), channel_id=1, source_target_pairs={{0,1},{1,3},{3,2},{2,0},{4,5},{5,7},{7,6},{6,4},{8,9},{9,11},{11,1... | collective-permute-start | bytes 1228808 | tf_op jit(solution)/shard_map/ppermute | solution.py:56
  45.9 7.6 %collective-permute-start.13 = (bf16[4,64,512]{2,1,0:T(8,128)(2,1)S(1)}, bf16[4,64,512]{2,1,0:T(8,128)(2,1)S(1)}, u32[]{:S(2)}, u32[]{:S(2)}) collective-permute-start(bf16[4,64,512]{2,1,0:T(8,128)(2,1)S(1)} %slice.45), channel_id=1, source_target_pairs={{0,8},{4,12},{8,0},{12,4},{16,24},{20,28},{24,16},{28,20},{1,9},{5... | collective-permute-start | bytes 786440 | tf_op jit(solution)/shard_map/ppermute | solution.py:46
  47.2 7.6 %collective-permute-start.12 = (bf16[4,64,512]{2,1,0:T(8,128)(2,1)S(1)}, bf16[4,64,512]{2,1,0:T(8,128)(2,1)S(1)}, u32[]{:S(2)}, u32[]{:S(2)}) collective-permute-start(bf16[4,64,512]{2,1,0:T(8,128)(2,1)S(1)} %slice.44), channel_id=1, source_target_pairs={{0,16},{4,20},{8,24},{12,28},{16,0},{20,4},{24,8},{28,12},{1,17},{... | collective-permute-start | bytes 786440 | tf_op jit(solution)/shard_map/ppermute | solution.py:46
  55.1 4.2 %collective-permute-start.15 = (bf16[4,8,64,512]{3,2,1,0:T(8,128)(2,1)S(1)}, bf16[4,8,64,512]{3,2,1,0:T(8,128)(2,1)S(1)}, u32[]{:S(2)}, u32[]{:S(2)}) collective-permute-start(bf16[4,8,64,512]{3,2,1,0:T(8,128)(2,1)S(1)} %pad_maximum_fusion.refs_0_), channel_id=1, source_target_pairs={{0,4},{4,0},{8,12},{12,8},{16,20},{20,16},{24,28},{28,24},{1,5},{5... | collective-permute-start | bytes 6291464 | tf_op jit(solution)/shard_map/ppermute | solution.py:46
  55.2 13.8 %collective-permute-start.19 = (bf16[400,512]{1,0:T(8,128)(2,1)S(1)}, bf16[400,512]{1,0:T(8,128)(2,1)S(1)}, u32[]{:S(2)}, u32[]{:S(2)}) collective-permute-start(bf16[400,512]{1,0:T(8,128)(2,1)S(1)} %collective-permute-done.14.cot_ref.refs_6_), channel_id=1, source_target_pairs={{0,1},{1,3},{3,2},{2,0},{4,5},{5,7},{7,6},{6,4},{8,9},{9,11},{11,1... | collective-permute-start | bytes 1228808 | tf_op jit(solution)/shard_map/ppermute | solution.py:56
  55.3 22.0 %collective-permute-start.17 = (bf16[400,512]{1,0:T(8,128)(2,1)S(1)}, bf16[400,512]{1,0:T(8,128)(2,1)S(1)}, u32[]{:S(2)}, u32[]{:S(2)}) collective-permute-start(bf16[400,512]{1,0:T(8,128)(2,1)S(1)} %collective-permute-done.9.hn2_ref.refs_1_), channel_id=1, source_target_pairs={{0,1},{1,3},{3,2},{2,0},{4,5},{5,7},{7,6},{6,4},{8,9},{9,11},{11,1... | collective-permute-start | bytes 1228808 | tf_op jit(solution)/shard_map/ppermute | solution.py:56
  68.9 17.1 %collective-permute-start.16 = (bf16[400,512]{1,0:T(8,128)(2,1)S(1)}, bf16[400,512]{1,0:T(8,128)(2,1)S(1)}, u32[]{:S(2)}, u32[]{:S(2)}) collective-permute-start(bf16[400,512]{1,0:T(8,128)(2,1)S(1)} %get-tuple-element.126), channel_id=1, source_target_pairs={{0,1},{1,3},{3,2},{2,0},{4,5},{5,7},{7,6},{6,4},{8,9},{9,11},{11,1... | collective-permute-start | bytes 1228808 | tf_op jit(solution)/shard_map/ppermute | solution.py:56
  77.3 17.6 %collective-permute-start.20 = (bf16[400,512]{1,0:T(8,128)(2,1)S(1)}, bf16[400,512]{1,0:T(8,128)(2,1)S(1)}, u32[]{:S(2)}, u32[]{:S(2)}) collective-permute-start(bf16[400,512]{1,0:T(8,128)(2,1)S(1)} %collective-permute-done.17.hn2_ref.refs_2_), channel_id=1, source_target_pairs={{0,1},{1,3},{3,2},{2,0},{4,5},{5,7},{7,6},{6,4},{8,9},{9,11},{11,1... | collective-permute-start | bytes 1228808 | tf_op jit(solution)/shard_map/ppermute | solution.py:56
  86.1 16.9 %collective-permute-start.18 = (bf16[400,512]{1,0:T(8,128)(2,1)S(1)}, bf16[400,512]{1,0:T(8,128)(2,1)S(1)}, u32[]{:S(2)}, u32[]{:S(2)}) collective-permute-start(bf16[400,512]{1,0:T(8,128)(2,1)S(1)} %sums.10), channel_id=1, source_target_pairs={{0,1},{1,3},{3,2},{2,0},{4,5},{5,7},{7,6},{6,4},{8,9},{9,11},{11,1... | collective-permute-start | bytes 1228808 | tf_op jit(solution)/shard_map/ppermute | solution.py:56
  103.2 11.9 %collective-permute-start.21 = (bf16[400,512]{1,0:T(8,128)(2,1)S(1)}, bf16[400,512]{1,0:T(8,128)(2,1)S(1)}, u32[]{:S(2)}, u32[]{:S(2)}) collective-permute-start(bf16[400,512]{1,0:T(8,128)(2,1)S(1)} %sums.11), channel_id=1, source_target_pairs={{0,1},{1,3},{3,2},{2,0},{4,5},{5,7},{7,6},{6,4},{8,9},{9,11},{11,1... | collective-permute-start | bytes 1228808 | tf_op jit(solution)/shard_map/ppermute | solution.py:56
  115.1 12.8 %collective-permute-start.22 = (bf16[4,2,4,64,512]{4,3,2,1,0:T(8,128)(2,1)S(1)}, bf16[4,2,4,64,512]{4,3,2,1,0:T(8,128)(2,1)S(1)}, u32[]{:S(2)}, u32[]{:S(2)}) collective-permute-start(bf16[4,2,4,64,512]{4,3,2,1,0:T(8,128)(2,1)S(1)} %get-tuple-element.145), channel_id=1, source_target_pairs={{0,4},{4,0},{8,12},{12,8},{16,20},{20,16},{24,28},{28,24},{1,5},{5... | collective-permute-start | bytes 6291464 | tf_op jit(solution)/shard_map/ppermute | solution.py:46
  115.1 12.8 %collective-permute-start.23 = (bf16[400,512]{1,0:T(8,128)(2,1)S(1)}, bf16[400,512]{1,0:T(8,128)(2,1)S(1)}, u32[]{:S(2)}, u32[]{:S(2)}) collective-permute-start(bf16[400,512]{1,0:T(8,128)(2,1)S(1)} %get-tuple-element.147), channel_id=1, source_target_pairs={{0,1},{1,3},{3,2},{2,0},{4,5},{5,7},{7,6},{6,4},{8,9},{9,11},{11,1... | collective-permute-start | bytes 1228808 | tf_op jit(solution)/shard_map/ppermute | solution.py:56
  127.9 2.8 %collective-permute-start.24 = (bf16[4,4,272,128]{3,2,1,0:T(8,128)(2,1)S(1)}, bf16[4,4,272,128]{3,2,1,0:T(8,128)(2,1)S(1)}, u32[]{:S(2)}, u32[]{:S(2)}) collective-permute-start(bf16[4,4,272,128]{3,2,1,0:T(8,128)(2,1)S(1)} %get-tuple-element.161), channel_id=1, source_target_pairs={{0,4},{4,0},{8,12},{12,8},{16,20},{20,16},{24,28},{28,24},{1,5},{5... | collective-permute-start | bytes 3342344 | tf_op jit(solution)/shard_map/ppermute | solution.py:46
  128.0 12.9 %collective-permute-start.25 = (bf16[400,512]{1,0:T(8,128)(2,1)S(1)}, bf16[400,512]{1,0:T(8,128)(2,1)S(1)}, u32[]{:S(2)}, u32[]{:S(2)}) collective-permute-start(bf16[400,512]{1,0:T(8,128)(2,1)S(1)} %sums.14), channel_id=1, source_target_pairs={{0,1},{1,3},{3,2},{2,0},{4,5},{5,7},{7,6},{6,4},{8,9},{9,11},{11,1... | collective-permute-start | bytes 1228808 | tf_op jit(solution)/shard_map/ppermute | solution.py:56
  130.9 8.8 %collective-permute-start.27 = (bf16[2,2,272,128]{3,2,1,0:T(8,128)(2,1)S(1)}, bf16[2,2,272,128]{3,2,1,0:T(8,128)(2,1)S(1)}, u32[]{:S(2)}, u32[]{:S(2)}) collective-permute-start(bf16[2,2,272,128]{3,2,1,0:T(8,128)(2,1)S(1)} %get-tuple-element.169), channel_id=1, source_target_pairs={{0,16},{4,20},{8,24},{12,28},{16,0},{20,4},{24,8},{28,12},{1,17},{... | collective-permute-start | bytes 835592 | tf_op jit(solution)/shard_map/ppermute | solution.py:46
  132.4 8.4 %collective-permute-start.26 = (bf16[2,2,272,128]{3,2,1,0:T(8,128)(2,1)S(1)}, bf16[2,2,272,128]{3,2,1,0:T(8,128)(2,1)S(1)}, u32[]{:S(2)}, u32[]{:S(2)}) collective-permute-start(bf16[2,2,272,128]{3,2,1,0:T(8,128)(2,1)S(1)} %get-tuple-element.162), channel_id=1, source_target_pairs={{0,8},{4,12},{8,0},{12,4},{16,24},{20,28},{24,16},{28,20},{1,9},{5... | collective-permute-start | bytes 835592 | tf_op jit(solution)/shard_map/ppermute | solution.py:46
  140.9 16.4 %copy-start = (f32[400,512]{1,0:T(8,128)S(1)}, f32[400,512]{1,0:T(8,128)}, u32[]{:S(2)}) copy-start(f32[400,512]{1,0:T(8,128)} %get-tuple-element.116.refs_4_) | copy-start | bytes 2457604
  141.0 16.3 %collective-permute-start.28 = (bf16[400,512]{1,0:T(8,128)(2,1)S(1)}, bf16[400,512]{1,0:T(8,128)(2,1)S(1)}, u32[]{:S(2)}, u32[]{:S(2)}) collective-permute-start(bf16[400,512]{1,0:T(8,128)(2,1)S(1)} %sums.16), channel_id=1, source_target_pairs={{0,1},{1,3},{3,2},{2,0},{4,5},{5,7},{7,6},{6,4},{8,9},{9,11},{11,1... | collective-permute-start | bytes 1228808 | tf_op jit(solution)/shard_map/ppermute | solution.py:56
  141.1 7.9 %collective-permute-start.29 = (bf16[2,272,128]{2,1,0:T(8,128)(2,1)S(1)}, bf16[2,272,128]{2,1,0:T(8,128)(2,1)S(1)}, u32[]{:S(2)}, u32[]{:S(2)}) collective-permute-start(bf16[2,272,128]{2,1,0:T(8,128)(2,1)S(1)} %get-tuple-element.173), channel_id=1, source_target_pairs={{0,16},{4,20},{8,24},{12,28},{16,0},{20,4},{24,8},{28,12},{1,17},{... | collective-permute-start | bytes 417800 | tf_op jit(solution)/shard_map/ppermute | solution.py:46
  142.4 6.5 %collective-permute-start.30 = (bf16[2,272,128]{2,1,0:T(8,128)(2,1)S(1)}, bf16[2,272,128]{2,1,0:T(8,128)(2,1)S(1)}, u32[]{:S(2)}, u32[]{:S(2)}) collective-permute-start(bf16[2,272,128]{2,1,0:T(8,128)(2,1)S(1)} %get-tuple-element.180), channel_id=1, source_target_pairs={{0,8},{4,12},{8,0},{12,4},{16,24},{20,28},{24,16},{28,20},{1,9},{5... | collective-permute-start | bytes 417800 | tf_op jit(solution)/shard_map/ppermute | solution.py:46
  143.0 15.8 %collective-permute-start.31 = (bf16[2,1,4,64,512]{4,3,2,1,0:T(8,128)(2,1)S(1)}, bf16[2,1,4,64,512]{4,3,2,1,0:T(8,128)(2,1)S(1)}, u32[]{:S(2)}, u32[]{:S(2)}) collective-permute-start(bf16[2,1,4,64,512]{4,3,2,1,0:T(8,128)(2,1)S(1)} %get-tuple-element.182), channel_id=1, source_target_pairs={{0,8},{4,12},{8,0},{12,4},{16,24},{20,28},{24,16},{28,20},{1,9},{5... | collective-permute-start | bytes 1572872 | tf_op jit(solution)/shard_map/ppermute | solution.py:46
  144.4 14.4 %collective-permute-start.32 = (bf16[2,1,4,64,512]{4,3,2,1,0:T(8,128)(2,1)S(1)}, bf16[2,1,4,64,512]{4,3,2,1,0:T(8,128)(2,1)S(1)}, u32[]{:S(2)}, u32[]{:S(2)}) collective-permute-start(bf16[2,1,4,64,512]{4,3,2,1,0:T(8,128)(2,1)S(1)} %get-tuple-element.183), channel_id=1, source_target_pairs={{0,16},{4,20},{8,24},{12,28},{16,0},{20,4},{24,8},{28,12},{1,17},{... | collective-permute-start | bytes 1572872 | tf_op jit(solution)/shard_map/ppermute | solution.py:46
  149.0 9.8 %collective-permute-start.33 = (bf16[2,272,128]{2,1,0:T(8,128)(2,1)S(1)}, bf16[2,272,128]{2,1,0:T(8,128)(2,1)S(1)}, u32[]{:S(2)}, u32[]{:S(2)}) collective-permute-start(bf16[2,272,128]{2,1,0:T(8,128)(2,1)S(1)} %get-tuple-element.184), channel_id=1, source_target_pairs={{0,2},{1,3},{2,0},{3,1},{4,6},{5,7},{6,4},{7,5},{8,10},{9,11},{10,... | collective-permute-start | bytes 417800 | tf_op jit(solution)/shard_map/ppermute | solution.py:46
  159.1 6.9 %collective-permute-start.35 = (bf16[1,4,64,512]{3,2,1,0:T(8,128)(2,1)S(1)}, bf16[1,4,64,512]{3,2,1,0:T(8,128)(2,1)S(1)}, u32[]{:S(2)}, u32[]{:S(2)}) collective-permute-start(bf16[1,4,64,512]{3,2,1,0:T(8,128)(2,1)S(1)} %get-tuple-element.202), channel_id=1, source_target_pairs={{0,16},{4,20},{8,24},{12,28},{16,0},{20,4},{24,8},{28,12},{1,17},{... | collective-permute-start | bytes 786440 | tf_op jit(solution)/shard_map/ppermute | solution.py:46
  160.6 4.4 %collective-permute-start.34 = (bf16[272,128]{1,0:T(8,128)(2,1)S(1)}, bf16[272,128]{1,0:T(8,128)(2,1)S(1)}, u32[]{:S(2)}, u32[]{:S(2)}) collective-permute-start(bf16[272,128]{1,0:T(8,128)(2,1)S(1)} %get-tuple-element.187), channel_id=1, source_target_pairs={{0,1},{1,0},{2,3},{3,2},{4,5},{5,4},{6,7},{7,6},{8,9},{9,8},{10,11... | collective-permute-start | bytes 208904 | tf_op jit(solution)/shard_map/ppermute | solution.py:46
  161.2 6.4 %collective-permute-start.36 = (bf16[1,4,64,512]{3,2,1,0:T(8,128)(2,1)S(1)}, bf16[1,4,64,512]{3,2,1,0:T(8,128)(2,1)S(1)}, u32[]{:S(2)}, u32[]{:S(2)}) collective-permute-start(bf16[1,4,64,512]{3,2,1,0:T(8,128)(2,1)S(1)} %get-tuple-element.205), channel_id=1, source_target_pairs={{0,8},{4,12},{8,0},{12,4},{16,24},{20,28},{24,16},{28,20},{1,9},{5... | collective-permute-start | bytes 786440 | tf_op jit(solution)/shard_map/ppermute | solution.py:46
